TPU v7x, 1024 devices: a whole 8x8x8 slice. The times are simulated.
1024 devices in a mesh: gx: 64 (over z, y), gy: 16 (over x, core).
Axes of the slice: x: 8, y: 8, z: 8, core: 2. Of those that a mesh axis runs over, the one named last changes fastest.
Arguments:
- adjoint_trace: bfloat16 [1024, 256, 16, 128], P('gx', 'gy'), may hold values from -6 to 6
- coupling: bfloat16 [7, 128, 128], replicated, may hold values from -0.1875 to 0.1875
- log_friction: float32 [512, 256, 128], P('gx', 'gy'), may hold values from -1 to 1
- send_column: int32 [64, 16, 256], P('gx', 'gy'), may hold values from 0 to 255, each once within a row
- live_count: int32 [64, 16, 16], P('gx', 'gy'), may hold values from 0 to 16, as said below
- target_node: int32 [64, 16, 16, 16], P('gx', 'gy'), may hold values from 0 to 127
Outputs:
- trace_update: bfloat16 [1024, 256, 16, 128], P('gx', 'gy')
- friction_gradient: float32 [512, 256, 128], P('gx', 'gy')
Inputs may be any that keep to these rules, and one draw needn't show every extreme that they name: Each row of send_column lists every local basal face once. `live_count`: in every row of devices along gy, one owner receives 16 live blocks from every device.
All inputs are finite; a program needn't handle non-finite values.
Results may differ from a plain program's by a relative error of at most 0.0059.
Values may be sent and summed in bfloat16 or wider, within the bound.
No kernel may reach another device: no remote copies, remote signals or barrier semaphores. Data moves between devices by JAX's collectives and lax.ppermute only.
A program may use at most 32 MiB of HBM per device.

v0:
```python
import jax
import jax.numpy as jnp
from jax import lax
from jax.sharding import PartitionSpec as P


def padded_2(block, sides, width):
    for axis, dim in sides:
        count = lax.axis_size(axis)
        forward = [(i, i + 1) for i in range(count - 1)]
        backward = [(target, source) for source, target in forward]
        low = lax.ppermute(
            lax.slice_in_dim(block, block.shape[dim] - width, None, axis=dim), axis, forward
        )
        high = lax.ppermute(lax.slice_in_dim(block, 0, width, axis=dim), axis, backward)
        block = jnp.concatenate([low, block, high], axis=dim)
    return block


def couple(extended, coupling):
    own = extended[1:-1, 1:-1]
    rows_a, rows_b, layers_n, width = own.shape
    zeros_layer = jnp.zeros((rows_a, rows_b, 1, width), jnp.bfloat16)
    below = jnp.concatenate([zeros_layer, own[:, :, :-1]], axis=2)
    above = jnp.concatenate([own[:, :, 1:], zeros_layer], axis=2)
    terms = [
        own,
        below,
        above,
        extended[:-2, 1:-1],
        extended[2:, 1:-1],
        extended[1:-1, :-2],
        extended[1:-1, 2:],
    ]
    total = jnp.zeros((rows_a * rows_b * layers_n, width), jnp.float32)
    for index in range(7):
        total = total + jnp.dot(
            terms[index].reshape(-1, width), coupling[index], preferred_element_type=jnp.float32
        )
    return total.reshape(rows_a, rows_b, layers_n, width).astype(jnp.bfloat16)


def stencil(extended):
    center = extended[1:-1, 1:-1]
    beside_all = extended[2:, 1:-1] + extended[:-2, 1:-1] + extended[1:-1, 2:] + extended[1:-1, :-2]
    return 1.3 * center - 0.2 * beside_all


def prior_once(field):
    extended = padded_2(field.astype(jnp.bfloat16), (("gx", 0), ("gy", 1)), 1).astype(field.dtype)
    return stencil(extended)


def per_device(adjoint_trace, coupling, log_friction, send_column, live_count, target_node):
    rows_a, rows_b, layers_n, width = adjoint_trace.shape
    padded = padded_2(adjoint_trace, (("gx", 0), ("gy", 1)), 1)
    trace_update = couple(padded, coupling)
    owners = lax.axis_size("gy")
    faces_dev = rows_a * rows_b
    slots = faces_dev // owners
    blocks_all = trace_update[:, :, 0, :].reshape(faces_dev, width)
    order = send_column.reshape(owners, slots)
    picked = blocks_all[order]
    live = jnp.arange(slots, dtype=jnp.int32)[None, :] < live_count.reshape(owners)[:, None]
    nodes = jnp.where(live, target_node.reshape(owners, slots), -1)
    received, received_nodes = (
        lax.all_to_all(picked, "gy", split_axis=0, concat_axis=0, tiled=True),
        lax.all_to_all(nodes, "gy", split_axis=0, concat_axis=0, tiled=True),
    )
    tile_a, tile_b = (log_friction.shape[0], log_friction.shape[1])
    tile_nodes = tile_a * tile_b
    onehot = (
        jnp.arange(tile_nodes, dtype=jnp.int32)[:, None] == received_nodes.reshape(-1)[None, :]
    ).astype(jnp.bfloat16)
    misfit = jnp.dot(
        onehot, received.reshape(-1, width), preferred_element_type=jnp.float32
    ).reshape(tile_a, tile_b, width)
    prior = prior_once(prior_once(log_friction))
    friction_gradient = jnp.exp(log_friction) * misfit + prior
    return (trace_update, friction_gradient)


def solution(mesh):
    in_specs = (
        P("gx", "gy", None, None),
        P(),
        P("gx", "gy", None),
        P("gx", "gy", None),
        P("gx", "gy", None),
        P("gx", "gy", None, None),
    )
    out_specs = (P("gx", "gy", None, None), P("gx", "gy", None))
    return jax.shard_map(
        per_device, mesh=mesh, in_specs=in_specs, out_specs=out_specs, check_vma=False
    )
```

profile of v0, /device:TPU:497, one launch (start us, length us, event | category | flops | bytes accessed | tf_op | source)
XLA Modules:
  0.0 99.7 jit_solution(2502654100199984615)
XLA Ops:
  0.6 0.8 convert_element_type.21
  2.1 4.5 %collective-permute-start.4 = (bf16[1,16,128]{2,1,0:T(8,128)(2,1)}, bf16[1,16,128]{2,1,0:T(8,128)(2,1)}, u32[]{:S(2)}, u32[]{:S(2)}) collective-permute-start(bf16[1,16,128]{2,1,0:T(8,128)(2,1)} %get-tuple-element.19), channel_id=1, source_target_pairs={{0,16},{16,32},{32,48},{48,64},{64,80},{80,96},{96,112},{112,128},... | collective-permute-start | bytes 12296 | tf_op jit(solution)/shard_map/ppermute | solution.py:12
  6.6 1.9 %collective-permute-start.5 = (bf16[1,16,128]{2,1,0:T(8,128)(2,1)}, bf16[1,16,128]{2,1,0:T(8,128)(2,1)}, u32[]{:S(2)}, u32[]{:S(2)}) collective-permute-start(bf16[1,16,128]{2,1,0:T(8,128)(2,1)} %get-tuple-element.20), channel_id=1, source_target_pairs={{16,0},{32,16},{48,32},{64,48},{80,64},{96,80},{112,96},{128,112},... | collective-permute-start | bytes 12296 | tf_op jit(solution)/shard_map/ppermute | solution.py:15
  8.5 1.5 %fusion.33 = (bf16[1,16,16,128]{3,2,1,0:T(8,128)(2,1)}, bf16[1,16,16,128]{3,2,1,0:T(8,128)(2,1)}) fusion(bf16[16,16,16,128]{3,2,1,0:T(8,128)(2,1)} %param.6), kind=kLoop, calls=%fused_computation.65 | loop fusion | bytes 262144 | tf_op jit(solution)/shard_map/slice | solution.py:15
  10.1 6.7 %collective-permute-start = (bf16[1,16,16,128]{3,2,1,0:T(8,128)(2,1)}, bf16[1,16,16,128]{3,2,1,0:T(8,128)(2,1)S(1)}, u32[]{:S(2)}, u32[]{:S(2)}) collective-permute-start(bf16[1,16,16,128]{3,2,1,0:T(8,128)(2,1)} %get-tuple-element.12), channel_id=1, source_target_pairs={{0,16},{16,32},{32,48},{48,64},{64,80},{80,96},{96,112},{112,128},... | collective-permute-start | bytes 196616 | tf_op jit(solution)/shard_map/ppermute | solution.py:12
  16.7 1.9 %collective-permute-start.1 = (bf16[1,16,16,128]{3,2,1,0:T(8,128)(2,1)}, bf16[1,16,16,128]{3,2,1,0:T(8,128)(2,1)S(1)}, u32[]{:S(2)}, u32[]{:S(2)}) collective-permute-start(bf16[1,16,16,128]{3,2,1,0:T(8,128)(2,1)} %get-tuple-element.11), channel_id=1, source_target_pairs={{16,0},{32,16},{48,32},{64,48},{80,64},{96,80},{112,96},{128,112},... | collective-permute-start | bytes 196616 | tf_op jit(solution)/shard_map/ppermute | solution.py:15
  18.7 1.4 %compare_select_fusion = s32[16,1,16]{2,1,0:T(1,128)} fusion(s32[16,1,16]{2,1,0:T(1,128)} %bitcast.57, s32[16]{0:T(128)} %bitcast.58), kind=kLoop, calls=%fused_computation.50 | loop fusion | flops 512 | bytes 2112 | tf_op jit(solution)/shard_map/jit(_where)/select_n | solution.py:65
  20.0 8.3 %all-to-all-start = ((s32[16,1,16]{2,1,0:T(1,128)}), s32[16,1,16]{2,1,0:T(1,128)S(1)}, u32[]{:S(2)}, u32[]{:S(2)}) async-start(s32[16,1,16]{2,1,0:T(1,128)} %compare_select_fusion), calls=%async_computation | async-start | bytes 16384 | tf_op jit(solution)/shard_map/all_to_all | solution.py:68
  28.3 2.1 %fusion.32 = (bf16[16,16,15,128]{3,2,1,0:T(8,128)(2,1)S(1)}, bf16[16,16,15,128]{3,2,1,0:T(8,128)(2,1)S(1)}) fusion(bf16[16,16,16,128]{3,2,1,0:T(8,128)(2,1)} %param.6), kind=kLoop, calls=%fused_computation.64 | loop fusion | bytes 3932160 | tf_op jit(solution)/shard_map/slice | solution.py:25
  33.5 1.1 %reduce.6 = s32[256]{0:T(256)} reduce(s32[1,1,256]{2,1,0:T(1,128)S(1)} %copy-done.6, s32[]{:T(128)} %broadcast.82), dimensions={0,1}, to_apply=%param.9.reduce_sub_computation.3 | reduce | bytes 2052 | tf_op args[3]
  34.6 0.7 reshape.143
  35.4 1.3 %pad_maximum_fusion.9 = (bf16[10,1,128]{2,1,0:T(2,128)(2,1)}, bf16[10,1,128]{2,1,0:T(2,128)(2,1)}) fusion(bf16[1,16,128]{2,1,0:T(8,128)(2,1)} %collective-permute-done.5, bf16[8,16,128]{2,1,0:T(8,128)(2,1)S(1)} %convert_element_type.21, bf16[1,16,128]{2,1,0:T(8,128)(2,1)} %collective-permute-done.4), kind=kLoop, calls=%fused_computation.60 | loop fusion | flops 15360 | bytes 46080 | tf_op jit(solution)/shard_map/slice | solution.py:13
  36.7 3.5 %collective-permute-start.6 = (bf16[10,1,128]{2,1,0:T(2,128)(2,1)}, bf16[10,1,128]{2,1,0:T(2,128)(2,1)}, u32[]{:S(2)}, u32[]{:S(2)}) collective-permute-start(bf16[10,1,128]{2,1,0:T(2,128)(2,1)} %get-tuple-element.15), channel_id=1, source_target_pairs={{0,1},{1,2},{2,3},{3,4},{4,5},{5,6},{6,7},{7,8},{8,9},{9,10},{10,1... | collective-permute-start | bytes 7688 | tf_op jit(solution)/shard_map/ppermute | solution.py:12
  40.2 1.9 %collective-permute-start.7 = (bf16[10,1,128]{2,1,0:T(2,128)(2,1)}, bf16[10,1,128]{2,1,0:T(2,128)(2,1)}, u32[]{:S(2)}, u32[]{:S(2)}) collective-permute-start(bf16[10,1,128]{2,1,0:T(2,128)(2,1)} %get-tuple-element.16), channel_id=1, source_target_pairs={{1,0},{2,1},{3,2},{4,3},{5,4},{6,5},{7,6},{8,7},{9,8},{10,9},{11,1... | collective-permute-start | bytes 7688 | tf_op jit(solution)/shard_map/ppermute | solution.py:15
  42.7 1.3 %reshape.147 = s32[256]{0:T(256)} reshape(s32[16,16,1]{1,0,2:T(8,128)} %compare_select_fusion.1) | data formatting | bytes 2048 | tf_op jit(solution)/shard_map/select_n | solution.py:63
  44.1 1.4 %collective-permute-done.7 = bf16[10,1,128]{2,1,0:T(2,128)(2,1)} collective-permute-done((bf16[10,1,128]{2,1,0:T(2,128)(2,1)}, bf16[10,1,128]{2,1,0:T(2,128)(2,1)}, u32[]{:S(2)}, u32[]{:S(2)}) %collective-permute-start.7) | collective-permute-done | bytes 2592 | tf_op jit(solution)/shard_map/ppermute | solution.py:15
  45.5 0.7 maximum_convert_fusion
  46.3 7.0 %collective-permute-start.8 = (bf16[1,16,128]{2,1,0:T(8,128)(2,1)S(1)}, bf16[1,16,128]{2,1,0:T(8,128)(2,1)S(1)}, u32[]{:S(2)}, u32[]{:S(2)}) collective-permute-start(bf16[1,16,128]{2,1,0:T(8,128)(2,1)S(1)} %get-tuple-element.17), channel_id=1, source_target_pairs={{0,16},{16,32},{32,48},{48,64},{64,80},{80,96},{96,112},{112,128},... | collective-permute-start | bytes 12296 | tf_op jit(solution)/shard_map/ppermute | solution.py:12
  53.2 1.9 %collective-permute-start.9 = (bf16[1,16,128]{2,1,0:T(8,128)(2,1)S(1)}, bf16[1,16,128]{2,1,0:T(8,128)(2,1)S(1)}, u32[]{:S(2)}, u32[]{:S(2)}) collective-permute-start(bf16[1,16,128]{2,1,0:T(8,128)(2,1)S(1)} %get-tuple-element.18), channel_id=1, source_target_pairs={{16,0},{32,16},{48,32},{64,48},{80,64},{96,80},{112,96},{128,112},... | collective-permute-start | bytes 12296 | tf_op jit(solution)/shard_map/ppermute | solution.py:15
  55.8 5.1 %collective-permute-done.9 = bf16[1,16,128]{2,1,0:T(8,128)(2,1)S(1)} collective-permute-done((bf16[1,16,128]{2,1,0:T(8,128)(2,1)S(1)}, bf16[1,16,128]{2,1,0:T(8,128)(2,1)S(1)}, u32[]{:S(2)}, u32[]{:S(2)}) %collective-permute-start.9) | collective-permute-done | bytes 4128 | tf_op jit(solution)/shard_map/ppermute | solution.py:15
  61.5 3.7 %collective-permute-start.10 = (bf16[10,1,128]{2,1,0:T(2,128)(2,1)}, bf16[10,1,128]{2,1,0:T(2,128)(2,1)}, u32[]{:S(2)}, u32[]{:S(2)}) collective-permute-start(bf16[10,1,128]{2,1,0:T(2,128)(2,1)} %get-tuple-element.13), channel_id=1, source_target_pairs={{0,1},{1,2},{2,3},{3,4},{4,5},{5,6},{6,7},{7,8},{8,9},{9,10},{10,1... | collective-permute-start | bytes 7688 | tf_op jit(solution)/shard_map/ppermute | solution.py:12
  65.2 1.9 %collective-permute-start.11 = (bf16[10,1,128]{2,1,0:T(2,128)(2,1)}, bf16[10,1,128]{2,1,0:T(2,128)(2,1)}, u32[]{:S(2)}, u32[]{:S(2)}) collective-permute-start(bf16[10,1,128]{2,1,0:T(2,128)(2,1)} %get-tuple-element.14), channel_id=1, source_target_pairs={{1,0},{2,1},{3,2},{4,3},{5,4},{6,5},{7,6},{8,7},{9,8},{10,9},{11,1... | collective-permute-start | bytes 7688 | tf_op jit(solution)/shard_map/ppermute | solution.py:15
  67.9 3.6 %collective-permute-start.2 = (bf16[18,1,16,128]{3,2,1,0:T(8,128)(2,1)S(1)}, bf16[18,1,16,128]{3,2,1,0:T(8,128)(2,1)S(1)}, u32[]{:S(2)}, u32[]{:S(2)}) collective-permute-start(bf16[18,1,16,128]{3,2,1,0:T(8,128)(2,1)S(1)} %get-tuple-element.4), channel_id=1, source_target_pairs={{0,1},{1,2},{2,3},{3,4},{4,5},{5,6},{6,7},{7,8},{8,9},{9,10},{10,1... | collective-permute-start | bytes 221192 | tf_op jit(solution)/shard_map/ppermute | solution.py:12
  71.6 1.9 %collective-permute-start.3 = (bf16[18,1,16,128]{3,2,1,0:T(8,128)(2,1)S(1)}, bf16[18,1,16,128]{3,2,1,0:T(8,128)(2,1)S(1)}, u32[]{:S(2)}, u32[]{:S(2)}) collective-permute-start(bf16[18,1,16,128]{3,2,1,0:T(8,128)(2,1)S(1)} %get-tuple-element.5), channel_id=1, source_target_pairs={{1,0},{2,1},{3,2},{4,3},{5,4},{6,5},{7,6},{8,7},{9,8},{10,9},{11,1... | collective-permute-start | bytes 221192 | tf_op jit(solution)/shard_map/ppermute | solution.py:15
  73.9 3.3 %collective-permute-done.3 = bf16[18,1,16,128]{3,2,1,0:T(8,128)(2,1)S(1)} collective-permute-done((bf16[18,1,16,128]{3,2,1,0:T(8,128)(2,1)S(1)}, bf16[18,1,16,128]{3,2,1,0:T(8,128)(2,1)S(1)}, u32[]{:S(2)}, u32[]{:S(2)}) %collective-permute-start.3) | collective-permute-done | bytes 73760 | tf_op jit(solution)/shard_map/ppermute | solution.py:15
  78.2 0.8 fusion.3
  79.0 1.0 copy-done.1
  80.1 1.5 %gather_fusion = bf16[256,128]{1,0:T(8,128)(2,1)} fusion(bf16[256,128]{1,0:T(8,128)(2,1)S(1)} %bitcast.47, s32[1024]{0:T(1024)S(1)} %pad_clamp_fusion), kind=kCustom, calls=%fused_computation | custom fusion | bytes 132096 | tf_op jit(solution)/shard_map/gather | solution.py:63
  81.6 9.5 %all-to-all-start.1 = ((bf16[16,16,128]{2,1,0:T(8,128)(2,1)}), bf16[16,16,128]{2,1,0:T(8,128)(2,1)S(1)}, u32[]{:S(2)}, u32[]{:S(2)}) async-start(bf16[16,16,128]{2,1,0:T(8,128)(2,1)} %bitcast.18), calls=%async_computation.1 | async-start | bytes 131072 | tf_op jit(solution)/shard_map/all_to_all | solution.py:67
  91.8 0.7 maximum_convert_fusion.1
  92.5 6.4 %all-to-all-done.1 = bf16[16,16,128]{2,1,0:T(8,128)(2,1)S(1)} async-done(((bf16[16,16,128]{2,1,0:T(8,128)(2,1)}), bf16[16,16,128]{2,1,0:T(8,128)(2,1)S(1)}, u32[]{:S(2)}, u32[]{:S(2)}) %all-to-all-start.1) | async-done | bytes 65568 | tf_op jit(solution)/shard_map/all_to_all | solution.py:67
  98.9 0.8 fusion.4
  (48 shorter events, 8.3 us)
Async XLA Ops:
  2.1 33.3 %collective-permute-start.4 = (bf16[1,16,128]{2,1,0:T(8,128)(2,1)}, bf16[1,16,128]{2,1,0:T(8,128)(2,1)}, u32[]{:S(2)}, u32[]{:S(2)}) collective-permute-start(bf16[1,16,128]{2,1,0:T(8,128)(2,1)} %get-tuple-element.19), channel_id=1, source_target_pairs={{0,16},{16,32},{32,48},{48,64},{64,80},{80,96},{96,112},{112,128},... | collective-permute-start | bytes 12296 | tf_op jit(solution)/shard_map/ppermute | solution.py:12
  6.6 28.8 %collective-permute-start.5 = (bf16[1,16,128]{2,1,0:T(8,128)(2,1)}, bf16[1,16,128]{2,1,0:T(8,128)(2,1)}, u32[]{:S(2)}, u32[]{:S(2)}) collective-permute-start(bf16[1,16,128]{2,1,0:T(8,128)(2,1)} %get-tuple-element.20), channel_id=1, source_target_pairs={{16,0},{32,16},{48,32},{64,48},{80,64},{96,80},{112,96},{128,112},... | collective-permute-start | bytes 12296 | tf_op jit(solution)/shard_map/ppermute | solution.py:15
  10.1 57.1 %collective-permute-start = (bf16[1,16,16,128]{3,2,1,0:T(8,128)(2,1)}, bf16[1,16,16,128]{3,2,1,0:T(8,128)(2,1)S(1)}, u32[]{:S(2)}, u32[]{:S(2)}) collective-permute-start(bf16[1,16,16,128]{3,2,1,0:T(8,128)(2,1)} %get-tuple-element.12), channel_id=1, source_target_pairs={{0,16},{16,32},{32,48},{48,64},{64,80},{80,96},{96,112},{112,128},... | collective-permute-start | bytes 196616 | tf_op jit(solution)/shard_map/ppermute | solution.py:12
  16.7 50.4 %collective-permute-start.1 = (bf16[1,16,16,128]{3,2,1,0:T(8,128)(2,1)}, bf16[1,16,16,128]{3,2,1,0:T(8,128)(2,1)S(1)}, u32[]{:S(2)}, u32[]{:S(2)}) collective-permute-start(bf16[1,16,16,128]{3,2,1,0:T(8,128)(2,1)} %get-tuple-element.11), channel_id=1, source_target_pairs={{16,0},{32,16},{48,32},{64,48},{80,64},{96,80},{112,96},{128,112},... | collective-permute-start | bytes 196616 | tf_op jit(solution)/shard_map/ppermute | solution.py:15
  20.0 61.5 %all-to-all-start = ((s32[16,1,16]{2,1,0:T(1,128)}), s32[16,1,16]{2,1,0:T(1,128)S(1)}, u32[]{:S(2)}, u32[]{:S(2)}) async-start(s32[16,1,16]{2,1,0:T(1,128)} %compare_select_fusion), calls=%async_computation | async-start | bytes 16384 | tf_op jit(solution)/shard_map/all_to_all | solution.py:68
  30.5 1.2 %copy-start = (bf16[16,16,16,128]{3,2,1,0:T(8,128)(2,1)S(1)}, bf16[16,16,16,128]{3,2,1,0:T(8,128)(2,1)}, u32[]{:S(2)}) copy-start(bf16[16,16,16,128]{3,2,1,0:T(8,128)(2,1)} %param.6) | copy-start | bytes 3145732
  30.5 1.2 %copy-start.2 = (bf16[7,128,128]{2,1,0:T(8,128)(2,1)S(1)}, bf16[7,128,128]{2,1,0:T(8,128)(2,1)}, u32[]{:S(2)}) copy-start(bf16[7,128,128]{2,1,0:T(8,128)(2,1)} %param.7) | copy-start | bytes 688132
  32.6 0.9 copy-start.6
  36.7 7.4 %collective-permute-start.6 = (bf16[10,1,128]{2,1,0:T(2,128)(2,1)}, bf16[10,1,128]{2,1,0:T(2,128)(2,1)}, u32[]{:S(2)}, u32[]{:S(2)}) collective-permute-start(bf16[10,1,128]{2,1,0:T(2,128)(2,1)} %get-tuple-element.15), channel_id=1, source_target_pairs={{0,1},{1,2},{2,3},{3,4},{4,5},{5,6},{6,7},{7,8},{8,9},{9,10},{10,1... | collective-permute-start | bytes 7688 | tf_op jit(solution)/shard_map/ppermute | solution.py:12
  40.2 5.3 %collective-permute-start.7 = (bf16[10,1,128]{2,1,0:T(2,128)(2,1)}, bf16[10,1,128]{2,1,0:T(2,128)(2,1)}, u32[]{:S(2)}, u32[]{:S(2)}) collective-permute-start(bf16[10,1,128]{2,1,0:T(2,128)(2,1)} %get-tuple-element.16), channel_id=1, source_target_pairs={{1,0},{2,1},{3,2},{4,3},{5,4},{6,5},{7,6},{8,7},{9,8},{10,9},{11,1... | collective-permute-start | bytes 7688 | tf_op jit(solution)/shard_map/ppermute | solution.py:15
  46.3 9.5 %collective-permute-start.8 = (bf16[1,16,128]{2,1,0:T(8,128)(2,1)S(1)}, bf16[1,16,128]{2,1,0:T(8,128)(2,1)S(1)}, u32[]{:S(2)}, u32[]{:S(2)}) collective-permute-start(bf16[1,16,128]{2,1,0:T(8,128)(2,1)S(1)} %get-tuple-element.17), channel_id=1, source_target_pairs={{0,16},{16,32},{32,48},{48,64},{64,80},{80,96},{96,112},{112,128},... | collective-permute-start | bytes 12296 | tf_op jit(solution)/shard_map/ppermute | solution.py:12
  53.2 7.7 %collective-permute-start.9 = (bf16[1,16,128]{2,1,0:T(8,128)(2,1)S(1)}, bf16[1,16,128]{2,1,0:T(8,128)(2,1)S(1)}, u32[]{:S(2)}, u32[]{:S(2)}) collective-permute-start(bf16[1,16,128]{2,1,0:T(8,128)(2,1)S(1)} %get-tuple-element.18), channel_id=1, source_target_pairs={{16,0},{32,16},{48,32},{64,48},{80,64},{96,80},{112,96},{128,112},... | collective-permute-start | bytes 12296 | tf_op jit(solution)/shard_map/ppermute | solution.py:15
  60.9 6.3 %copy-start.4 = (bf16[1,16,128]{2,1,0:T(8,128)(2,1)}, bf16[1,16,128]{2,1,0:T(8,128)(2,1)S(1)}, u32[]{:S(2)}) copy-start(bf16[1,16,128]{2,1,0:T(8,128)(2,1)S(1)} %collective-permute-done.9) | copy-start | bytes 12292
  61.5 30.2 %collective-permute-start.10 = (bf16[10,1,128]{2,1,0:T(2,128)(2,1)}, bf16[10,1,128]{2,1,0:T(2,128)(2,1)}, u32[]{:S(2)}, u32[]{:S(2)}) collective-permute-start(bf16[10,1,128]{2,1,0:T(2,128)(2,1)} %get-tuple-element.13), channel_id=1, source_target_pairs={{0,1},{1,2},{2,3},{3,4},{4,5},{5,6},{6,7},{7,8},{8,9},{9,10},{10,1... | collective-permute-start | bytes 7688 | tf_op jit(solution)/shard_map/ppermute | solution.py:12
  65.2 26.5 %collective-permute-start.11 = (bf16[10,1,128]{2,1,0:T(2,128)(2,1)}, bf16[10,1,128]{2,1,0:T(2,128)(2,1)}, u32[]{:S(2)}, u32[]{:S(2)}) collective-permute-start(bf16[10,1,128]{2,1,0:T(2,128)(2,1)} %get-tuple-element.14), channel_id=1, source_target_pairs={{1,0},{2,1},{3,2},{4,3},{5,4},{6,5},{7,6},{8,7},{9,8},{10,9},{11,1... | collective-permute-start | bytes 7688 | tf_op jit(solution)/shard_map/ppermute | solution.py:15
  67.9 6.0 %collective-permute-start.2 = (bf16[18,1,16,128]{3,2,1,0:T(8,128)(2,1)S(1)}, bf16[18,1,16,128]{3,2,1,0:T(8,128)(2,1)S(1)}, u32[]{:S(2)}, u32[]{:S(2)}) collective-permute-start(bf16[18,1,16,128]{3,2,1,0:T(8,128)(2,1)S(1)} %get-tuple-element.4), channel_id=1, source_target_pairs={{0,1},{1,2},{2,3},{3,4},{4,5},{5,6},{6,7},{7,8},{8,9},{9,10},{10,1... | collective-permute-start | bytes 221192 | tf_op jit(solution)/shard_map/ppermute | solution.py:12
  71.6 5.7 %collective-permute-start.3 = (bf16[18,1,16,128]{3,2,1,0:T(8,128)(2,1)S(1)}, bf16[18,1,16,128]{3,2,1,0:T(8,128)(2,1)S(1)}, u32[]{:S(2)}, u32[]{:S(2)}) collective-permute-start(bf16[18,1,16,128]{3,2,1,0:T(8,128)(2,1)S(1)} %get-tuple-element.5), channel_id=1, source_target_pairs={{1,0},{2,1},{3,2},{4,3},{5,4},{6,5},{7,6},{8,7},{9,8},{10,9},{11,1... | collective-permute-start | bytes 221192 | tf_op jit(solution)/shard_map/ppermute | solution.py:15
  78.2 13.5 %copy-start.5 = (bf16[1,16,128]{2,1,0:T(8,128)(2,1)S(1)}, bf16[1,16,128]{2,1,0:T(8,128)(2,1)}, u32[]{:S(2)}) copy-start(bf16[1,16,128]{2,1,0:T(8,128)(2,1)} %copy-done.4) | copy-start | bytes 12292
  78.2 20.6 %copy-start.3 = (f32[8,16,128]{2,1,0:T(8,128)S(1)}, f32[8,16,128]{2,1,0:T(8,128)}, u32[]{:S(2)}) copy-start(f32[8,16,128]{2,1,0:T(8,128)} %param.8) | copy-start | bytes 196612
  79.0 1.0 copy-start.1
  81.6 17.3 %all-to-all-start.1 = ((bf16[16,16,128]{2,1,0:T(8,128)(2,1)}), bf16[16,16,128]{2,1,0:T(8,128)(2,1)S(1)}, u32[]{:S(2)}, u32[]{:S(2)}) async-start(bf16[16,16,128]{2,1,0:T(8,128)(2,1)} %bitcast.18), calls=%async_computation.1 | async-start | bytes 131072 | tf_op jit(solution)/shard_map/all_to_all | solution.py:67
where the time goes:
time: 101 us; the launch traced here: 99.7 us
  starting transfers between devices  58.3 us (58%)
  waiting for transfers between devices  16.2 us (16%)
  local copies, waits for them, and re-layouts  10.7 us (11%)
  other arithmetic  9.43 us (9%)
  matrix products  4.11 us (4%)
    ppermute x6, starting transfers between devices, padded_2(): lax.ppermute(lax.slice_in_dim(block, block.shape[dim] - width, None, axis...  29 us
    ppermute x6, starting transfers between devices, padded_2(): lax.ppermute(lax.slice_in_dim(block, 0, width, axis=dim), axis, backward)  11.5 us
    ppermute x6, waiting for transfers between devices, padded_2(): lax.ppermute(lax.slice_in_dim(block, 0, width, axis=dim), axis, backward)  9.83 us
    all_to_all x1, starting transfers between devices, per_device(): lax.all_to_all(picked, 'gy', split_axis=0, concat_axis=0, tiled=True)  9.49 us
    all_to_all x1, starting transfers between devices, per_device(): lax.all_to_all(nodes, 'gy', split_axis=0, concat_axis=0, tiled=True)  8.29 us
    all_to_all x1, waiting for transfers between devices, per_device(): lax.all_to_all(picked, 'gy', split_axis=0, concat_axis=0, tiled=True)  6.37 us
    dot_general x7, matrix products, couple(): jnp.dot(terms[index].reshape(-1, width), coupling[index], preferred_eleme...  3.26 us
    slice x1, local copies, waits for them, and re-layouts, couple(): above = jnp.concatenate([own[:, :, 1:], zeros_layer], axis=2)  2.12 us
  transfers between devices with their start and end apart: 14, of which 4 were waited for; matrix products, arithmetic and copies ran while one was open for 20% of the time, Pallas kernels for 0%

commit v1 on v0

v1 whole, which is shorter than its diff:
```python
import functools

import jax
import jax.numpy as jnp
from jax import lax
from jax.experimental import pallas as pl
from jax.experimental.pallas import tpu as pltpu
from jax.sharding import PartitionSpec as P

F32 = jnp.float32
BF16 = jnp.bfloat16
VMEM = pl.BlockSpec(memory_space=pltpu.VMEM)
ANY = pl.BlockSpec(memory_space=pl.ANY)
MSG = 24


def dot(a, b):
    return jnp.dot(a, b, preferred_element_type=F32)


def shift(block, axis, step):
    count = lax.axis_size(axis)
    pairs = [(i, i + step) for i in range(count) if 0 <= i + step < count]
    return lax.ppermute(block, axis, pairs)


def pack_body(adj, logf, to_a_hi, to_a_lo, to_b_hi, to_b_lo, sems):
    ca, cb = adj.shape[0], adj.shape[1]
    pa, pb = logf.shape[0], logf.shape[1]
    copies = [
        pltpu.make_async_copy(adj.at[ca - 1], to_a_hi.at[pl.ds(0, cb)], sems.at[0]),
        pltpu.make_async_copy(adj.at[0], to_a_lo.at[pl.ds(0, cb)], sems.at[1]),
        pltpu.make_async_copy(adj.at[:, cb - 1], to_b_hi.at[pl.ds(0, ca)], sems.at[2]),
        pltpu.make_async_copy(adj.at[:, 0], to_b_lo.at[pl.ds(0, ca)], sems.at[3]),
    ]
    for copy in copies:
        copy.start()
    to_a_hi[cb:cb + 2] = logf[pa - 2:pa].astype(BF16)
    to_a_lo[cb:cb + 2] = logf[0:2].astype(BF16)
    to_b_hi[ca] = jnp.concatenate([logf[:, pb - 2, :], logf[:, pb - 1, :]], axis=0).astype(BF16)
    to_b_lo[ca] = jnp.concatenate([logf[:, 0, :], logf[:, 1, :]], axis=0).astype(BF16)
    for copy in copies:
        copy.wait()


def local_body(adj, coupling, send, live, nodes, base, pick, ids, wide):
    ca, cb, nl, width = adj.shape
    faces = ca * cb
    for a in range(ca):
        wide[a * cb * 8:(a + 1) * cb * 8] = adj[a, :, 0:8, :].astype(F32).reshape(cb * 8, width)
    low = wide[pl.ds(0, faces, stride=8), :].astype(BF16)
    above = wide[pl.ds(1, faces, stride=8), :].astype(BF16)
    total = dot(low, coupling[0]) + dot(above, coupling[2])
    zeros = jnp.zeros((cb, width), F32)
    total = total + jnp.concatenate([zeros, dot(low[:faces - cb], coupling[3])], axis=0)
    total = total + jnp.concatenate([dot(low[cb:], coupling[4]), zeros], axis=0)
    column = lax.broadcasted_iota(jnp.int32, (faces, width), 0) % cb
    before = pltpu.roll(dot(low, coupling[5]), 1, 0)
    after = pltpu.roll(dot(low, coupling[6]), faces - 1, 0)
    total = total + jnp.where(column > 0, before, 0.0) + jnp.where(column < cb - 1, after, 0.0)
    base[...] = total
    face = lax.broadcasted_iota(jnp.int32, (faces, faces), 0)
    picked_by = jnp.where(send[0] == face, 1.0, 0.0)
    pick[...] = picked_by.T.astype(BF16)
    owners, slots = nodes.shape[2], nodes.shape[3]
    sub = lax.broadcasted_iota(jnp.int32, (slots, width), 0)
    lane = lax.broadcasted_iota(jnp.int32, (slots, width), 1)
    spread = jnp.where(lane % slots == sub, 1.0, 0.0).astype(BF16)
    listed = dot(nodes[0, 0].astype(F32).astype(BF16), spread) + 1.0
    owner = lax.broadcasted_iota(jnp.int32, (owners, owners), 0)
    other = lax.broadcasted_iota(jnp.int32, (owners, owners), 1)
    counts = jnp.sum(jnp.where(owner == other, live[0].astype(F32), 0.0), axis=1, keepdims=True)
    lane = lax.broadcasted_iota(jnp.int32, (owners, width), 1)
    mine = lane // slots == lax.axis_index("gy") % (width // slots)
    alive = (lane % slots).astype(F32) < counts
    ids[...] = jnp.where(jnp.logical_and(mine, alive), listed, 0.0)


def message_body(base, pick, ids, coupling, a_lo, a_hi, b_lo, b_hi, out, total, wide):
    faces, width = base.shape
    owners, slots = out.shape[0], faces // out.shape[0]
    cb = a_lo.shape[0] - 2
    ca = b_lo.shape[0] - 1
    for k, halo in enumerate((a_lo, a_hi, b_lo, b_hi)):
        rows = cb if k < 2 else ca
        wide[k * rows * 8:(k + 1) * rows * 8] = (
            halo[0:rows, 0:8, :].astype(F32).reshape(rows * 8, width)
        )

    def edge(k, rows):
        return wide[pl.ds(k * rows * 8, rows, stride=8), :].astype(BF16)

    total[...] = base[...]
    total[0:cb] += dot(edge(0, cb), coupling[3])
    total[faces - cb:faces] += dot(edge(1, cb), coupling[4])
    total[pl.ds(0, ca, stride=cb), :] += dot(edge(2, ca), coupling[5])
    total[pl.ds(cb - 1, ca, stride=cb), :] += dot(edge(3, ca), coupling[6])
    picked = dot(pick[...], total[...].astype(BF16)).astype(BF16)
    here = lax.axis_index("gy")
    pb = a_lo.shape[1]
    top = a_lo[cb + 1].astype(F32)
    bottom = a_hi[cb].astype(F32)
    sub = lax.broadcasted_iota(jnp.int32, (MSG - slots, width), 0)

    def extra(o, column):
        rows = jnp.where(sub == 0, ids[o:o + 1, :], 0.0)
        rows = jnp.where(sub == 1, top[column:column + 1, :], rows)
        return jnp.where(sub == 2, bottom[column:column + 1, :], rows)

    for o in range(owners):
        out[o, 0:slots] = picked[o * slots:(o + 1) * slots]
        out[o, slots:MSG] = jnp.where(o > here, extra(o, pb - 1), extra(o, 0)).astype(BF16)


def update_body(adj, coupling, logf, a_lo, a_hi, b_lo, b_hi, after, out, prior, scale,
                held, field, once, sems):
    del after
    ca, cb, nl, width = adj.shape
    rows = cb * nl
    layer = lax.broadcasted_iota(jnp.int32, (rows, width), 0) % nl
    copies = []
    for a in range(ca):
        own = adj[a].reshape(rows, width)
        down = adj[a - 1] if a > 0 else a_lo[0:cb]
        up = adj[a + 1] if a < ca - 1 else a_hi[0:cb]
        total = dot(own, coupling[0])
        below = pltpu.roll(dot(own, coupling[1]), 1, 0)
        above = pltpu.roll(dot(own, coupling[2]), rows - 1, 0)
        total = total + jnp.where(layer > 0, below, 0.0) + jnp.where(layer < nl - 1, above, 0.0)
        total = total + dot(down.reshape(rows, width), coupling[3])
        total = total + dot(up.reshape(rows, width), coupling[4])
        before = jnp.concatenate([b_lo[a], own[:rows - nl]], axis=0)
        behind = jnp.concatenate([own[nl:], b_hi[a]], axis=0)
        total = total + dot(before, coupling[5]) + dot(behind, coupling[6])
        held[a] = total.astype(BF16).reshape(cb, nl, width)
        copy = pltpu.make_async_copy(held.at[a], out.at[a], sems.at[a])
        copy.start()
        copies.append(copy)
    pa, pb = logf.shape[0], logf.shape[1]
    off = 8
    field[...] = jnp.zeros(field.shape, F32)
    field[2:pa + 2, off:off + pb] = logf[...]
    field[0:2, off:off + pb] = a_lo[cb:cb + 2].astype(F32)
    field[pa + 2:pa + 4, off:off + pb] = a_hi[cb:cb + 2].astype(F32)
    side_lo, side_hi = b_lo[ca].astype(F32), b_hi[ca].astype(F32)
    for r in range(pa):
        for c in range(2):
            field[r + 2, off - 2 + c:off - 1 + c] = side_lo[c * pa + r:c * pa + r + 1]
            field[r + 2, off + pb + c:off + pb + c + 1] = side_hi[c * pa + r:c * pa + r + 1]

    def stencil(ref, a, b, na, nb):
        beside = ref[a + 1:a + 1 + na, b:b + nb] + ref[a - 1:a - 1 + na, b:b + nb]
        beside = beside + ref[a:a + na, b + 1:b + 1 + nb] + ref[a:a + na, b - 1:b - 1 + nb]
        return 1.3 * ref[a:a + na, b:b + nb] - 0.2 * beside

    i, j = lax.axis_index("gx"), lax.axis_index("gy")
    last_i, last_j = lax.axis_size("gx") - 1, lax.axis_size("gy") - 1
    once[...] = jnp.zeros(once.shape, F32)
    once[1:pa + 1, off:off + pb] = stencil(field, 2, off, pa, pb)
    once[0:1, off:off + pb] = jnp.where(i > 0, stencil(field, 1, off, 1, pb), 0.0)
    once[pa + 1:pa + 2, off:off + pb] = jnp.where(i < last_i, stencil(field, pa + 2, off, 1, pb), 0.0)
    once[1:pa + 1, off - 1:off] = jnp.where(j > 0, stencil(field, 2, off - 1, pa, 1), 0.0)
    once[1:pa + 1, off + pb:off + pb + 1] = jnp.where(j < last_j, stencil(field, 2, off + pb, pa, 1), 0.0)
    prior[...] = stencil(once, 1, off, pa, pb)
    scale[...] = jnp.exp(logf[...])
    for copy in copies:
        copy.wait()


def gradient_body(got, prior, scale, out):
    owners, _, width = got.shape
    pa, pb, _ = out.shape
    slots = 16
    per_row = width // slots
    tail = got[:, slots:MSG, :].astype(F32)
    listed = [jnp.sum(tail[k:k + per_row], axis=0)[0:1] for k in range(0, owners, per_row)]
    listed = jnp.concatenate(listed, axis=1)
    node = lax.broadcasted_iota(jnp.int32, (pa * pb, owners * slots), 0).astype(F32) + 1.0
    onehot = jnp.where(node == listed, 1.0, 0.0).astype(BF16)
    blocks = got[:, 0:slots, :].reshape(owners * slots, width)
    misfit = dot(onehot, blocks).reshape(pa, pb, width)
    out[...] = scale[...] * misfit + prior[...]
    j = lax.axis_index("gy")
    for side, column in ((-1, 0), (1, pb - 1)):
        inside = jnp.logical_and(j + side >= 0, j + side < owners)
        source = jnp.clip(j + side, 0, owners - 1)
        corners = jnp.where(inside, got[source, slots:MSG, :].astype(F32) * 0.08, 0.0)
        out[0, column:column + 1] += corners[1:2]
        out[pa - 1, column:column + 1] += corners[2:3]


def cost(flops, size):
    return pl.CostEstimate(flops=flops, bytes_accessed=size, transcendentals=0)


def per_device(adjoint_trace, coupling, log_friction, send_column, live_count, target_node):
    ca, cb, nl, width = adjoint_trace.shape
    pa, pb, _ = log_friction.shape
    owners = lax.axis_size("gy")
    faces = ca * cb
    shape = jax.ShapeDtypeStruct
    wire = pltpu.CompilerParams(vmem_limit_bytes=16 * 2**20)

    to_a_hi, to_a_lo, to_b_hi, to_b_lo = pl.pallas_call(
        pack_body,
        out_shape=(
            shape((cb + 2, nl, width), BF16),
            shape((cb + 2, nl, width), BF16),
            shape((ca + 1, nl, width), BF16),
            shape((ca + 1, nl, width), BF16),
        ),
        in_specs=[ANY, VMEM],
        out_specs=(VMEM,) * 4,
        scratch_shapes=[pltpu.SemaphoreType.DMA((4,))],
        compiler_params=wire,
        name="pack",
    )(adjoint_trace, log_friction)
    a_lo = shift(to_a_hi, "gx", 1)
    a_hi = shift(to_a_lo, "gx", -1)
    b_lo = shift(to_b_hi, "gy", 1)
    b_hi = shift(to_b_lo, "gy", -1)

    base, pick, ids = pl.pallas_call(
        local_body,
        out_shape=(
            shape((faces, width), F32),
            shape((faces, faces), BF16),
            shape((owners, width), F32),
        ),
        in_specs=[VMEM] * 5,
        out_specs=(VMEM,) * 3,
        scratch_shapes=[pltpu.VMEM((faces * 8, width), F32)],
        compiler_params=wire,
        cost_estimate=cost(2 * 6 * faces * width * width, 2 * 2**20),
        name="local",
    )(adjoint_trace, coupling, send_column, live_count, target_node)

    message = pl.pallas_call(
        message_body,
        out_shape=shape((owners, MSG, width), BF16),
        in_specs=[VMEM] * 8,
        out_specs=VMEM,
        scratch_shapes=[
            pltpu.VMEM((faces, width), F32),
            pltpu.VMEM((2 * (ca + cb) * 8, width), F32),
        ],
        compiler_params=wire,
        cost_estimate=cost(2 * faces * faces * width, 2**20),
        name="message",
    )(base, pick, ids, coupling, a_lo, a_hi, b_lo, b_hi)

    received = lax.all_to_all(message, "gy", split_axis=0, concat_axis=0, tiled=True)

    update, prior, scale = pl.pallas_call(
        update_body,
        out_shape=(
            shape(adjoint_trace.shape, BF16),
            shape(log_friction.shape, F32),
            shape(log_friction.shape, F32),
        ),
        in_specs=[VMEM] * 7 + [ANY],
        out_specs=(ANY, VMEM, VMEM),
        scratch_shapes=[
            pltpu.VMEM(adjoint_trace.shape, BF16),
            pltpu.VMEM((pa + 4, pb + 16, width), F32),
            pltpu.VMEM((pa + 2, pb + 16, width), F32),
            pltpu.SemaphoreType.DMA((ca,)),
        ],
        compiler_params=wire,
        cost_estimate=cost(2 * 7 * faces * nl * width * width, 4 * 2**20),
        name="update",
    )(adjoint_trace, coupling, log_friction, a_lo, a_hi, b_lo, b_hi, message)

    gradient = pl.pallas_call(
        gradient_body,
        out_shape=shape(log_friction.shape, F32),
        in_specs=[VMEM] * 3,
        out_specs=VMEM,
        compiler_params=wire,
        cost_estimate=cost(2 * pa * pb * faces * width, 2**19),
        name="gradient",
    )(received, prior, scale)
    return update, gradient


def solution(mesh):
    in_specs = (
        P("gx", "gy", None, None),
        P(),
        P("gx", "gy", None),
        P("gx", "gy", None),
        P("gx", "gy", None),
        P("gx", "gy", None, None),
    )
    out_specs = (P("gx", "gy", None, None), P("gx", "gy", None))
    return jax.shard_map(
        per_device, mesh=mesh, in_specs=in_specs, out_specs=out_specs, check_vma=False
    )
```

time: 101 us -> 39.6 us (0.39)
  the two profiles are of different devices: /device:TPU:497 before, /device:TPU:513 now
where the time goes in v1:
time: 39.6 us; the launch traced here: 39.2 us
  starting transfers between devices  22.2 us (56%)
  waiting for transfers between devices  8.89 us (22%)
  Pallas kernels  5.23 us (13%)
  local copies, waits for them, and re-layouts  2.09 us (5%)
  between operations  0.77 us (2%)
    ppermute x4, starting transfers between devices, shift(): return lax.ppermute(block, axis, pairs)  14.9 us
    all_to_all x1, starting transfers between devices, per_device(): lax.all_to_all(message, 'gy', split_axis=0, concat_axis=0, tiled=True)  7.3 us
    all_to_all x1, waiting for transfers between devices, per_device(): lax.all_to_all(message, 'gy', split_axis=0, concat_axis=0, tiled=True)  5.58 us
    ppermute x4, waiting for transfers between devices, shift(): return lax.ppermute(block, axis, pairs)  3.31 us
    pallas_call x1, Pallas kernels, per_device(): pl.pallas_call(update_body, out_shape=(shape(adjoint_trace.shape, BF16),...  2.89 us
    unnamed x16, local copies, waits for them, and re-layouts  2.09 us
    pallas_call x1, Pallas kernels, per_device(): pl.pallas_call(message_body, out_shape=shape((owners, MSG, width), BF16),...  0.99 us
    pallas_call x1, Pallas kernels, per_device(): pl.pallas_call(gradient_body, out_shape=shape(log_friction.shape, F32), i...  0.8 us
  transfers between devices with their start and end apart: 5, of which 2 were waited for; matrix products, arithmetic and copies ran while one was open for 0% of the time, Pallas kernels for 8%

profile of v1, /device:TPU:513, one launch (start us, length us, event | category | flops | bytes accessed | tf_op | source)
XLA Modules:
  0.0 39.2 jit_solution(463344123214878141)
XLA Ops:
  0.6 0.0 copy-start
  0.6 1.2 %copy-done = bf16[16,16,16,128]{3,2,1,0:T(8,128)(2,1)S(1)} copy-done((bf16[16,16,16,128]{3,2,1,0:T(8,128)(2,1)S(1)}, bf16[16,16,16,128]{3,2,1,0:T(8,128)(2,1)}, u32[]{:S(2)}) %copy-start) | copy-done | bytes 1048600
  1.9 0.0 copy-start.3
  1.9 0.8 %copy-done.3 = f32[8,16,128]{2,1,0:T(8,128)S(1)} copy-done((f32[8,16,128]{2,1,0:T(8,128)S(1)}, f32[8,16,128]{2,1,0:T(8,128)}, u32[]{:S(2)}) %copy-start.3) | copy-done | bytes 65560
  2.7 0.0 copy-start.2
  2.7 0.0 copy-start.5
  2.7 0.2 pack.1
  2.9 3.3 %collective-permute-start = (bf16[18,16,128]{2,1,0:T(8,128)(2,1)S(1)}, bf16[18,16,128]{2,1,0:T(8,128)(2,1)S(1)}, u32[]{:S(2)}, u32[]{:S(2)}) collective-permute-start(bf16[18,16,128]{2,1,0:T(8,128)(2,1)S(1)} %get-tuple-element.12), channel_id=1, source_target_pairs={{0,16},{16,32},{32,48},{48,64},{64,80},{80,96},{96,112},{112,128},... | collective-permute-start | bytes 221192 | tf_op jit(solution)/shard_map/ppermute | solution.py:24
  6.3 5.3 %collective-permute-start.1 = (bf16[18,16,128]{2,1,0:T(8,128)(2,1)S(1)}, bf16[18,16,128]{2,1,0:T(8,128)(2,1)S(1)}, u32[]{:S(2)}, u32[]{:S(2)}) collective-permute-start(bf16[18,16,128]{2,1,0:T(8,128)(2,1)S(1)} %get-tuple-element.13), channel_id=1, source_target_pairs={{16,0},{32,16},{48,32},{64,48},{80,64},{96,80},{112,96},{128,112},... | collective-permute-start | bytes 221192 | tf_op jit(solution)/shard_map/ppermute | solution.py:24
  11.6 0.0 copy-start.6
  11.6 0.0 copy-start.7
  11.6 4.2 %collective-permute-start.2 = (bf16[17,16,128]{2,1,0:T(8,128)(2,1)S(1)}, bf16[17,16,128]{2,1,0:T(8,128)(2,1)S(1)}, u32[]{:S(2)}, u32[]{:S(2)}) collective-permute-start(bf16[17,16,128]{2,1,0:T(8,128)(2,1)S(1)} %get-tuple-element.14), channel_id=1, source_target_pairs={{0,1},{1,2},{2,3},{3,4},{4,5},{5,6},{6,7},{7,8},{8,9},{9,10},{10,1... | collective-permute-start | bytes 208904 | tf_op jit(solution)/shard_map/ppermute | solution.py:24
  15.8 0.0 copy-start.1
  15.8 2.1 %collective-permute-start.3 = (bf16[17,16,128]{2,1,0:T(8,128)(2,1)S(1)}, bf16[17,16,128]{2,1,0:T(8,128)(2,1)S(1)}, u32[]{:S(2)}, u32[]{:S(2)}) collective-permute-start(bf16[17,16,128]{2,1,0:T(8,128)(2,1)S(1)} %get-tuple-element.15), channel_id=1, source_target_pairs={{1,0},{2,1},{3,2},{4,3},{5,4},{6,5},{7,6},{8,7},{9,8},{10,9},{11,1... | collective-permute-start | bytes 208904 | tf_op jit(solution)/shard_map/ppermute | solution.py:24
  17.9 0.0 copy-done.2
  17.9 0.0 copy-done.5
  17.9 0.0 copy-done.6
  17.9 0.0 copy-done.7
  17.9 0.3 local.1
  18.3 0.0 collective-permute-done.2.b_lo
  18.3 3.3 %collective-permute-done.3.b_hi = bf16[17,16,128]{2,1,0:T(8,128)(2,1)S(1)} collective-permute-done((bf16[17,16,128]{2,1,0:T(8,128)(2,1)S(1)}, bf16[17,16,128]{2,1,0:T(8,128)(2,1)S(1)}, u32[]{:S(2)}, u32[]{:S(2)}) %collective-permute-start.3) | collective-permute-done | bytes 69664 | tf_op jit(solution)/shard_map/ppermute | solution.py:24
  21.6 0.0 collective-permute-done.a_lo
  21.6 0.0 collective-permute-done.1.a_hi
  21.6 1.0 %message.1.after = bf16[16,24,128]{2,1,0:T(8,128)(2,1)} custom-call(f32[256,128]{1,0:T(8,128)S(1)} %get-tuple-element.16.base, bf16[256,256]{1,0:T(8,128)(2,1)S(1)} %get-tuple-element.17.pick, f32[16,128]{1,0:T(8,128)S(1)} %get-tuple-element.18.ids, bf16[7,128,128]{2,1,0:T(8,128)(2,1)S(1)} %copy-done.2, bf16[18,16,128]{2,1,0:T(8,128)(2,1)S(1)} %collective-permute-done.a_lo, ...), custom_call_target="tpu_custom_call" | custom-call | flops 16777216 | bytes 1048576 | tf_op jit(solution)/shard_map/message/pallas_call | solution.py:238
  22.6 0.0 copy-start.4
  22.6 7.3 %all-to-all-start = ((bf16[16,24,128]{2,1,0:T(8,128)(2,1)}), bf16[16,24,128]{2,1,0:T(8,128)(2,1)S(1)}, u32[]{:S(2)}, u32[]{:S(2)}) async-start(bf16[16,24,128]{2,1,0:T(8,128)(2,1)} %message.1.after), calls=%async_computation | async-start | bytes 196608 | tf_op jit(solution)/shard_map/all_to_all | solution.py:252
  29.9 0.0 copy-done.1
  29.9 0.0 copy-done.4
  29.9 2.9 %update.1 = (bf16[16,16,16,128]{3,2,1,0:T(8,128)(2,1)}, f32[8,16,128]{2,1,0:T(8,128)S(1)}, f32[8,16,128]{2,1,0:T(8,128)S(1)}) custom-call(bf16[16,16,16,128]{3,2,1,0:T(8,128)(2,1)S(1)} %copy-done.1, bf16[7,128,128]{2,1,0:T(8,128)(2,1)S(1)} %copy-done.2, f32[8,16,128]{2,1,0:T(8,128)S(1)} %copy-done.4, bf16[18,16,128]{2,1,0:T(8,128)(2,1)S(1)} %collective-permute-done.a_lo, ...), custom_call_target="tpu_custom_call" | custom-call | flops 939524096 | bytes 4194304 | tf_op jit(solution)/shard_map/update/pallas_call | solution.py:254
  32.8 5.6 %all-to-all-done.got = bf16[16,24,128]{2,1,0:T(8,128)(2,1)S(1)} async-done(((bf16[16,24,128]{2,1,0:T(8,128)(2,1)}), bf16[16,24,128]{2,1,0:T(8,128)(2,1)S(1)}, u32[]{:S(2)}, u32[]{:S(2)}) %all-to-all-start) | async-done | bytes 98336 | tf_op jit(solution)/shard_map/all_to_all | solution.py:252
  38.4 0.8 %gradient.1 = f32[8,16,128]{2,1,0:T(8,128)} custom-call(bf16[16,24,128]{2,1,0:T(8,128)(2,1)S(1)} %all-to-all-done.got, f32[8,16,128]{2,1,0:T(8,128)S(1)} %get-tuple-element.20.prior, f32[8,16,128]{2,1,0:T(8,128)S(1)} %get-tuple-element.21.scale), custom_call_target="tpu_custom_call" | custom-call | flops 8388608 | bytes 524288 | tf_op jit(solution)/shard_map/gradient/pallas_call | solution.py:274
Async XLA Ops:
  0.6 1.2 %copy-start = (bf16[16,16,16,128]{3,2,1,0:T(8,128)(2,1)S(1)}, bf16[16,16,16,128]{3,2,1,0:T(8,128)(2,1)}, u32[]{:S(2)}) copy-start(bf16[16,16,16,128]{3,2,1,0:T(8,128)(2,1)} %adj.5) | copy-start | bytes 3145732
  1.9 0.8 %copy-start.3 = (f32[8,16,128]{2,1,0:T(8,128)S(1)}, f32[8,16,128]{2,1,0:T(8,128)}, u32[]{:S(2)}) copy-start(f32[8,16,128]{2,1,0:T(8,128)} %logf.3) | copy-start | bytes 196612
  2.7 15.2 %copy-start.2 = (bf16[7,128,128]{2,1,0:T(8,128)(2,1)S(1)}, bf16[7,128,128]{2,1,0:T(8,128)(2,1)}, u32[]{:S(2)}) copy-start(bf16[7,128,128]{2,1,0:T(8,128)(2,1)} %coupling.5) | copy-start | bytes 688132
  2.7 15.2 %copy-start.5 = (s32[1,1,16,16]{3,2,1,0:T(8,128)S(1)}, s32[1,1,16,16]{3,2,1,0:T(8,128)}, u32[]{:S(2)}) copy-start(s32[1,1,16,16]{3,2,1,0:T(8,128)} %nodes.1) | copy-start | bytes 3076
  2.9 18.7 %collective-permute-start = (bf16[18,16,128]{2,1,0:T(8,128)(2,1)S(1)}, bf16[18,16,128]{2,1,0:T(8,128)(2,1)S(1)}, u32[]{:S(2)}, u32[]{:S(2)}) collective-permute-start(bf16[18,16,128]{2,1,0:T(8,128)(2,1)S(1)} %get-tuple-element.12), channel_id=1, source_target_pairs={{0,16},{16,32},{32,48},{48,64},{64,80},{80,96},{96,112},{112,128},... | collective-permute-start | bytes 221192 | tf_op jit(solution)/shard_map/ppermute | solution.py:24
  6.3 15.3 %collective-permute-start.1 = (bf16[18,16,128]{2,1,0:T(8,128)(2,1)S(1)}, bf16[18,16,128]{2,1,0:T(8,128)(2,1)S(1)}, u32[]{:S(2)}, u32[]{:S(2)}) collective-permute-start(bf16[18,16,128]{2,1,0:T(8,128)(2,1)S(1)} %get-tuple-element.13), channel_id=1, source_target_pairs={{16,0},{32,16},{48,32},{64,48},{80,64},{96,80},{112,96},{128,112},... | collective-permute-start | bytes 221192 | tf_op jit(solution)/shard_map/ppermute | solution.py:24
  11.6 6.4 %copy-start.6 = (s32[1,1,256]{2,1,0:T(1,128)S(1)}, s32[1,1,256]{2,1,0:T(1,128)}, u32[]{:S(2)}) copy-start(s32[1,1,256]{2,1,0:T(1,128)} %send.1) | copy-start | bytes 3076
  11.6 6.4 %copy-start.7 = (s32[1,1,16]{2,1,0:T(1,128)S(1)}, s32[1,1,16]{2,1,0:T(1,128)}, u32[]{:S(2)}) copy-start(s32[1,1,16]{2,1,0:T(1,128)} %live.1) | copy-start | bytes 196
  11.6 6.7 %collective-permute-start.2 = (bf16[17,16,128]{2,1,0:T(8,128)(2,1)S(1)}, bf16[17,16,128]{2,1,0:T(8,128)(2,1)S(1)}, u32[]{:S(2)}, u32[]{:S(2)}) collective-permute-start(bf16[17,16,128]{2,1,0:T(8,128)(2,1)S(1)} %get-tuple-element.14), channel_id=1, source_target_pairs={{0,1},{1,2},{2,3},{3,4},{4,5},{5,6},{6,7},{7,8},{8,9},{9,10},{10,1... | collective-permute-start | bytes 208904 | tf_op jit(solution)/shard_map/ppermute | solution.py:24
  15.8 14.1 %copy-start.1 = (bf16[16,16,16,128]{3,2,1,0:T(8,128)(2,1)S(1)}, bf16[16,16,16,128]{3,2,1,0:T(8,128)(2,1)}, u32[]{:S(2)}) copy-start(bf16[16,16,16,128]{3,2,1,0:T(8,128)(2,1)} %adj.5) | copy-start | bytes 3145732
  15.8 5.8 %collective-permute-start.3 = (bf16[17,16,128]{2,1,0:T(8,128)(2,1)S(1)}, bf16[17,16,128]{2,1,0:T(8,128)(2,1)S(1)}, u32[]{:S(2)}, u32[]{:S(2)}) collective-permute-start(bf16[17,16,128]{2,1,0:T(8,128)(2,1)S(1)} %get-tuple-element.15), channel_id=1, source_target_pairs={{1,0},{2,1},{3,2},{4,3},{5,4},{6,5},{7,6},{8,7},{9,8},{10,9},{11,1... | collective-permute-start | bytes 208904 | tf_op jit(solution)/shard_map/ppermute | solution.py:24
  22.6 7.3 %copy-start.4 = (f32[8,16,128]{2,1,0:T(8,128)S(1)}, f32[8,16,128]{2,1,0:T(8,128)}, u32[]{:S(2)}) copy-start(f32[8,16,128]{2,1,0:T(8,128)} %logf.3) | copy-start | bytes 196612
  22.6 15.8 %all-to-all-start = ((bf16[16,24,128]{2,1,0:T(8,128)(2,1)}), bf16[16,24,128]{2,1,0:T(8,128)(2,1)S(1)}, u32[]{:S(2)}, u32[]{:S(2)}) async-start(bf16[16,24,128]{2,1,0:T(8,128)(2,1)} %message.1.after), calls=%async_computation | async-start | bytes 196608 | tf_op jit(solution)/shard_map/all_to_all | solution.py:252

commit v2 on v1

--- a/solution.py
+++ b/solution.py
@@ -11,11 +11,16 @@
 BF16 = jnp.bfloat16
 VMEM = pl.BlockSpec(memory_space=pltpu.VMEM)
 ANY = pl.BlockSpec(memory_space=pl.ANY)
+HBM = pl.BlockSpec(memory_space=pltpu.HBM)
 MSG = 24
 
 
 def dot(a, b):
     return jnp.dot(a, b, preferred_element_type=F32)
+
+
+def in_hbm(array):
+    return pltpu.with_memory_space_constraint(array, pltpu.HBM)
 
 
 def shift(block, axis, step):
@@ -24,7 +29,7 @@
     return lax.ppermute(block, axis, pairs)
 
 
-def pack_body(adj, logf, to_a_hi, to_a_lo, to_b_hi, to_b_lo, sems):
+def pack_body(adj, logf_hbm, coupling, to_a_hi, to_a_lo, to_b_hi, to_b_lo, blocks, logf, sems):
     ca, cb = adj.shape[0], adj.shape[1]
     pa, pb = logf.shape[0], logf.shape[1]
     copies = [
@@ -32,9 +37,13 @@
         pltpu.make_async_copy(adj.at[0], to_a_lo.at[pl.ds(0, cb)], sems.at[1]),
         pltpu.make_async_copy(adj.at[:, cb - 1], to_b_hi.at[pl.ds(0, ca)], sems.at[2]),
         pltpu.make_async_copy(adj.at[:, 0], to_b_lo.at[pl.ds(0, ca)], sems.at[3]),
+        pltpu.make_async_copy(coupling, blocks, sems.at[4]),
     ]
+    fields = pltpu.make_async_copy(logf_hbm, logf, sems.at[5])
+    fields.start()
     for copy in copies:
         copy.start()
+    fields.wait()
     to_a_hi[cb:cb + 2] = logf[pa - 2:pa].astype(BF16)
     to_a_lo[cb:cb + 2] = logf[0:2].astype(BF16)
     to_b_hi[ca] = jnp.concatenate([logf[:, pb - 2, :], logf[:, pb - 1, :]], axis=0).astype(BF16)
@@ -112,9 +121,8 @@
         out[o, slots:MSG] = jnp.where(o > here, extra(o, pb - 1), extra(o, 0)).astype(BF16)
 
 
-def update_body(adj, coupling, logf, a_lo, a_hi, b_lo, b_hi, after, out, prior, scale,
+def update_body(adj, coupling, logf, a_lo, a_hi, b_lo, b_hi, out, prior, scale,
                 held, field, once, sems):
-    del after
     ca, cb, nl, width = adj.shape
     rows = cb * nl
     layer = lax.broadcasted_iota(jnp.int32, (rows, width), 0) % nl
@@ -201,20 +209,21 @@
     shape = jax.ShapeDtypeStruct
     wire = pltpu.CompilerParams(vmem_limit_bytes=16 * 2**20)
 
-    to_a_hi, to_a_lo, to_b_hi, to_b_lo = pl.pallas_call(
+    to_a_hi, to_a_lo, to_b_hi, to_b_lo, blocks = pl.pallas_call(
         pack_body,
         out_shape=(
             shape((cb + 2, nl, width), BF16),
             shape((cb + 2, nl, width), BF16),
             shape((ca + 1, nl, width), BF16),
             shape((ca + 1, nl, width), BF16),
+            shape(coupling.shape, BF16),
         ),
-        in_specs=[ANY, VMEM],
-        out_specs=(VMEM,) * 4,
-        scratch_shapes=[pltpu.SemaphoreType.DMA((4,))],
+        in_specs=[HBM] * 3,
+        out_specs=(VMEM,) * 5,
+        scratch_shapes=[pltpu.VMEM(log_friction.shape, F32), pltpu.SemaphoreType.DMA((6,))],
         compiler_params=wire,
         name="pack",
-    )(adjoint_trace, log_friction)
+    )(in_hbm(adjoint_trace), in_hbm(log_friction), in_hbm(coupling))
     a_lo = shift(to_a_hi, "gx", 1)
     a_hi = shift(to_a_lo, "gx", -1)
     b_lo = shift(to_b_hi, "gy", 1)
@@ -233,7 +242,7 @@
         compiler_params=wire,
         cost_estimate=cost(2 * 6 * faces * width * width, 2 * 2**20),
         name="local",
-    )(adjoint_trace, coupling, send_column, live_count, target_node)
+    )(adjoint_trace, blocks, send_column, live_count, target_node)
 
     message = pl.pallas_call(
         message_body,
@@ -247,7 +256,7 @@
         compiler_params=wire,
         cost_estimate=cost(2 * faces * faces * width, 2**20),
         name="message",
-    )(base, pick, ids, coupling, a_lo, a_hi, b_lo, b_hi)
+    )(base, pick, ids, blocks, a_lo, a_hi, b_lo, b_hi)
 
     received = lax.all_to_all(message, "gy", split_axis=0, concat_axis=0, tiled=True)
 
@@ -258,8 +267,8 @@
             shape(log_friction.shape, F32),
             shape(log_friction.shape, F32),
         ),
-        in_specs=[VMEM] * 7 + [ANY],
-        out_specs=(ANY, VMEM, VMEM),
+        in_specs=[VMEM] * 7,
+        out_specs=(HBM, VMEM, VMEM),
         scratch_shapes=[
             pltpu.VMEM(adjoint_trace.shape, BF16),
             pltpu.VMEM((pa + 4, pb + 16, width), F32),
@@ -269,7 +278,7 @@
         compiler_params=wire,
         cost_estimate=cost(2 * 7 * faces * nl * width * width, 4 * 2**20),
         name="update",
-    )(adjoint_trace, coupling, log_friction, a_lo, a_hi, b_lo, b_hi, message)
+    )(adjoint_trace, blocks, log_friction, a_lo, a_hi, b_lo, b_hi)
 
     gradient = pl.pallas_call(
         gradient_body,

time: 39.6 us -> 38.3 us (0.967)
  local copies, waits for them, and re-layouts: 2.09 us -> 0.02 us
  Pallas kernels: 5.23 us -> 6.23 us
    unnamed x16 -> x10, local copies, waits for them, and re-layouts: 2.09 us -> 0.02 us
    pallas_call x1, Pallas kernels: 0.23 us -> 1.24 us  [per_device(): pl.pallas_call(pack_body, out_shape=(shape((cb + 2, nl, width), BF16), sh...]
where the time goes in v2:
time: 38.3 us; the launch traced here: 38 us
  starting transfers between devices  22.1 us (58%)
  waiting for transfers between devices  8.9 us (23%)
  Pallas kernels  6.23 us (16%)
  between operations  0.76 us (2%)
    ppermute x4, starting transfers between devices, shift(): return lax.ppermute(block, axis, pairs)  14.8 us
    all_to_all x1, starting transfers between devices, per_device(): lax.all_to_all(message, 'gy', split_axis=0, concat_axis=0, tiled=True)  7.3 us
    all_to_all x1, waiting for transfers between devices, per_device(): lax.all_to_all(message, 'gy', split_axis=0, concat_axis=0, tiled=True)  5.59 us
    ppermute x4, waiting for transfers between devices, shift(): return lax.ppermute(block, axis, pairs)  3.31 us
    pallas_call x1, Pallas kernels, per_device(): pl.pallas_call(update_body, out_shape=(shape(adjoint_trace.shape, BF16),...  2.89 us
    pallas_call x1, Pallas kernels, per_device(): pl.pallas_call(pack_body, out_shape=(shape((cb + 2, nl, width), BF16), sh...  1.24 us
    pallas_call x1, Pallas kernels, per_device(): pl.pallas_call(message_body, out_shape=shape((owners, MSG, width), BF16),...  0.97 us
    pallas_call x1, Pallas kernels, per_device(): pl.pallas_call(gradient_body, out_shape=shape(log_friction.shape, F32), i...  0.8 us
  transfers between devices with their start and end apart: 5, of which 2 were waited for; matrix products, arithmetic and copies ran while one was open for 0% of the time, Pallas kernels for 8%

profile of v2, /device:TPU:513, one launch (start us, length us, event | category | flops | bytes accessed | tf_op | source)
XLA Modules:
  0.0 38.0 jit_solution(11033702037788481127)
XLA Ops:
  0.6 0.0 copy-start
  0.6 0.0 copy-start.4
  0.6 1.2 %pack.1 = (bf16[18,16,128]{2,1,0:T(8,128)(2,1)S(1)}, bf16[18,16,128]{2,1,0:T(8,128)(2,1)S(1)}, bf16[17,16,128]{2,1,0:T(8,128)(2,1)S(1)}, bf16[17,16,128]{2,1,0:T(8,128)(2,1)S(1)}, bf16[7,128,128]{2,1,0:T(8,128)(2,1)S(1)}) custom-call(bf16[16,16,16,128]{3,2,1,0:T(8,128)(2,1)} %adj.5, f32[8,16,128]{2,1,0:T(8,128)} %logf.1, bf16[7,128,128]{2,1,0:T(8,128)(2,1)} %coupling.1), custom_call_target="tpu_custom_call" | custom-call | tf_op jit(solution)/shard_map/pack/pallas_call | solution.py:212
  1.9 0.0 copy-start.2
  1.9 3.3 %collective-permute-start = (bf16[18,16,128]{2,1,0:T(8,128)(2,1)S(1)}, bf16[18,16,128]{2,1,0:T(8,128)(2,1)S(1)}, u32[]{:S(2)}, u32[]{:S(2)}) collective-permute-start(bf16[18,16,128]{2,1,0:T(8,128)(2,1)S(1)} %get-tuple-element.14), channel_id=1, source_target_pairs={{0,16},{16,32},{32,48},{48,64},{64,80},{80,96},{96,112},{112,128},... | collective-permute-start | bytes 221192 | tf_op jit(solution)/shard_map/ppermute | solution.py:29
  5.2 5.3 %collective-permute-start.1 = (bf16[18,16,128]{2,1,0:T(8,128)(2,1)S(1)}, bf16[18,16,128]{2,1,0:T(8,128)(2,1)S(1)}, u32[]{:S(2)}, u32[]{:S(2)}) collective-permute-start(bf16[18,16,128]{2,1,0:T(8,128)(2,1)S(1)} %get-tuple-element.15), channel_id=1, source_target_pairs={{16,0},{32,16},{48,32},{64,48},{80,64},{96,80},{112,96},{128,112},... | collective-permute-start | bytes 221192 | tf_op jit(solution)/shard_map/ppermute | solution.py:29
  10.5 4.2 %collective-permute-start.2 = (bf16[17,16,128]{2,1,0:T(8,128)(2,1)S(1)}, bf16[17,16,128]{2,1,0:T(8,128)(2,1)S(1)}, u32[]{:S(2)}, u32[]{:S(2)}) collective-permute-start(bf16[17,16,128]{2,1,0:T(8,128)(2,1)S(1)} %get-tuple-element.16), channel_id=1, source_target_pairs={{0,1},{1,2},{2,3},{3,4},{4,5},{5,6},{6,7},{7,8},{8,9},{9,10},{10,1... | collective-permute-start | bytes 208904 | tf_op jit(solution)/shard_map/ppermute | solution.py:29
  14.8 0.0 copy-start.3
  14.8 1.9 %collective-permute-start.3 = (bf16[17,16,128]{2,1,0:T(8,128)(2,1)S(1)}, bf16[17,16,128]{2,1,0:T(8,128)(2,1)S(1)}, u32[]{:S(2)}, u32[]{:S(2)}) collective-permute-start(bf16[17,16,128]{2,1,0:T(8,128)(2,1)S(1)} %get-tuple-element.17), channel_id=1, source_target_pairs={{1,0},{2,1},{3,2},{4,3},{5,4},{6,5},{7,6},{8,7},{9,8},{10,9},{11,1... | collective-permute-start | bytes 208904 | tf_op jit(solution)/shard_map/ppermute | solution.py:29
  16.7 0.0 copy-done
  16.7 0.0 copy-done.4
  16.7 0.0 copy-done.2
  16.7 0.0 copy-done.3
  16.8 0.3 local.1
  17.1 0.0 collective-permute-done.2.b_lo
  17.1 3.3 %collective-permute-done.3.b_hi = bf16[17,16,128]{2,1,0:T(8,128)(2,1)S(1)} collective-permute-done((bf16[17,16,128]{2,1,0:T(8,128)(2,1)S(1)}, bf16[17,16,128]{2,1,0:T(8,128)(2,1)S(1)}, u32[]{:S(2)}, u32[]{:S(2)}) %collective-permute-start.3) | collective-permute-done | bytes 69664 | tf_op jit(solution)/shard_map/ppermute | solution.py:29
  20.4 0.0 collective-permute-done.a_lo
  20.4 0.0 collective-permute-done.1.a_hi
  20.4 1.0 %message.1 = bf16[16,24,128]{2,1,0:T(8,128)(2,1)} custom-call(f32[256,128]{1,0:T(8,128)S(1)} %get-tuple-element.19.base, bf16[256,256]{1,0:T(8,128)(2,1)S(1)} %get-tuple-element.20.pick, f32[16,128]{1,0:T(8,128)S(1)} %get-tuple-element.21.ids, bf16[7,128,128]{2,1,0:T(8,128)(2,1)S(1)} %get-tuple-element.13.coupling, ...), custom_call_target="tpu_custom_call" | custom-call | flops 16777216 | bytes 1048576 | tf_op jit(solution)/shard_map/message/pallas_call | solution.py:247
  21.4 0.0 copy-start.1
  21.4 7.3 %all-to-all-start = ((bf16[16,24,128]{2,1,0:T(8,128)(2,1)}), bf16[16,24,128]{2,1,0:T(8,128)(2,1)S(1)}, u32[]{:S(2)}, u32[]{:S(2)}) async-start(bf16[16,24,128]{2,1,0:T(8,128)(2,1)} %message.1), calls=%async_computation | async-start | bytes 196608 | tf_op jit(solution)/shard_map/all_to_all | solution.py:261
  28.7 0.0 copy-done.1
  28.7 2.9 %update.1 = (bf16[16,16,16,128]{3,2,1,0:T(8,128)(2,1)}, f32[8,16,128]{2,1,0:T(8,128)S(1)}, f32[8,16,128]{2,1,0:T(8,128)S(1)}) custom-call(bf16[16,16,16,128]{3,2,1,0:T(8,128)(2,1)S(1)} %copy-done, bf16[7,128,128]{2,1,0:T(8,128)(2,1)S(1)} %get-tuple-element.13.coupling, f32[8,16,128]{2,1,0:T(8,128)S(1)} %copy-done.1, ...), custom_call_target="tpu_custom_call" | custom-call | flops 939524096 | bytes 4194304 | tf_op jit(solution)/shard_map/update/pallas_call | solution.py:263
  31.6 5.6 %all-to-all-done.got = bf16[16,24,128]{2,1,0:T(8,128)(2,1)S(1)} async-done(((bf16[16,24,128]{2,1,0:T(8,128)(2,1)}), bf16[16,24,128]{2,1,0:T(8,128)(2,1)S(1)}, u32[]{:S(2)}, u32[]{:S(2)}) %all-to-all-start) | async-done | bytes 98336 | tf_op jit(solution)/shard_map/all_to_all | solution.py:261
  37.2 0.8 %gradient.1 = f32[8,16,128]{2,1,0:T(8,128)} custom-call(bf16[16,24,128]{2,1,0:T(8,128)(2,1)S(1)} %all-to-all-done.got, f32[8,16,128]{2,1,0:T(8,128)S(1)} %get-tuple-element.22.prior, f32[8,16,128]{2,1,0:T(8,128)S(1)} %get-tuple-element.23.scale), custom_call_target="tpu_custom_call" | custom-call | flops 8388608 | bytes 524288 | tf_op jit(solution)/shard_map/gradient/pallas_call | solution.py:283
Async XLA Ops:
  0.6 16.1 %copy-start = (bf16[16,16,16,128]{3,2,1,0:T(8,128)(2,1)S(1)}, bf16[16,16,16,128]{3,2,1,0:T(8,128)(2,1)}, u32[]{:S(2)}) copy-start(bf16[16,16,16,128]{3,2,1,0:T(8,128)(2,1)} %adj.5) | copy-start | bytes 3145732
  0.6 16.1 %copy-start.4 = (s32[1,1,16]{2,1,0:T(1,128)S(1)}, s32[1,1,16]{2,1,0:T(1,128)}, u32[]{:S(2)}) copy-start(s32[1,1,16]{2,1,0:T(1,128)} %live.1) | copy-start | bytes 196
  1.9 14.8 %copy-start.2 = (s32[1,1,16,16]{3,2,1,0:T(8,128)S(1)}, s32[1,1,16,16]{3,2,1,0:T(8,128)}, u32[]{:S(2)}) copy-start(s32[1,1,16,16]{3,2,1,0:T(8,128)} %nodes.1) | copy-start | bytes 3076
  1.9 18.5 %collective-permute-start = (bf16[18,16,128]{2,1,0:T(8,128)(2,1)S(1)}, bf16[18,16,128]{2,1,0:T(8,128)(2,1)S(1)}, u32[]{:S(2)}, u32[]{:S(2)}) collective-permute-start(bf16[18,16,128]{2,1,0:T(8,128)(2,1)S(1)} %get-tuple-element.14), channel_id=1, source_target_pairs={{0,16},{16,32},{32,48},{48,64},{64,80},{80,96},{96,112},{112,128},... | collective-permute-start | bytes 221192 | tf_op jit(solution)/shard_map/ppermute | solution.py:29
  5.2 15.2 %collective-permute-start.1 = (bf16[18,16,128]{2,1,0:T(8,128)(2,1)S(1)}, bf16[18,16,128]{2,1,0:T(8,128)(2,1)S(1)}, u32[]{:S(2)}, u32[]{:S(2)}) collective-permute-start(bf16[18,16,128]{2,1,0:T(8,128)(2,1)S(1)} %get-tuple-element.15), channel_id=1, source_target_pairs={{16,0},{32,16},{48,32},{64,48},{80,64},{96,80},{112,96},{128,112},... | collective-permute-start | bytes 221192 | tf_op jit(solution)/shard_map/ppermute | solution.py:29
  10.5 6.6 %collective-permute-start.2 = (bf16[17,16,128]{2,1,0:T(8,128)(2,1)S(1)}, bf16[17,16,128]{2,1,0:T(8,128)(2,1)S(1)}, u32[]{:S(2)}, u32[]{:S(2)}) collective-permute-start(bf16[17,16,128]{2,1,0:T(8,128)(2,1)S(1)} %get-tuple-element.16), channel_id=1, source_target_pairs={{0,1},{1,2},{2,3},{3,4},{4,5},{5,6},{6,7},{7,8},{8,9},{9,10},{10,1... | collective-permute-start | bytes 208904 | tf_op jit(solution)/shard_map/ppermute | solution.py:29
  14.8 2.0 %copy-start.3 = (s32[1,1,256]{2,1,0:T(1,128)S(1)}, s32[1,1,256]{2,1,0:T(1,128)}, u32[]{:S(2)}) copy-start(s32[1,1,256]{2,1,0:T(1,128)} %send.1) | copy-start | bytes 3076
  14.8 5.6 %collective-permute-start.3 = (bf16[17,16,128]{2,1,0:T(8,128)(2,1)S(1)}, bf16[17,16,128]{2,1,0:T(8,128)(2,1)S(1)}, u32[]{:S(2)}, u32[]{:S(2)}) collective-permute-start(bf16[17,16,128]{2,1,0:T(8,128)(2,1)S(1)} %get-tuple-element.17), channel_id=1, source_target_pairs={{1,0},{2,1},{3,2},{4,3},{5,4},{6,5},{7,6},{8,7},{9,8},{10,9},{11,1... | collective-permute-start | bytes 208904 | tf_op jit(solution)/shard_map/ppermute | solution.py:29
  21.4 7.3 %copy-start.1 = (f32[8,16,128]{2,1,0:T(8,128)S(1)}, f32[8,16,128]{2,1,0:T(8,128)}, u32[]{:S(2)}) copy-start(f32[8,16,128]{2,1,0:T(8,128)} %logf.1) | copy-start | bytes 196612
  21.4 15.8 %all-to-all-start = ((bf16[16,24,128]{2,1,0:T(8,128)(2,1)}), bf16[16,24,128]{2,1,0:T(8,128)(2,1)S(1)}, u32[]{:S(2)}, u32[]{:S(2)}) async-start(bf16[16,24,128]{2,1,0:T(8,128)(2,1)} %message.1), calls=%async_computation | async-start | bytes 196608 | tf_op jit(solution)/shard_map/all_to_all | solution.py:261

commit v3 on v2

--- a/solution.py
+++ b/solution.py
@@ -1,5 +1,3 @@
-import functools
-
 import jax
 import jax.numpy as jnp
 from jax import lax
@@ -10,7 +8,6 @@
 F32 = jnp.float32
 BF16 = jnp.bfloat16
 VMEM = pl.BlockSpec(memory_space=pltpu.VMEM)
-ANY = pl.BlockSpec(memory_space=pl.ANY)
 HBM = pl.BlockSpec(memory_space=pltpu.HBM)
 MSG = 24
 
@@ -29,30 +26,66 @@
     return lax.ppermute(block, axis, pairs)
 
 
-def pack_body(adj, logf_hbm, coupling, to_a_hi, to_a_lo, to_b_hi, to_b_lo, blocks, logf, sems):
-    ca, cb = adj.shape[0], adj.shape[1]
-    pa, pb = logf.shape[0], logf.shape[1]
-    copies = [
-        pltpu.make_async_copy(adj.at[ca - 1], to_a_hi.at[pl.ds(0, cb)], sems.at[0]),
-        pltpu.make_async_copy(adj.at[0], to_a_lo.at[pl.ds(0, cb)], sems.at[1]),
-        pltpu.make_async_copy(adj.at[:, cb - 1], to_b_hi.at[pl.ds(0, ca)], sems.at[2]),
-        pltpu.make_async_copy(adj.at[:, 0], to_b_lo.at[pl.ds(0, ca)], sems.at[3]),
-        pltpu.make_async_copy(coupling, blocks, sems.at[4]),
+def swap(block, first):
+    count = lax.axis_size("gx")
+    pairs = [(i, i + 1) for i in range(first, count - 1, 2)]
+    return lax.ppermute(block, "gx", pairs + [(j, i) for i, j in pairs])
+
+
+def pack_body(adj_hbm, logf_hbm, coupling_hbm, send_hbm, live_hbm, nodes_hbm,
+              to_first, to_second, to_b_hi, to_b_lo, coupling, pick, ids,
+              logf, send, live, nodes, sems):
+    ca, cb = adj_hbm.shape[0], adj_hbm.shape[1]
+    pa, pb, width = logf.shape
+    odd = lax.axis_index("gx") % 2
+    column = (ca - 1) * (1 - odd)
+    row = (pa - 2) * (1 - odd)
+    small = [
+        pltpu.make_async_copy(source, target, sems.at[k])
+        for k, (source, target) in enumerate(
+            ((logf_hbm, logf), (send_hbm, send), (live_hbm, live), (nodes_hbm, nodes))
+        )
     ]
-    fields = pltpu.make_async_copy(logf_hbm, logf, sems.at[5])
-    fields.start()
-    for copy in copies:
+    large = [
+        pltpu.make_async_copy(source, target, sems.at[4 + k])
+        for k, (source, target) in enumerate(
+            (
+                (adj_hbm.at[column], to_first.at[pl.ds(0, cb)]),
+                (adj_hbm.at[ca - 1 - column], to_second.at[pl.ds(0, cb)]),
+                (adj_hbm.at[:, cb - 1], to_b_hi.at[pl.ds(0, ca)]),
+                (adj_hbm.at[:, 0], to_b_lo.at[pl.ds(0, ca)]),
+                (coupling_hbm, coupling),
+            )
+        )
+    ]
+    for copy in small + large:
         copy.start()
-    fields.wait()
-    to_a_hi[cb:cb + 2] = logf[pa - 2:pa].astype(BF16)
-    to_a_lo[cb:cb + 2] = logf[0:2].astype(BF16)
+    for copy in small:
+        copy.wait()
+    to_first[cb:cb + 2] = logf[pl.ds(row, 2)].astype(BF16)
+    to_second[cb:cb + 2] = logf[pl.ds(pa - 2 - row, 2)].astype(BF16)
     to_b_hi[ca] = jnp.concatenate([logf[:, pb - 2, :], logf[:, pb - 1, :]], axis=0).astype(BF16)
     to_b_lo[ca] = jnp.concatenate([logf[:, 0, :], logf[:, 1, :]], axis=0).astype(BF16)
-    for copy in copies:
+    faces = pick.shape[0]
+    face = lax.broadcasted_iota(jnp.int32, (faces, faces), 0)
+    pick[...] = jnp.where(send[0] == face, 1.0, 0.0).T.astype(BF16)
+    owners, slots = nodes.shape[2], nodes.shape[3]
+    sub = lax.broadcasted_iota(jnp.int32, (slots, width), 0)
+    lane = lax.broadcasted_iota(jnp.int32, (slots, width), 1)
+    spread = jnp.where(lane % slots == sub, 1.0, 0.0).astype(BF16)
+    listed = dot(nodes[0, 0].astype(F32).astype(BF16), spread) + 1.0
+    owner = lax.broadcasted_iota(jnp.int32, (owners, owners), 0)
+    other = lax.broadcasted_iota(jnp.int32, (owners, owners), 1)
+    counts = jnp.sum(jnp.where(owner == other, live[0].astype(F32), 0.0), axis=1, keepdims=True)
+    lane = lax.broadcasted_iota(jnp.int32, (owners, width), 1)
+    mine = lane // slots == lax.axis_index("gy") % (width // slots)
+    alive = (lane % slots).astype(F32) < counts
+    ids[...] = jnp.where(jnp.logical_and(mine, alive), listed, 0.0)
+    for copy in large:
         copy.wait()
 
 
-def local_body(adj, coupling, send, live, nodes, base, pick, ids, wide):
+def local_body(adj, coupling, base, wide):
     ca, cb, nl, width = adj.shape
     faces = ca * cb
     for a in range(ca):
@@ -68,36 +101,27 @@
     after = pltpu.roll(dot(low, coupling[6]), faces - 1, 0)
     total = total + jnp.where(column > 0, before, 0.0) + jnp.where(column < cb - 1, after, 0.0)
     base[...] = total
-    face = lax.broadcasted_iota(jnp.int32, (faces, faces), 0)
-    picked_by = jnp.where(send[0] == face, 1.0, 0.0)
-    pick[...] = picked_by.T.astype(BF16)
-    owners, slots = nodes.shape[2], nodes.shape[3]
-    sub = lax.broadcasted_iota(jnp.int32, (slots, width), 0)
-    lane = lax.broadcasted_iota(jnp.int32, (slots, width), 1)
-    spread = jnp.where(lane % slots == sub, 1.0, 0.0).astype(BF16)
-    listed = dot(nodes[0, 0].astype(F32).astype(BF16), spread) + 1.0
-    owner = lax.broadcasted_iota(jnp.int32, (owners, owners), 0)
-    other = lax.broadcasted_iota(jnp.int32, (owners, owners), 1)
-    counts = jnp.sum(jnp.where(owner == other, live[0].astype(F32), 0.0), axis=1, keepdims=True)
-    lane = lax.broadcasted_iota(jnp.int32, (owners, width), 1)
-    mine = lane // slots == lax.axis_index("gy") % (width // slots)
-    alive = (lane % slots).astype(F32) < counts
-    ids[...] = jnp.where(jnp.logical_and(mine, alive), listed, 0.0)
-
-
-def message_body(base, pick, ids, coupling, a_lo, a_hi, b_lo, b_hi, out, total, wide):
+
+
+def message_body(base, pick, ids, coupling, first, second, b_lo, b_hi, out, total, wide):
     faces, width = base.shape
     owners, slots = out.shape[0], faces // out.shape[0]
-    cb = a_lo.shape[0] - 2
+    cb = first.shape[0] - 2
     ca = b_lo.shape[0] - 1
-    for k, halo in enumerate((a_lo, a_hi, b_lo, b_hi)):
+    odd = lax.axis_index("gx") % 2 == 1
+    for k, halo in enumerate((first, second, b_lo, b_hi)):
         rows = cb if k < 2 else ca
         wide[k * rows * 8:(k + 1) * rows * 8] = (
             halo[0:rows, 0:8, :].astype(F32).reshape(rows * 8, width)
         )
 
+    def row(k, rows):
+        return wide[pl.ds(k * rows * 8, rows, stride=8), :]
+
     def edge(k, rows):
-        return wide[pl.ds(k * rows * 8, rows, stride=8), :].astype(BF16)
+        if k < 2:
+            return jnp.where(odd, row(k, rows), row(1 - k, rows)).astype(BF16)
+        return row(k, rows).astype(BF16)
 
     total[...] = base[...]
     total[0:cb] += dot(edge(0, cb), coupling[3])
@@ -106,9 +130,9 @@
     total[pl.ds(cb - 1, ca, stride=cb), :] += dot(edge(3, ca), coupling[6])
     picked = dot(pick[...], total[...].astype(BF16)).astype(BF16)
     here = lax.axis_index("gy")
-    pb = a_lo.shape[1]
-    top = a_lo[cb + 1].astype(F32)
-    bottom = a_hi[cb].astype(F32)
+    pb = first.shape[1]
+    top = jnp.where(odd, first[cb + 1].astype(F32), second[cb + 1].astype(F32))
+    bottom = jnp.where(odd, second[cb].astype(F32), first[cb].astype(F32))
     sub = lax.broadcasted_iota(jnp.int32, (MSG - slots, width), 0)
 
     def extra(o, column):
@@ -121,11 +145,23 @@
         out[o, slots:MSG] = jnp.where(o > here, extra(o, pb - 1), extra(o, 0)).astype(BF16)
 
 
-def update_body(adj, coupling, logf, a_lo, a_hi, b_lo, b_hi, out, prior, scale,
-                held, field, once, sems):
+def update_body(adj, coupling, logf, first, second, b_lo, b_hi, out, prior, scale,
+                a_lo, a_hi, held, field, once, sems):
     ca, cb, nl, width = adj.shape
     rows = cb * nl
     layer = lax.broadcasted_iota(jnp.int32, (rows, width), 0) % nl
+    odd = lax.axis_index("gx") % 2 == 1
+
+    @pl.when(odd)
+    def _():
+        a_lo[...] = first[...]
+        a_hi[...] = second[...]
+
+    @pl.when(jnp.logical_not(odd))
+    def _():
+        a_lo[...] = second[...]
+        a_hi[...] = first[...]
+
     copies = []
     for a in range(ca):
         own = adj[a].reshape(rows, width)
@@ -209,7 +245,7 @@
     shape = jax.ShapeDtypeStruct
     wire = pltpu.CompilerParams(vmem_limit_bytes=16 * 2**20)
 
-    to_a_hi, to_a_lo, to_b_hi, to_b_lo, blocks = pl.pallas_call(
+    to_first, to_second, to_b_hi, to_b_lo, blocks, pick, ids = pl.pallas_call(
         pack_body,
         out_shape=(
             shape((cb + 2, nl, width), BF16),
@@ -217,32 +253,36 @@
             shape((ca + 1, nl, width), BF16),
             shape((ca + 1, nl, width), BF16),
             shape(coupling.shape, BF16),
-        ),
-        in_specs=[HBM] * 3,
-        out_specs=(VMEM,) * 5,
-        scratch_shapes=[pltpu.VMEM(log_friction.shape, F32), pltpu.SemaphoreType.DMA((6,))],
-        compiler_params=wire,
-        name="pack",
-    )(in_hbm(adjoint_trace), in_hbm(log_friction), in_hbm(coupling))
-    a_lo = shift(to_a_hi, "gx", 1)
-    a_hi = shift(to_a_lo, "gx", -1)
-    b_lo = shift(to_b_hi, "gy", 1)
-    b_hi = shift(to_b_lo, "gy", -1)
-
-    base, pick, ids = pl.pallas_call(
-        local_body,
-        out_shape=(
-            shape((faces, width), F32),
             shape((faces, faces), BF16),
             shape((owners, width), F32),
         ),
-        in_specs=[VMEM] * 5,
-        out_specs=(VMEM,) * 3,
+        in_specs=[HBM] * 6,
+        out_specs=(VMEM,) * 7,
+        scratch_shapes=[
+            pltpu.VMEM(log_friction.shape, F32),
+            pltpu.VMEM(send_column.shape, jnp.int32),
+            pltpu.VMEM(live_count.shape, jnp.int32),
+            pltpu.VMEM(target_node.shape, jnp.int32),
+            pltpu.SemaphoreType.DMA((9,)),
+        ],
+        compiler_params=wire,
+        name="pack",
+    )(*map(in_hbm, (adjoint_trace, log_friction, coupling, send_column, live_count, target_node)))
+    first = swap(to_first, 0)
+    second = swap(to_second, 1)
+    b_lo = shift(to_b_hi, "gy", 1)
+    b_hi = shift(to_b_lo, "gy", -1)
+
+    base = pl.pallas_call(
+        local_body,
+        out_shape=shape((faces, width), F32),
+        in_specs=[VMEM] * 2,
+        out_specs=VMEM,
         scratch_shapes=[pltpu.VMEM((faces * 8, width), F32)],
         compiler_params=wire,
         cost_estimate=cost(2 * 6 * faces * width * width, 2 * 2**20),
         name="local",
-    )(adjoint_trace, blocks, send_column, live_count, target_node)
+    )(adjoint_trace, blocks)
 
     message = pl.pallas_call(
         message_body,
@@ -256,7 +296,7 @@
         compiler_params=wire,
         cost_estimate=cost(2 * faces * faces * width, 2**20),
         name="message",
-    )(base, pick, ids, blocks, a_lo, a_hi, b_lo, b_hi)
+    )(base, pick, ids, blocks, first, second, b_lo, b_hi)
 
     received = lax.all_to_all(message, "gy", split_axis=0, concat_axis=0, tiled=True)
 
@@ -270,6 +310,8 @@
         in_specs=[VMEM] * 7,
         out_specs=(HBM, VMEM, VMEM),
         scratch_shapes=[
+            pltpu.VMEM((cb + 2, nl, width), BF16),
+            pltpu.VMEM((cb + 2, nl, width), BF16),
             pltpu.VMEM(adjoint_trace.shape, BF16),
             pltpu.VMEM((pa + 4, pb + 16, width), F32),
             pltpu.VMEM((pa + 2, pb + 16, width), F32),
@@ -278,7 +320,7 @@
         compiler_params=wire,
         cost_estimate=cost(2 * 7 * faces * nl * width * width, 4 * 2**20),
         name="update",
-    )(adjoint_trace, blocks, log_friction, a_lo, a_hi, b_lo, b_hi)
+    )(adjoint_trace, blocks, log_friction, first, second, b_lo, b_hi)
 
     gradient = pl.pallas_call(
         gradient_body,

time: 38.3 us -> 38.3 us (level)
  the two profiles are of different devices: /device:TPU:513 before, /device:TPU:33 now
where the time goes in v3:
time: 38.3 us; the launch traced here: 38 us
  starting transfers between devices  24.8 us (65%)
  Pallas kernels  6.34 us (17%)
  waiting for transfers between devices  6.13 us (16%)
  between operations  0.72 us (2%)
    ppermute x2, starting transfers between devices, shift(): return lax.ppermute(block, axis, pairs)  15.8 us
    all_to_all x1, waiting for transfers between devices, per_device(): lax.all_to_all(message, 'gy', split_axis=0, concat_axis=0, tiled=True)  5.59 us
    ppermute x2, starting transfers between devices, swap(): return lax.ppermute(block, 'gx', pairs + [(j, i) for i, j in pairs])  5.24 us
    all_to_all x1, starting transfers between devices, per_device(): lax.all_to_all(message, 'gy', split_axis=0, concat_axis=0, tiled=True)  3.78 us
    pallas_call x1, Pallas kernels, per_device(): pl.pallas_call(update_body, out_shape=(shape(adjoint_trace.shape, BF16),...  2.91 us
    pallas_call x1, Pallas kernels, per_device(): pl.pallas_call(pack_body, out_shape=(shape((cb + 2, nl, width), BF16), sh...  1.31 us
    pallas_call x1, Pallas kernels, per_device(): pl.pallas_call(message_body, out_shape=shape((owners, MSG, width), BF16),...  0.98 us
    pallas_call x1, Pallas kernels, per_device(): pl.pallas_call(gradient_body, out_shape=shape(log_friction.shape, F32), i...  0.8 us
  transfers between devices with their start and end apart: 5, of which 2 were waited for; matrix products, arithmetic and copies ran while one was open for 0% of the time, Pallas kernels for 9%

profile of v3, /device:TPU:33, one launch (start us, length us, event | category | flops | bytes accessed | tf_op | source)
XLA Modules:
  0.0 38.0 jit_solution(1217398854432056756)
XLA Ops:
  0.6 0.0 copy-start
  0.6 1.3 %pack.1 = (bf16[18,16,128]{2,1,0:T(8,128)(2,1)S(1)}, bf16[18,16,128]{2,1,0:T(8,128)(2,1)S(1)}, bf16[17,16,128]{2,1,0:T(8,128)(2,1)S(1)}, bf16[17,16,128]{2,1,0:T...) custom-call(bf16[16,16,16,128]{3,2,1,0:T(8,128)(2,1)} %adj.3, ...), custom_call_target="tpu_custom_call" | custom-call | tf_op jit(solution)/shard_map/pack/pallas_call | solution.py:248
  2.0 3.3 %collective-permute-start = (bf16[18,16,128]{2,1,0:T(8,128)(2,1)S(1)}, bf16[18,16,128]{2,1,0:T(8,128)(2,1)S(1)}, u32[]{:S(2)}, u32[]{:S(2)}) collective-permute-start(bf16[18,16,128]{2,1,0:T(8,128)(2,1)S(1)} %get-tuple-element.13), channel_id=1, source_target_pairs={{0,16},{32,48},{64,80},{96,112},{128,144},{160,176},{192,208},{224... | collective-permute-start | bytes 221192 | tf_op jit(solution)/shard_map/ppermute | solution.py:32
  5.3 1.9 %collective-permute-start.1 = (bf16[18,16,128]{2,1,0:T(8,128)(2,1)S(1)}, bf16[18,16,128]{2,1,0:T(8,128)(2,1)S(1)}, u32[]{:S(2)}, u32[]{:S(2)}) collective-permute-start(bf16[18,16,128]{2,1,0:T(8,128)(2,1)S(1)} %get-tuple-element.14), channel_id=1, source_target_pairs={{16,32},{48,64},{80,96},{112,128},{144,160},{176,192},{208,224},{2... | collective-permute-start | bytes 221192 | tf_op jit(solution)/shard_map/ppermute | solution.py:32
  7.2 4.0 %collective-permute-start.2 = (bf16[17,16,128]{2,1,0:T(8,128)(2,1)S(1)}, bf16[17,16,128]{2,1,0:T(8,128)(2,1)S(1)}, u32[]{:S(2)}, u32[]{:S(2)}) collective-permute-start(bf16[17,16,128]{2,1,0:T(8,128)(2,1)S(1)} %get-tuple-element.15), channel_id=1, source_target_pairs={{0,1},{1,2},{2,3},{3,4},{4,5},{5,6},{6,7},{7,8},{8,9},{9,10},{10,1... | collective-permute-start | bytes 208904 | tf_op jit(solution)/shard_map/ppermute | solution.py:26
  11.2 11.8 %collective-permute-start.3 = (bf16[17,16,128]{2,1,0:T(8,128)(2,1)S(1)}, bf16[17,16,128]{2,1,0:T(8,128)(2,1)S(1)}, u32[]{:S(2)}, u32[]{:S(2)}) collective-permute-start(bf16[17,16,128]{2,1,0:T(8,128)(2,1)S(1)} %get-tuple-element.16), channel_id=1, source_target_pairs={{1,0},{2,1},{3,2},{4,3},{5,4},{6,5},{7,6},{8,7},{9,8},{10,9},{11,1... | collective-permute-start | bytes 208904 | tf_op jit(solution)/shard_map/ppermute | solution.py:26
  23.0 0.0 copy-done
  23.0 0.3 local.1.base
  23.4 0.0 collective-permute-done.2.b_lo
  23.4 0.5 %collective-permute-done.3.b_hi = bf16[17,16,128]{2,1,0:T(8,128)(2,1)S(1)} collective-permute-done((bf16[17,16,128]{2,1,0:T(8,128)(2,1)S(1)}, bf16[17,16,128]{2,1,0:T(8,128)(2,1)S(1)}, u32[]{:S(2)}, u32[]{:S(2)}) %collective-permute-start.3) | collective-permute-done | bytes 69664 | tf_op jit(solution)/shard_map/ppermute | solution.py:26
  23.9 0.0 collective-permute-done.first
  23.9 0.0 collective-permute-done.1.second
  23.9 1.0 %message.1 = bf16[16,24,128]{2,1,0:T(8,128)(2,1)} custom-call(f32[256,128]{1,0:T(8,128)S(1)} %local.1.base, bf16[256,256]{1,0:T(8,128)(2,1)S(1)} %get-tuple-element.18.pick, f32[16,128]{1,0:T(8,128)S(1)} %get-tuple-element.19.ids, bf16[7,128,128]{2,1,0:T(8,128)(2,1)S(1)} %get-tuple-element.12.coupling, bf16[18,16,128]{2,1,0:T(8,128)(2,1)S(1)} %collective-permute-done.first, ...), custom_call_target="tpu_custom_call" | custom-call | flops 16777216 | bytes 1048576 | tf_op jit(solution)/shard_map/message/pallas_call | solution.py:287
  24.9 0.0 copy-start.1
  24.9 3.8 %all-to-all-start = ((bf16[16,24,128]{2,1,0:T(8,128)(2,1)}), bf16[16,24,128]{2,1,0:T(8,128)(2,1)S(1)}, u32[]{:S(2)}, u32[]{:S(2)}) async-start(bf16[16,24,128]{2,1,0:T(8,128)(2,1)} %message.1), calls=%async_computation | async-start | bytes 196608 | tf_op jit(solution)/shard_map/all_to_all | solution.py:301
  28.7 0.0 copy-done.1
  28.7 2.9 %update.1 = (bf16[16,16,16,128]{3,2,1,0:T(8,128)(2,1)}, f32[8,16,128]{2,1,0:T(8,128)S(1)}, f32[8,16,128]{2,1,0:T(8,128)S(1)}) custom-call(bf16[16,16,16,128]{3,2,1,0:T(8,128)(2,1)S(1)} %copy-done, bf16[7,128,128]{2,1,0:T(8,128)(2,1)S(1)} %get-tuple-element.12.coupling, f32[8,16,128]{2,1,0:T(8,128)S(1)} %copy-done.1, ...), custom_call_target="tpu_custom_call" | custom-call | flops 939524096 | bytes 4194304 | tf_op jit(solution)/shard_map/update/pallas_call | solution.py:303
  31.6 5.6 %all-to-all-done.got = bf16[16,24,128]{2,1,0:T(8,128)(2,1)S(1)} async-done(((bf16[16,24,128]{2,1,0:T(8,128)(2,1)}), bf16[16,24,128]{2,1,0:T(8,128)(2,1)S(1)}, u32[]{:S(2)}, u32[]{:S(2)}) %all-to-all-start) | async-done | bytes 98336 | tf_op jit(solution)/shard_map/all_to_all | solution.py:301
  37.2 0.8 %gradient.1 = f32[8,16,128]{2,1,0:T(8,128)} custom-call(bf16[16,24,128]{2,1,0:T(8,128)(2,1)S(1)} %all-to-all-done.got, f32[8,16,128]{2,1,0:T(8,128)S(1)} %get-tuple-element.20.prior, f32[8,16,128]{2,1,0:T(8,128)S(1)} %get-tuple-element.21.scale), custom_call_target="tpu_custom_call" | custom-call | flops 8388608 | bytes 524288 | tf_op jit(solution)/shard_map/gradient/pallas_call | solution.py:325
Async XLA Ops:
  0.6 22.4 %copy-start = (bf16[16,16,16,128]{3,2,1,0:T(8,128)(2,1)S(1)}, bf16[16,16,16,128]{3,2,1,0:T(8,128)(2,1)}, u32[]{:S(2)}) copy-start(bf16[16,16,16,128]{3,2,1,0:T(8,128)(2,1)} %adj.3) | copy-start | bytes 3145732
  2.0 21.9 %collective-permute-start = (bf16[18,16,128]{2,1,0:T(8,128)(2,1)S(1)}, bf16[18,16,128]{2,1,0:T(8,128)(2,1)S(1)}, u32[]{:S(2)}, u32[]{:S(2)}) collective-permute-start(bf16[18,16,128]{2,1,0:T(8,128)(2,1)S(1)} %get-tuple-element.13), channel_id=1, source_target_pairs={{0,16},{32,48},{64,80},{96,112},{128,144},{160,176},{192,208},{224... | collective-permute-start | bytes 221192 | tf_op jit(solution)/shard_map/ppermute | solution.py:32
  5.3 18.6 %collective-permute-start.1 = (bf16[18,16,128]{2,1,0:T(8,128)(2,1)S(1)}, bf16[18,16,128]{2,1,0:T(8,128)(2,1)S(1)}, u32[]{:S(2)}, u32[]{:S(2)}) collective-permute-start(bf16[18,16,128]{2,1,0:T(8,128)(2,1)S(1)} %get-tuple-element.14), channel_id=1, source_target_pairs={{16,32},{48,64},{80,96},{112,128},{144,160},{176,192},{208,224},{2... | collective-permute-start | bytes 221192 | tf_op jit(solution)/shard_map/ppermute | solution.py:32
  7.2 16.1 %collective-permute-start.2 = (bf16[17,16,128]{2,1,0:T(8,128)(2,1)S(1)}, bf16[17,16,128]{2,1,0:T(8,128)(2,1)S(1)}, u32[]{:S(2)}, u32[]{:S(2)}) collective-permute-start(bf16[17,16,128]{2,1,0:T(8,128)(2,1)S(1)} %get-tuple-element.15), channel_id=1, source_target_pairs={{0,1},{1,2},{2,3},{3,4},{4,5},{5,6},{6,7},{7,8},{8,9},{9,10},{10,1... | collective-permute-start | bytes 208904 | tf_op jit(solution)/shard_map/ppermute | solution.py:26
  11.2 12.7 %collective-permute-start.3 = (bf16[17,16,128]{2,1,0:T(8,128)(2,1)S(1)}, bf16[17,16,128]{2,1,0:T(8,128)(2,1)S(1)}, u32[]{:S(2)}, u32[]{:S(2)}) collective-permute-start(bf16[17,16,128]{2,1,0:T(8,128)(2,1)S(1)} %get-tuple-element.16), channel_id=1, source_target_pairs={{1,0},{2,1},{3,2},{4,3},{5,4},{6,5},{7,6},{8,7},{9,8},{10,9},{11,1... | collective-permute-start | bytes 208904 | tf_op jit(solution)/shard_map/ppermute | solution.py:26
  24.9 3.8 %copy-start.1 = (f32[8,16,128]{2,1,0:T(8,128)S(1)}, f32[8,16,128]{2,1,0:T(8,128)}, u32[]{:S(2)}) copy-start(f32[8,16,128]{2,1,0:T(8,128)} %logf.1) | copy-start | bytes 196612
  24.9 12.3 %all-to-all-start = ((bf16[16,24,128]{2,1,0:T(8,128)(2,1)}), bf16[16,24,128]{2,1,0:T(8,128)(2,1)S(1)}, u32[]{:S(2)}, u32[]{:S(2)}) async-start(bf16[16,24,128]{2,1,0:T(8,128)(2,1)} %message.1), calls=%async_computation | async-start | bytes 196608 | tf_op jit(solution)/shard_map/all_to_all | solution.py:301

commit v4 on v2

--- a/solution.py
+++ b/solution.py
@@ -1,5 +1,3 @@
-import functools
-
 import jax
 import jax.numpy as jnp
 from jax import lax
@@ -10,7 +8,6 @@
 F32 = jnp.float32
 BF16 = jnp.bfloat16
 VMEM = pl.BlockSpec(memory_space=pltpu.VMEM)
-ANY = pl.BlockSpec(memory_space=pl.ANY)
 HBM = pl.BlockSpec(memory_space=pltpu.HBM)
 MSG = 24
 
@@ -29,25 +26,41 @@
     return lax.ppermute(block, axis, pairs)
 
 
-def pack_body(adj, logf_hbm, coupling, to_a_hi, to_a_lo, to_b_hi, to_b_lo, blocks, logf, sems):
-    ca, cb = adj.shape[0], adj.shape[1]
-    pa, pb = logf.shape[0], logf.shape[1]
+def swap(block, first):
+    count = lax.axis_size("gy")
+    pairs = [(i, i + 1) for i in range(first, count - 1, 2)]
+    return lax.ppermute(block, "gy", pairs + [(j, i) for i, j in pairs])
+
+
+def pack_body(adj_hbm, logf_hbm, coupling_hbm, to_a_hi, to_a_lo, to_far, to_near, coupling,
+              logf, sems):
+    ca, cb = adj_hbm.shape[0], adj_hbm.shape[1]
+    pa, pb, _ = logf.shape
+    odd = lax.axis_index("gy") % 2
+    column = (cb - 1) * (1 - odd)
+    fields = pltpu.make_async_copy(logf_hbm, logf, sems.at[0])
     copies = [
-        pltpu.make_async_copy(adj.at[ca - 1], to_a_hi.at[pl.ds(0, cb)], sems.at[0]),
-        pltpu.make_async_copy(adj.at[0], to_a_lo.at[pl.ds(0, cb)], sems.at[1]),
-        pltpu.make_async_copy(adj.at[:, cb - 1], to_b_hi.at[pl.ds(0, ca)], sems.at[2]),
-        pltpu.make_async_copy(adj.at[:, 0], to_b_lo.at[pl.ds(0, ca)], sems.at[3]),
-        pltpu.make_async_copy(coupling, blocks, sems.at[4]),
+        pltpu.make_async_copy(source, target, sems.at[1 + k])
+        for k, (source, target) in enumerate(
+            (
+                (adj_hbm.at[ca - 1], to_a_hi.at[pl.ds(0, cb)]),
+                (adj_hbm.at[0], to_a_lo.at[pl.ds(0, cb)]),
+                (adj_hbm.at[:, cb - 1 - column], to_far.at[pl.ds(0, ca)]),
+                (adj_hbm.at[:, column], to_near.at[pl.ds(0, ca)]),
+                (coupling_hbm, coupling),
+            )
+        )
     ]
-    fields = pltpu.make_async_copy(logf_hbm, logf, sems.at[5])
     fields.start()
     for copy in copies:
         copy.start()
     fields.wait()
     to_a_hi[cb:cb + 2] = logf[pa - 2:pa].astype(BF16)
     to_a_lo[cb:cb + 2] = logf[0:2].astype(BF16)
-    to_b_hi[ca] = jnp.concatenate([logf[:, pb - 2, :], logf[:, pb - 1, :]], axis=0).astype(BF16)
-    to_b_lo[ca] = jnp.concatenate([logf[:, 0, :], logf[:, 1, :]], axis=0).astype(BF16)
+    hi = jnp.concatenate([logf[:, pb - 2, :], logf[:, pb - 1, :]], axis=0)
+    lo = jnp.concatenate([logf[:, 0, :], logf[:, 1, :]], axis=0)
+    to_far[ca] = jnp.where(odd == 1, hi, lo).astype(BF16)
+    to_near[ca] = jnp.where(odd == 1, lo, hi).astype(BF16)
     for copy in copies:
         copy.wait()
 
@@ -69,8 +82,7 @@
     total = total + jnp.where(column > 0, before, 0.0) + jnp.where(column < cb - 1, after, 0.0)
     base[...] = total
     face = lax.broadcasted_iota(jnp.int32, (faces, faces), 0)
-    picked_by = jnp.where(send[0] == face, 1.0, 0.0)
-    pick[...] = picked_by.T.astype(BF16)
+    pick[...] = jnp.where(send[0] == face, 1.0, 0.0).T.astype(BF16)
     owners, slots = nodes.shape[2], nodes.shape[3]
     sub = lax.broadcasted_iota(jnp.int32, (slots, width), 0)
     lane = lax.broadcasted_iota(jnp.int32, (slots, width), 1)
@@ -85,19 +97,26 @@
     ids[...] = jnp.where(jnp.logical_and(mine, alive), listed, 0.0)
 
 
-def message_body(base, pick, ids, coupling, a_lo, a_hi, b_lo, b_hi, out, total, wide):
+def message_body(base, pick, ids, coupling, a_lo, a_hi, far, near, out, total, wide):
     faces, width = base.shape
     owners, slots = out.shape[0], faces // out.shape[0]
     cb = a_lo.shape[0] - 2
-    ca = b_lo.shape[0] - 1
-    for k, halo in enumerate((a_lo, a_hi, b_lo, b_hi)):
+    ca = far.shape[0] - 1
+    here = lax.axis_index("gy")
+    odd = here % 2 == 1
+    for k, halo in enumerate((a_lo, a_hi, far, near)):
         rows = cb if k < 2 else ca
         wide[k * rows * 8:(k + 1) * rows * 8] = (
             halo[0:rows, 0:8, :].astype(F32).reshape(rows * 8, width)
         )
 
+    def row(k, rows):
+        return wide[pl.ds(k * rows * 8, rows, stride=8), :]
+
     def edge(k, rows):
-        return wide[pl.ds(k * rows * 8, rows, stride=8), :].astype(BF16)
+        if k < 2:
+            return row(k, rows).astype(BF16)
+        return jnp.where(odd, row(5 - k, rows), row(k, rows)).astype(BF16)
 
     total[...] = base[...]
     total[0:cb] += dot(edge(0, cb), coupling[3])
@@ -105,7 +124,6 @@
     total[pl.ds(0, ca, stride=cb), :] += dot(edge(2, ca), coupling[5])
     total[pl.ds(cb - 1, ca, stride=cb), :] += dot(edge(3, ca), coupling[6])
     picked = dot(pick[...], total[...].astype(BF16)).astype(BF16)
-    here = lax.axis_index("gy")
     pb = a_lo.shape[1]
     top = a_lo[cb + 1].astype(F32)
     bottom = a_hi[cb].astype(F32)
@@ -121,11 +139,23 @@
         out[o, slots:MSG] = jnp.where(o > here, extra(o, pb - 1), extra(o, 0)).astype(BF16)
 
 
-def update_body(adj, coupling, logf, a_lo, a_hi, b_lo, b_hi, out, prior, scale,
-                held, field, once, sems):
+def update_body(adj, coupling, logf, a_lo, a_hi, far, near, out, prior, scale,
+                b_lo, b_hi, held, field, once, sems):
     ca, cb, nl, width = adj.shape
     rows = cb * nl
     layer = lax.broadcasted_iota(jnp.int32, (rows, width), 0) % nl
+    odd = lax.axis_index("gy") % 2 == 1
+
+    @pl.when(odd)
+    def _():
+        b_lo[...] = near[...]
+        b_hi[...] = far[...]
+
+    @pl.when(jnp.logical_not(odd))
+    def _():
+        b_lo[...] = far[...]
+        b_hi[...] = near[...]
+
     copies = []
     for a in range(ca):
         own = adj[a].reshape(rows, width)
@@ -209,7 +239,7 @@
     shape = jax.ShapeDtypeStruct
     wire = pltpu.CompilerParams(vmem_limit_bytes=16 * 2**20)
 
-    to_a_hi, to_a_lo, to_b_hi, to_b_lo, blocks = pl.pallas_call(
+    to_a_hi, to_a_lo, to_far, to_near, blocks = pl.pallas_call(
         pack_body,
         out_shape=(
             shape((cb + 2, nl, width), BF16),
@@ -223,11 +253,11 @@
         scratch_shapes=[pltpu.VMEM(log_friction.shape, F32), pltpu.SemaphoreType.DMA((6,))],
         compiler_params=wire,
         name="pack",
-    )(in_hbm(adjoint_trace), in_hbm(log_friction), in_hbm(coupling))
+    )(*map(in_hbm, (adjoint_trace, log_friction, coupling)))
     a_lo = shift(to_a_hi, "gx", 1)
     a_hi = shift(to_a_lo, "gx", -1)
-    b_lo = shift(to_b_hi, "gy", 1)
-    b_hi = shift(to_b_lo, "gy", -1)
+    far = swap(to_far, 1)
+    near = swap(to_near, 0)
 
     base, pick, ids = pl.pallas_call(
         local_body,
@@ -256,7 +286,7 @@
         compiler_params=wire,
         cost_estimate=cost(2 * faces * faces * width, 2**20),
         name="message",
-    )(base, pick, ids, blocks, a_lo, a_hi, b_lo, b_hi)
+    )(base, pick, ids, blocks, a_lo, a_hi, far, near)
 
     received = lax.all_to_all(message, "gy", split_axis=0, concat_axis=0, tiled=True)
 
@@ -270,6 +300,8 @@
         in_specs=[VMEM] * 7,
         out_specs=(HBM, VMEM, VMEM),
         scratch_shapes=[
+            pltpu.VMEM((ca + 1, nl, width), BF16),
+            pltpu.VMEM((ca + 1, nl, width), BF16),
             pltpu.VMEM(adjoint_trace.shape, BF16),
             pltpu.VMEM((pa + 4, pb + 16, width), F32),
             pltpu.VMEM((pa + 2, pb + 16, width), F32),
@@ -278,7 +310,7 @@
         compiler_params=wire,
         cost_estimate=cost(2 * 7 * faces * nl * width * width, 4 * 2**20),
         name="update",
-    )(adjoint_trace, blocks, log_friction, a_lo, a_hi, b_lo, b_hi)
+    )(adjoint_trace, blocks, log_friction, a_lo, a_hi, far, near)
 
     gradient = pl.pallas_call(
         gradient_body,

time: 38.3 us -> 37.7 us (0.984)
  the two profiles are of different devices: /device:TPU:513 before, /device:TPU:1 now
where the time goes in v4:
time: 37.7 us; the launch traced here: 37.3 us
  starting transfers between devices  24.2 us (64%)
  Pallas kernels  6.25 us (17%)
  waiting for transfers between devices  6.09 us (16%)
  between operations  0.76 us (2%)
    ppermute x2, starting transfers between devices, swap(): return lax.ppermute(block, 'gy', pairs + [(j, i) for i, j in pairs])  13.9 us
    all_to_all x1, waiting for transfers between devices, per_device(): lax.all_to_all(message, 'gy', split_axis=0, concat_axis=0, tiled=True)  5.59 us
    ppermute x2, starting transfers between devices, shift(): return lax.ppermute(block, axis, pairs)  5.44 us
    all_to_all x1, starting transfers between devices, per_device(): lax.all_to_all(message, 'gy', split_axis=0, concat_axis=0, tiled=True)  4.88 us
    pallas_call x1, Pallas kernels, per_device(): pl.pallas_call(update_body, out_shape=(shape(adjoint_trace.shape, BF16),...  2.91 us
    pallas_call x1, Pallas kernels, per_device(): pl.pallas_call(pack_body, out_shape=(shape((cb + 2, nl, width), BF16), sh...  1.24 us
    pallas_call x1, Pallas kernels, per_device(): pl.pallas_call(message_body, out_shape=shape((owners, MSG, width), BF16),...  0.97 us
    pallas_call x1, Pallas kernels, per_device(): pl.pallas_call(gradient_body, out_shape=shape(log_friction.shape, F32), i...  0.8 us
  transfers between devices with their start and end apart: 5, of which 2 were waited for; matrix products, arithmetic and copies ran while one was open for 0% of the time, Pallas kernels for 9%

profile of v4, /device:TPU:1, one launch (start us, length us, event | category | flops | bytes accessed | tf_op | source)
XLA Modules:
  0.0 37.3 jit_solution(8597891920951531711)
XLA Ops:
  0.6 0.0 copy-start
  0.6 0.0 copy-start.4
  0.6 1.2 %pack.1 = (bf16[18,16,128]{2,1,0:T(8,128)(2,1)S(1)}, bf16[18,16,128]{2,1,0:T(8,128)(2,1)S(1)}, bf16[17,16,128]{2,1,0:T(8,128)(2,1)S(1)}, bf16[17,16,128]{2,1,0:T(8,128)(2,1)S(1)}, bf16[7,128,128]{2,1,0:T(8,128)(2,1)S(1)}) custom-call(bf16[16,16,16,128]{3,2,1,0:T(8,128)(2,1)} %adj.3, f32[8,16,128]{2,1,0:T(8,128)} %logf.1, bf16[7,128,128]{2,1,0:T(8,128)(2,1)} %coupling_hbm.1), custom_call_target="tpu_custom_call" | custom-call | tf_op jit(solution)/shard_map/pack/pallas_call | solution.py:242
  1.9 0.0 copy-start.2
  1.9 4.1 %collective-permute-start = (bf16[18,16,128]{2,1,0:T(8,128)(2,1)S(1)}, bf16[18,16,128]{2,1,0:T(8,128)(2,1)S(1)}, u32[]{:S(2)}, u32[]{:S(2)}) collective-permute-start(bf16[18,16,128]{2,1,0:T(8,128)(2,1)S(1)} %get-tuple-element.14), channel_id=1, source_target_pairs={{0,16},{16,32},{32,48},{48,64},{64,80},{80,96},{96,112},{112,128},... | collective-permute-start | bytes 221192 | tf_op jit(solution)/shard_map/ppermute | solution.py:26
  6.1 1.3 %collective-permute-start.1 = (bf16[18,16,128]{2,1,0:T(8,128)(2,1)S(1)}, bf16[18,16,128]{2,1,0:T(8,128)(2,1)S(1)}, u32[]{:S(2)}, u32[]{:S(2)}) collective-permute-start(bf16[18,16,128]{2,1,0:T(8,128)(2,1)S(1)} %get-tuple-element.15), channel_id=1, source_target_pairs={{16,0},{32,16},{48,32},{64,48},{80,64},{96,80},{112,96},{128,112},... | collective-permute-start | bytes 221192 | tf_op jit(solution)/shard_map/ppermute | solution.py:26
  7.4 4.0 %collective-permute-start.2 = (bf16[17,16,128]{2,1,0:T(8,128)(2,1)S(1)}, bf16[17,16,128]{2,1,0:T(8,128)(2,1)S(1)}, u32[]{:S(2)}, u32[]{:S(2)}) collective-permute-start(bf16[17,16,128]{2,1,0:T(8,128)(2,1)S(1)} %get-tuple-element.16), channel_id=1, source_target_pairs={{1,2},{3,4},{5,6},{7,8},{9,10},{11,12},{13,14},{2,1},{4,3},{6,5},{... | collective-permute-start | bytes 208904 | tf_op jit(solution)/shard_map/ppermute | solution.py:32
  11.3 0.0 copy-start.3
  11.3 9.9 %collective-permute-start.3 = (bf16[17,16,128]{2,1,0:T(8,128)(2,1)S(1)}, bf16[17,16,128]{2,1,0:T(8,128)(2,1)S(1)}, u32[]{:S(2)}, u32[]{:S(2)}) collective-permute-start(bf16[17,16,128]{2,1,0:T(8,128)(2,1)S(1)} %get-tuple-element.17), channel_id=1, source_target_pairs={{0,1},{2,3},{4,5},{6,7},{8,9},{10,11},{12,13},{14,15},{1,0},{3,2},... | collective-permute-start | bytes 208904 | tf_op jit(solution)/shard_map/ppermute | solution.py:32
  21.3 0.0 copy-done
  21.3 0.0 copy-done.4
  21.3 0.0 copy-done.2
  21.3 0.0 copy-done.3
  21.3 0.3 local.1
  21.6 0.0 collective-permute-done.2.far
  21.7 0.5 %collective-permute-done.3.near = bf16[17,16,128]{2,1,0:T(8,128)(2,1)S(1)} collective-permute-done((bf16[17,16,128]{2,1,0:T(8,128)(2,1)S(1)}, bf16[17,16,128]{2,1,0:T(8,128)(2,1)S(1)}, u32[]{:S(2)}, u32[]{:S(2)}) %collective-permute-start.3) | collective-permute-done | bytes 69664 | tf_op jit(solution)/shard_map/ppermute | solution.py:32
  22.1 0.0 collective-permute-done.a_lo
  22.2 0.0 collective-permute-done.1.a_hi
  22.2 1.0 %message.1 = bf16[16,24,128]{2,1,0:T(8,128)(2,1)} custom-call(f32[256,128]{1,0:T(8,128)S(1)} %get-tuple-element.19.base, bf16[256,256]{1,0:T(8,128)(2,1)S(1)} %get-tuple-element.20.pick, f32[16,128]{1,0:T(8,128)S(1)} %get-tuple-element.21.ids, bf16[7,128,128]{2,1,0:T(8,128)(2,1)S(1)} %get-tuple-element.13.coupling, ...), custom_call_target="tpu_custom_call" | custom-call | flops 16777216 | bytes 1048576 | tf_op jit(solution)/shard_map/message/pallas_call | solution.py:277
  23.1 0.0 copy-start.1
  23.1 4.9 %all-to-all-start = ((bf16[16,24,128]{2,1,0:T(8,128)(2,1)}), bf16[16,24,128]{2,1,0:T(8,128)(2,1)S(1)}, u32[]{:S(2)}, u32[]{:S(2)}) async-start(bf16[16,24,128]{2,1,0:T(8,128)(2,1)} %message.1), calls=%async_computation | async-start | bytes 196608 | tf_op jit(solution)/shard_map/all_to_all | solution.py:291
  28.0 0.0 copy-done.1
  28.0 2.9 %update.1 = (bf16[16,16,16,128]{3,2,1,0:T(8,128)(2,1)}, f32[8,16,128]{2,1,0:T(8,128)S(1)}, f32[8,16,128]{2,1,0:T(8,128)S(1)}) custom-call(bf16[16,16,16,128]{3,2,1,0:T(8,128)(2,1)S(1)} %copy-done, bf16[7,128,128]{2,1,0:T(8,128)(2,1)S(1)} %get-tuple-element.13.coupling, f32[8,16,128]{2,1,0:T(8,128)S(1)} %copy-done.1, ...), custom_call_target="tpu_custom_call" | custom-call | flops 939524096 | bytes 4194304 | tf_op jit(solution)/shard_map/update/pallas_call | solution.py:293
  30.9 5.6 %all-to-all-done.got = bf16[16,24,128]{2,1,0:T(8,128)(2,1)S(1)} async-done(((bf16[16,24,128]{2,1,0:T(8,128)(2,1)}), bf16[16,24,128]{2,1,0:T(8,128)(2,1)S(1)}, u32[]{:S(2)}, u32[]{:S(2)}) %all-to-all-start) | async-done | bytes 98336 | tf_op jit(solution)/shard_map/all_to_all | solution.py:291
  36.5 0.8 %gradient.1 = f32[8,16,128]{2,1,0:T(8,128)} custom-call(bf16[16,24,128]{2,1,0:T(8,128)(2,1)S(1)} %all-to-all-done.got, f32[8,16,128]{2,1,0:T(8,128)S(1)} %get-tuple-element.22.prior, f32[8,16,128]{2,1,0:T(8,128)S(1)} %get-tuple-element.23.scale), custom_call_target="tpu_custom_call" | custom-call | flops 8388608 | bytes 524288 | tf_op jit(solution)/shard_map/gradient/pallas_call | solution.py:315
Async XLA Ops:
  0.6 20.6 %copy-start = (bf16[16,16,16,128]{3,2,1,0:T(8,128)(2,1)S(1)}, bf16[16,16,16,128]{3,2,1,0:T(8,128)(2,1)}, u32[]{:S(2)}) copy-start(bf16[16,16,16,128]{3,2,1,0:T(8,128)(2,1)} %adj.3) | copy-start | bytes 3145732
  0.6 20.6 %copy-start.4 = (s32[1,1,16]{2,1,0:T(1,128)S(1)}, s32[1,1,16]{2,1,0:T(1,128)}, u32[]{:S(2)}) copy-start(s32[1,1,16]{2,1,0:T(1,128)} %live.1) | copy-start | bytes 196
  1.9 19.4 %copy-start.2 = (s32[1,1,16,16]{3,2,1,0:T(8,128)S(1)}, s32[1,1,16,16]{3,2,1,0:T(8,128)}, u32[]{:S(2)}) copy-start(s32[1,1,16,16]{3,2,1,0:T(8,128)} %nodes.1) | copy-start | bytes 3076
  1.9 20.2 %collective-permute-start = (bf16[18,16,128]{2,1,0:T(8,128)(2,1)S(1)}, bf16[18,16,128]{2,1,0:T(8,128)(2,1)S(1)}, u32[]{:S(2)}, u32[]{:S(2)}) collective-permute-start(bf16[18,16,128]{2,1,0:T(8,128)(2,1)S(1)} %get-tuple-element.14), channel_id=1, source_target_pairs={{0,16},{16,32},{32,48},{48,64},{64,80},{80,96},{96,112},{112,128},... | collective-permute-start | bytes 221192 | tf_op jit(solution)/shard_map/ppermute | solution.py:26
  6.1 16.1 %collective-permute-start.1 = (bf16[18,16,128]{2,1,0:T(8,128)(2,1)S(1)}, bf16[18,16,128]{2,1,0:T(8,128)(2,1)S(1)}, u32[]{:S(2)}, u32[]{:S(2)}) collective-permute-start(bf16[18,16,128]{2,1,0:T(8,128)(2,1)S(1)} %get-tuple-element.15), channel_id=1, source_target_pairs={{16,0},{32,16},{48,32},{64,48},{80,64},{96,80},{112,96},{128,112},... | collective-permute-start | bytes 221192 | tf_op jit(solution)/shard_map/ppermute | solution.py:26
  7.4 14.3 %collective-permute-start.2 = (bf16[17,16,128]{2,1,0:T(8,128)(2,1)S(1)}, bf16[17,16,128]{2,1,0:T(8,128)(2,1)S(1)}, u32[]{:S(2)}, u32[]{:S(2)}) collective-permute-start(bf16[17,16,128]{2,1,0:T(8,128)(2,1)S(1)} %get-tuple-element.16), channel_id=1, source_target_pairs={{1,2},{3,4},{5,6},{7,8},{9,10},{11,12},{13,14},{2,1},{4,3},{6,5},{... | collective-permute-start | bytes 208904 | tf_op jit(solution)/shard_map/ppermute | solution.py:32
  11.3 10.0 %copy-start.3 = (s32[1,1,256]{2,1,0:T(1,128)S(1)}, s32[1,1,256]{2,1,0:T(1,128)}, u32[]{:S(2)}) copy-start(s32[1,1,256]{2,1,0:T(1,128)} %send.1) | copy-start | bytes 3076
  11.3 10.8 %collective-permute-start.3 = (bf16[17,16,128]{2,1,0:T(8,128)(2,1)S(1)}, bf16[17,16,128]{2,1,0:T(8,128)(2,1)S(1)}, u32[]{:S(2)}, u32[]{:S(2)}) collective-permute-start(bf16[17,16,128]{2,1,0:T(8,128)(2,1)S(1)} %get-tuple-element.17), channel_id=1, source_target_pairs={{0,1},{2,3},{4,5},{6,7},{8,9},{10,11},{12,13},{14,15},{1,0},{3,2},... | collective-permute-start | bytes 208904 | tf_op jit(solution)/shard_map/ppermute | solution.py:32
  23.1 4.9 %copy-start.1 = (f32[8,16,128]{2,1,0:T(8,128)S(1)}, f32[8,16,128]{2,1,0:T(8,128)}, u32[]{:S(2)}) copy-start(f32[8,16,128]{2,1,0:T(8,128)} %logf.1) | copy-start | bytes 196612
  23.1 13.4 %all-to-all-start = ((bf16[16,24,128]{2,1,0:T(8,128)(2,1)}), bf16[16,24,128]{2,1,0:T(8,128)(2,1)S(1)}, u32[]{:S(2)}, u32[]{:S(2)}) async-start(bf16[16,24,128]{2,1,0:T(8,128)(2,1)} %message.1), calls=%async_computation | async-start | bytes 196608 | tf_op jit(solution)/shard_map/all_to_all | solution.py:291

commit v5 on v4

--- a/solution.py
+++ b/solution.py
@@ -20,33 +20,28 @@
     return pltpu.with_memory_space_constraint(array, pltpu.HBM)
 
 
-def shift(block, axis, step):
+def swap(block, axis, first):
     count = lax.axis_size(axis)
-    pairs = [(i, i + step) for i in range(count) if 0 <= i + step < count]
-    return lax.ppermute(block, axis, pairs)
-
-
-def swap(block, first):
-    count = lax.axis_size("gy")
     pairs = [(i, i + 1) for i in range(first, count - 1, 2)]
-    return lax.ppermute(block, "gy", pairs + [(j, i) for i, j in pairs])
-
-
-def pack_body(adj_hbm, logf_hbm, coupling_hbm, to_a_hi, to_a_lo, to_far, to_near, coupling,
+    return lax.ppermute(block, axis, pairs + [(j, i) for i, j in pairs])
+
+
+def pack_body(adj_hbm, logf_hbm, coupling_hbm, to_a_far, to_a_near, to_b_far, to_b_near, coupling,
               logf, sems):
     ca, cb = adj_hbm.shape[0], adj_hbm.shape[1]
     pa, pb, _ = logf.shape
-    odd = lax.axis_index("gy") % 2
-    column = (cb - 1) * (1 - odd)
+    odd_a, odd_b = lax.axis_index("gx") % 2, lax.axis_index("gy") % 2
+    near_a, near_b = (ca - 1) * (1 - odd_a), (cb - 1) * (1 - odd_b)
+    row = (pa - 2) * (1 - odd_a)
     fields = pltpu.make_async_copy(logf_hbm, logf, sems.at[0])
     copies = [
         pltpu.make_async_copy(source, target, sems.at[1 + k])
         for k, (source, target) in enumerate(
             (
-                (adj_hbm.at[ca - 1], to_a_hi.at[pl.ds(0, cb)]),
-                (adj_hbm.at[0], to_a_lo.at[pl.ds(0, cb)]),
-                (adj_hbm.at[:, cb - 1 - column], to_far.at[pl.ds(0, ca)]),
-                (adj_hbm.at[:, column], to_near.at[pl.ds(0, ca)]),
+                (adj_hbm.at[ca - 1 - near_a], to_a_far.at[pl.ds(0, cb)]),
+                (adj_hbm.at[near_a], to_a_near.at[pl.ds(0, cb)]),
+                (adj_hbm.at[:, cb - 1 - near_b], to_b_far.at[pl.ds(0, ca)]),
+                (adj_hbm.at[:, near_b], to_b_near.at[pl.ds(0, ca)]),
                 (coupling_hbm, coupling),
             )
         )
@@ -55,12 +50,12 @@
     for copy in copies:
         copy.start()
     fields.wait()
-    to_a_hi[cb:cb + 2] = logf[pa - 2:pa].astype(BF16)
-    to_a_lo[cb:cb + 2] = logf[0:2].astype(BF16)
+    to_a_far[cb:cb + 2] = logf[pl.ds(pa - 2 - row, 2)].astype(BF16)
+    to_a_near[cb:cb + 2] = logf[pl.ds(row, 2)].astype(BF16)
     hi = jnp.concatenate([logf[:, pb - 2, :], logf[:, pb - 1, :]], axis=0)
     lo = jnp.concatenate([logf[:, 0, :], logf[:, 1, :]], axis=0)
-    to_far[ca] = jnp.where(odd == 1, hi, lo).astype(BF16)
-    to_near[ca] = jnp.where(odd == 1, lo, hi).astype(BF16)
+    to_b_far[ca] = jnp.where(odd_b == 1, hi, lo).astype(BF16)
+    to_b_near[ca] = jnp.where(odd_b == 1, lo, hi).astype(BF16)
     for copy in copies:
         copy.wait()
 
@@ -97,14 +92,14 @@
     ids[...] = jnp.where(jnp.logical_and(mine, alive), listed, 0.0)
 
 
-def message_body(base, pick, ids, coupling, a_lo, a_hi, far, near, out, total, wide):
+def message_body(base, pick, ids, coupling, a_far, a_near, b_far, b_near, out, total, wide):
     faces, width = base.shape
     owners, slots = out.shape[0], faces // out.shape[0]
-    cb = a_lo.shape[0] - 2
-    ca = far.shape[0] - 1
+    cb = a_far.shape[0] - 2
+    ca = b_far.shape[0] - 1
     here = lax.axis_index("gy")
-    odd = here % 2 == 1
-    for k, halo in enumerate((a_lo, a_hi, far, near)):
+    odd_a, odd_b = lax.axis_index("gx") % 2 == 1, here % 2 == 1
+    for k, halo in enumerate((a_far, a_near, b_far, b_near)):
         rows = cb if k < 2 else ca
         wide[k * rows * 8:(k + 1) * rows * 8] = (
             halo[0:rows, 0:8, :].astype(F32).reshape(rows * 8, width)
@@ -114,9 +109,8 @@
         return wide[pl.ds(k * rows * 8, rows, stride=8), :]
 
     def edge(k, rows):
-        if k < 2:
-            return row(k, rows).astype(BF16)
-        return jnp.where(odd, row(5 - k, rows), row(k, rows)).astype(BF16)
+        odd = odd_a if k < 2 else odd_b
+        return jnp.where(odd, row(k ^ 1, rows), row(k, rows)).astype(BF16)
 
     total[...] = base[...]
     total[0:cb] += dot(edge(0, cb), coupling[3])
@@ -124,9 +118,9 @@
     total[pl.ds(0, ca, stride=cb), :] += dot(edge(2, ca), coupling[5])
     total[pl.ds(cb - 1, ca, stride=cb), :] += dot(edge(3, ca), coupling[6])
     picked = dot(pick[...], total[...].astype(BF16)).astype(BF16)
-    pb = a_lo.shape[1]
-    top = a_lo[cb + 1].astype(F32)
-    bottom = a_hi[cb].astype(F32)
+    pb = a_far.shape[1]
+    top = jnp.where(odd_a, a_near[cb + 1].astype(F32), a_far[cb + 1].astype(F32))
+    bottom = jnp.where(odd_a, a_far[cb].astype(F32), a_near[cb].astype(F32))
     sub = lax.broadcasted_iota(jnp.int32, (MSG - slots, width), 0)
 
     def extra(o, column):
@@ -139,22 +133,21 @@
         out[o, slots:MSG] = jnp.where(o > here, extra(o, pb - 1), extra(o, 0)).astype(BF16)
 
 
-def update_body(adj, coupling, logf, a_lo, a_hi, far, near, out, prior, scale,
-                b_lo, b_hi, held, field, once, sems):
+def update_body(adj, coupling, logf, a_far, a_near, b_far, b_near, out, prior, scale,
+                a_lo, a_hi, b_lo, b_hi, held, field, once, sems):
     ca, cb, nl, width = adj.shape
     rows = cb * nl
     layer = lax.broadcasted_iota(jnp.int32, (rows, width), 0) % nl
-    odd = lax.axis_index("gy") % 2 == 1
-
-    @pl.when(odd)
-    def _():
-        b_lo[...] = near[...]
-        b_hi[...] = far[...]
-
-    @pl.when(jnp.logical_not(odd))
-    def _():
-        b_lo[...] = far[...]
-        b_hi[...] = near[...]
+    for axis, far, near, lo, hi in (
+        ("gx", a_far, a_near, a_lo, a_hi), ("gy", b_far, b_near, b_lo, b_hi)
+    ):
+        odd = lax.axis_index(axis) % 2 == 1
+        for which, low, high in ((odd, near, far), (jnp.logical_not(odd), far, near)):
+
+            @pl.when(which)
+            def _():
+                lo[...] = low[...]
+                hi[...] = high[...]
 
     copies = []
     for a in range(ca):
@@ -239,7 +232,7 @@
     shape = jax.ShapeDtypeStruct
     wire = pltpu.CompilerParams(vmem_limit_bytes=16 * 2**20)
 
-    to_a_hi, to_a_lo, to_far, to_near, blocks = pl.pallas_call(
+    to_a_far, to_a_near, to_b_far, to_b_near, blocks = pl.pallas_call(
         pack_body,
         out_shape=(
             shape((cb + 2, nl, width), BF16),
@@ -254,10 +247,10 @@
         compiler_params=wire,
         name="pack",
     )(*map(in_hbm, (adjoint_trace, log_friction, coupling)))
-    a_lo = shift(to_a_hi, "gx", 1)
-    a_hi = shift(to_a_lo, "gx", -1)
-    far = swap(to_far, 1)
-    near = swap(to_near, 0)
+    a_far = swap(to_a_far, "gx", 1)
+    a_near = swap(to_a_near, "gx", 0)
+    b_far = swap(to_b_far, "gy", 1)
+    b_near = swap(to_b_near, "gy", 0)
 
     base, pick, ids = pl.pallas_call(
         local_body,
@@ -286,7 +279,7 @@
         compiler_params=wire,
         cost_estimate=cost(2 * faces * faces * width, 2**20),
         name="message",
-    )(base, pick, ids, blocks, a_lo, a_hi, far, near)
+    )(base, pick, ids, blocks, a_far, a_near, b_far, b_near)
 
     received = lax.all_to_all(message, "gy", split_axis=0, concat_axis=0, tiled=True)
 
@@ -300,6 +293,8 @@
         in_specs=[VMEM] * 7,
         out_specs=(HBM, VMEM, VMEM),
         scratch_shapes=[
+            pltpu.VMEM((cb + 2, nl, width), BF16),
+            pltpu.VMEM((cb + 2, nl, width), BF16),
             pltpu.VMEM((ca + 1, nl, width), BF16),
             pltpu.VMEM((ca + 1, nl, width), BF16),
             pltpu.VMEM(adjoint_trace.shape, BF16),
@@ -310,7 +305,7 @@
         compiler_params=wire,
         cost_estimate=cost(2 * 7 * faces * nl * width * width, 4 * 2**20),
         name="update",
-    )(adjoint_trace, blocks, log_friction, a_lo, a_hi, far, near)
+    )(adjoint_trace, blocks, log_friction, a_far, a_near, b_far, b_near)
 
     gradient = pl.pallas_call(
         gradient_body,

time: 37.7 us -> 37 us (0.981)
  starting transfers between devices: 24.2 us -> 23.6 us
    all_to_all x1, starting transfers between devices: 4.88 us -> 4.25 us  [per_device(): lax.all_to_all(message, 'gy', split_axis=0, concat_axis=0, tiled=True)]
where the time goes in v5:
time: 37 us; the launch traced here: 36.7 us
  starting transfers between devices  23.6 us (64%)
  Pallas kernels  6.28 us (17%)
  waiting for transfers between devices  6.07 us (16%)
  between operations  0.76 us (2%)
    ppermute x4, starting transfers between devices, swap(): return lax.ppermute(block, axis, pairs + [(j, i) for i, j in pairs])  19.3 us
    all_to_all x1, waiting for transfers between devices, per_device(): lax.all_to_all(message, 'gy', split_axis=0, concat_axis=0, tiled=True)  5.57 us
    all_to_all x1, starting transfers between devices, per_device(): lax.all_to_all(message, 'gy', split_axis=0, concat_axis=0, tiled=True)  4.25 us
    pallas_call x1, Pallas kernels, per_device(): pl.pallas_call(update_body, out_shape=(shape(adjoint_trace.shape, BF16),...  2.94 us
    pallas_call x1, Pallas kernels, per_device(): pl.pallas_call(pack_body, out_shape=(shape((cb + 2, nl, width), BF16), sh...  1.24 us
    pallas_call x1, Pallas kernels, per_device(): pl.pallas_call(message_body, out_shape=shape((owners, MSG, width), BF16),...  0.97 us
    pallas_call x1, Pallas kernels, per_device(): pl.pallas_call(gradient_body, out_shape=shape(log_friction.shape, F32), i...  0.8 us
  transfers between devices with their start and end apart: 5, of which 2 were waited for; matrix products, arithmetic and copies ran while one was open for 0% of the time, Pallas kernels for 9%

profile of v5, /device:TPU:1, one launch (start us, length us, event | category | flops | bytes accessed | tf_op | source)
XLA Modules:
  0.0 36.7 jit_solution(12401487945492616508)
XLA Ops:
  0.6 0.0 copy-start
  0.6 0.0 copy-start.4
  0.6 1.2 %pack.1 = (bf16[18,16,128]{2,1,0:T(8,128)(2,1)S(1)}, bf16[18,16,128]{2,1,0:T(8,128)(2,1)S(1)}, bf16[17,16,128]{2,1,0:T(8,128)(2,1)S(1)}, bf16[17,16,128]{2,1,0:T(8,128)(2,1)S(1)}, bf16[7,128,128]{2,1,0:T(8,128)(2,1)S(1)}) custom-call(bf16[16,16,16,128]{3,2,1,0:T(8,128)(2,1)} %adj.3, f32[8,16,128]{2,1,0:T(8,128)} %logf.1, bf16[7,128,128]{2,1,0:T(8,128)(2,1)} %coupling_hbm.1), custom_call_target="tpu_custom_call" | custom-call | tf_op jit(solution)/shard_map/pack/pallas_call | solution.py:235
  1.9 0.0 copy-start.2
  1.9 0.7 %collective-permute-start = (bf16[18,16,128]{2,1,0:T(8,128)(2,1)S(1)}, bf16[18,16,128]{2,1,0:T(8,128)(2,1)S(1)}, u32[]{:S(2)}, u32[]{:S(2)}) collective-permute-start(bf16[18,16,128]{2,1,0:T(8,128)(2,1)S(1)} %get-tuple-element.14), channel_id=1, source_target_pairs={{16,32},{48,64},{80,96},{112,128},{144,160},{176,192},{208,224},{2... | collective-permute-start | bytes 221192 | tf_op jit(solution)/shard_map/ppermute | solution.py:26
  2.6 6.8 %collective-permute-start.1 = (bf16[18,16,128]{2,1,0:T(8,128)(2,1)S(1)}, bf16[18,16,128]{2,1,0:T(8,128)(2,1)S(1)}, u32[]{:S(2)}, u32[]{:S(2)}) collective-permute-start(bf16[18,16,128]{2,1,0:T(8,128)(2,1)S(1)} %get-tuple-element.15), channel_id=1, source_target_pairs={{0,16},{32,48},{64,80},{96,112},{128,144},{160,176},{192,208},{224... | collective-permute-start | bytes 221192 | tf_op jit(solution)/shard_map/ppermute | solution.py:26
  9.4 4.2 %collective-permute-start.2 = (bf16[17,16,128]{2,1,0:T(8,128)(2,1)S(1)}, bf16[17,16,128]{2,1,0:T(8,128)(2,1)S(1)}, u32[]{:S(2)}, u32[]{:S(2)}) collective-permute-start(bf16[17,16,128]{2,1,0:T(8,128)(2,1)S(1)} %get-tuple-element.16), channel_id=1, source_target_pairs={{1,2},{3,4},{5,6},{7,8},{9,10},{11,12},{13,14},{2,1},{4,3},{6,5},{... | collective-permute-start | bytes 208904 | tf_op jit(solution)/shard_map/ppermute | solution.py:26
  13.6 0.0 copy-start.3
  13.6 7.6 %collective-permute-start.3 = (bf16[17,16,128]{2,1,0:T(8,128)(2,1)S(1)}, bf16[17,16,128]{2,1,0:T(8,128)(2,1)S(1)}, u32[]{:S(2)}, u32[]{:S(2)}) collective-permute-start(bf16[17,16,128]{2,1,0:T(8,128)(2,1)S(1)} %get-tuple-element.17), channel_id=1, source_target_pairs={{0,1},{2,3},{4,5},{6,7},{8,9},{10,11},{12,13},{14,15},{1,0},{3,2},... | collective-permute-start | bytes 208904 | tf_op jit(solution)/shard_map/ppermute | solution.py:26
  21.3 0.0 copy-done
  21.3 0.0 copy-done.4
  21.3 0.0 copy-done.2
  21.3 0.0 copy-done.3
  21.3 0.3 local.1
  21.6 0.0 collective-permute-done.2.b_far
  21.7 0.5 %collective-permute-done.3.b_near = bf16[17,16,128]{2,1,0:T(8,128)(2,1)S(1)} collective-permute-done((bf16[17,16,128]{2,1,0:T(8,128)(2,1)S(1)}, bf16[17,16,128]{2,1,0:T(8,128)(2,1)S(1)}, u32[]{:S(2)}, u32[]{:S(2)}) %collective-permute-start.3) | collective-permute-done | bytes 69664 | tf_op jit(solution)/shard_map/ppermute | solution.py:26
  22.1 0.0 collective-permute-done.a_far
  22.2 0.0 collective-permute-done.1.a_near
  22.2 1.0 %message.1 = bf16[16,24,128]{2,1,0:T(8,128)(2,1)} custom-call(f32[256,128]{1,0:T(8,128)S(1)} %get-tuple-element.19.base, bf16[256,256]{1,0:T(8,128)(2,1)S(1)} %get-tuple-element.20.pick, f32[16,128]{1,0:T(8,128)S(1)} %get-tuple-element.21.ids, bf16[7,128,128]{2,1,0:T(8,128)(2,1)S(1)} %get-tuple-element.13.coupling, ...), custom_call_target="tpu_custom_call" | custom-call | flops 16777216 | bytes 1048576 | tf_op jit(solution)/shard_map/message/pallas_call | solution.py:270
  23.1 0.0 copy-start.1
  23.1 4.2 %all-to-all-start = ((bf16[16,24,128]{2,1,0:T(8,128)(2,1)}), bf16[16,24,128]{2,1,0:T(8,128)(2,1)S(1)}, u32[]{:S(2)}, u32[]{:S(2)}) async-start(bf16[16,24,128]{2,1,0:T(8,128)(2,1)} %message.1), calls=%async_computation | async-start | bytes 196608 | tf_op jit(solution)/shard_map/all_to_all | solution.py:284
  27.4 0.0 copy-done.1
  27.4 2.9 %update.1 = (bf16[16,16,16,128]{3,2,1,0:T(8,128)(2,1)}, f32[8,16,128]{2,1,0:T(8,128)S(1)}, f32[8,16,128]{2,1,0:T(8,128)S(1)}) custom-call(bf16[16,16,16,128]{3,2,1,0:T(8,128)(2,1)S(1)} %copy-done, bf16[7,128,128]{2,1,0:T(8,128)(2,1)S(1)} %get-tuple-element.13.coupling, f32[8,16,128]{2,1,0:T(8,128)S(1)} %copy-done.1, ...), custom_call_target="tpu_custom_call" | custom-call | flops 939524096 | bytes 4194304 | tf_op jit(solution)/shard_map/update/pallas_call | solution.py:286
  30.3 5.6 %all-to-all-done.got = bf16[16,24,128]{2,1,0:T(8,128)(2,1)S(1)} async-done(((bf16[16,24,128]{2,1,0:T(8,128)(2,1)}), bf16[16,24,128]{2,1,0:T(8,128)(2,1)S(1)}, u32[]{:S(2)}, u32[]{:S(2)}) %all-to-all-start) | async-done | bytes 98336 | tf_op jit(solution)/shard_map/all_to_all | solution.py:284
  35.9 0.8 %gradient.1 = f32[8,16,128]{2,1,0:T(8,128)} custom-call(bf16[16,24,128]{2,1,0:T(8,128)(2,1)S(1)} %all-to-all-done.got, f32[8,16,128]{2,1,0:T(8,128)S(1)} %get-tuple-element.22.prior, f32[8,16,128]{2,1,0:T(8,128)S(1)} %get-tuple-element.23.scale), custom_call_target="tpu_custom_call" | custom-call | flops 8388608 | bytes 524288 | tf_op jit(solution)/shard_map/gradient/pallas_call | solution.py:310
Async XLA Ops:
  0.6 20.6 %copy-start = (bf16[16,16,16,128]{3,2,1,0:T(8,128)(2,1)S(1)}, bf16[16,16,16,128]{3,2,1,0:T(8,128)(2,1)}, u32[]{:S(2)}) copy-start(bf16[16,16,16,128]{3,2,1,0:T(8,128)(2,1)} %adj.3) | copy-start | bytes 3145732
  0.6 20.6 %copy-start.4 = (s32[1,1,16]{2,1,0:T(1,128)S(1)}, s32[1,1,16]{2,1,0:T(1,128)}, u32[]{:S(2)}) copy-start(s32[1,1,16]{2,1,0:T(1,128)} %live.1) | copy-start | bytes 196
  1.9 19.4 %copy-start.2 = (s32[1,1,16,16]{3,2,1,0:T(8,128)S(1)}, s32[1,1,16,16]{3,2,1,0:T(8,128)}, u32[]{:S(2)}) copy-start(s32[1,1,16,16]{3,2,1,0:T(8,128)} %nodes.1) | copy-start | bytes 3076
  1.9 20.2 %collective-permute-start = (bf16[18,16,128]{2,1,0:T(8,128)(2,1)S(1)}, bf16[18,16,128]{2,1,0:T(8,128)(2,1)S(1)}, u32[]{:S(2)}, u32[]{:S(2)}) collective-permute-start(bf16[18,16,128]{2,1,0:T(8,128)(2,1)S(1)} %get-tuple-element.14), channel_id=1, source_target_pairs={{16,32},{48,64},{80,96},{112,128},{144,160},{176,192},{208,224},{2... | collective-permute-start | bytes 221192 | tf_op jit(solution)/shard_map/ppermute | solution.py:26
  2.6 19.6 %collective-permute-start.1 = (bf16[18,16,128]{2,1,0:T(8,128)(2,1)S(1)}, bf16[18,16,128]{2,1,0:T(8,128)(2,1)S(1)}, u32[]{:S(2)}, u32[]{:S(2)}) collective-permute-start(bf16[18,16,128]{2,1,0:T(8,128)(2,1)S(1)} %get-tuple-element.15), channel_id=1, source_target_pairs={{0,16},{32,48},{64,80},{96,112},{128,144},{160,176},{192,208},{224... | collective-permute-start | bytes 221192 | tf_op jit(solution)/shard_map/ppermute | solution.py:26
  9.4 12.3 %collective-permute-start.2 = (bf16[17,16,128]{2,1,0:T(8,128)(2,1)S(1)}, bf16[17,16,128]{2,1,0:T(8,128)(2,1)S(1)}, u32[]{:S(2)}, u32[]{:S(2)}) collective-permute-start(bf16[17,16,128]{2,1,0:T(8,128)(2,1)S(1)} %get-tuple-element.16), channel_id=1, source_target_pairs={{1,2},{3,4},{5,6},{7,8},{9,10},{11,12},{13,14},{2,1},{4,3},{6,5},{... | collective-permute-start | bytes 208904 | tf_op jit(solution)/shard_map/ppermute | solution.py:26
  13.6 7.7 %copy-start.3 = (s32[1,1,256]{2,1,0:T(1,128)S(1)}, s32[1,1,256]{2,1,0:T(1,128)}, u32[]{:S(2)}) copy-start(s32[1,1,256]{2,1,0:T(1,128)} %send.1) | copy-start | bytes 3076
  13.6 8.5 %collective-permute-start.3 = (bf16[17,16,128]{2,1,0:T(8,128)(2,1)S(1)}, bf16[17,16,128]{2,1,0:T(8,128)(2,1)S(1)}, u32[]{:S(2)}, u32[]{:S(2)}) collective-permute-start(bf16[17,16,128]{2,1,0:T(8,128)(2,1)S(1)} %get-tuple-element.17), channel_id=1, source_target_pairs={{0,1},{2,3},{4,5},{6,7},{8,9},{10,11},{12,13},{14,15},{1,0},{3,2},... | collective-permute-start | bytes 208904 | tf_op jit(solution)/shard_map/ppermute | solution.py:26
  23.1 4.3 %copy-start.1 = (f32[8,16,128]{2,1,0:T(8,128)S(1)}, f32[8,16,128]{2,1,0:T(8,128)}, u32[]{:S(2)}) copy-start(f32[8,16,128]{2,1,0:T(8,128)} %logf.1) | copy-start | bytes 196612
  23.1 12.8 %all-to-all-start = ((bf16[16,24,128]{2,1,0:T(8,128)(2,1)}), bf16[16,24,128]{2,1,0:T(8,128)(2,1)S(1)}, u32[]{:S(2)}, u32[]{:S(2)}) async-start(bf16[16,24,128]{2,1,0:T(8,128)(2,1)} %message.1), calls=%async_computation | async-start | bytes 196608 | tf_op jit(solution)/shard_map/all_to_all | solution.py:284

commit v6 on v5

--- a/solution.py
+++ b/solution.py
@@ -9,7 +9,7 @@
 BF16 = jnp.bfloat16
 VMEM = pl.BlockSpec(memory_space=pltpu.VMEM)
 HBM = pl.BlockSpec(memory_space=pltpu.HBM)
-MSG = 24
+MSG = 20
 
 
 def dot(a, b):
@@ -129,8 +129,9 @@
         return jnp.where(sub == 2, bottom[column:column + 1, :], rows)
 
     for o in range(owners):
-        out[o, 0:slots] = picked[o * slots:(o + 1) * slots]
-        out[o, slots:MSG] = jnp.where(o > here, extra(o, pb - 1), extra(o, 0)).astype(BF16)
+        out[o, 0:slots // 2] = picked[o * slots:(o + 1) * slots].reshape(slots // 2, 2, width)
+        rest = jnp.where(o > here, extra(o, pb - 1), extra(o, 0)).astype(BF16)
+        out[o, slots // 2:MSG // 2] = rest.reshape((MSG - slots) // 2, 2, width)
 
 
 def update_body(adj, coupling, logf, a_far, a_near, b_far, b_near, out, prior, scale,
@@ -199,23 +200,23 @@
 
 
 def gradient_body(got, prior, scale, out):
-    owners, _, width = got.shape
+    owners, _, _, width = got.shape
     pa, pb, _ = out.shape
     slots = 16
     per_row = width // slots
-    tail = got[:, slots:MSG, :].astype(F32)
+    tail = got[:, slots // 2:MSG // 2].reshape(owners, MSG - slots, width).astype(F32)
     listed = [jnp.sum(tail[k:k + per_row], axis=0)[0:1] for k in range(0, owners, per_row)]
     listed = jnp.concatenate(listed, axis=1)
     node = lax.broadcasted_iota(jnp.int32, (pa * pb, owners * slots), 0).astype(F32) + 1.0
     onehot = jnp.where(node == listed, 1.0, 0.0).astype(BF16)
-    blocks = got[:, 0:slots, :].reshape(owners * slots, width)
+    blocks = got[:, 0:slots // 2].reshape(owners * slots, width)
     misfit = dot(onehot, blocks).reshape(pa, pb, width)
     out[...] = scale[...] * misfit + prior[...]
     j = lax.axis_index("gy")
     for side, column in ((-1, 0), (1, pb - 1)):
         inside = jnp.logical_and(j + side >= 0, j + side < owners)
         source = jnp.clip(j + side, 0, owners - 1)
-        corners = jnp.where(inside, got[source, slots:MSG, :].astype(F32) * 0.08, 0.0)
+        corners = jnp.where(inside, got[source, slots // 2:MSG // 2].reshape(MSG - slots, width).astype(F32) * 0.08, 0.0)
         out[0, column:column + 1] += corners[1:2]
         out[pa - 1, column:column + 1] += corners[2:3]
 
@@ -247,8 +248,8 @@
         compiler_params=wire,
         name="pack",
     )(*map(in_hbm, (adjoint_trace, log_friction, coupling)))
+    a_near = swap(to_a_near, "gx", 0)
     a_far = swap(to_a_far, "gx", 1)
-    a_near = swap(to_a_near, "gx", 0)
     b_far = swap(to_b_far, "gy", 1)
     b_near = swap(to_b_near, "gy", 0)
 
@@ -269,7 +270,7 @@
 
     message = pl.pallas_call(
         message_body,
-        out_shape=shape((owners, MSG, width), BF16),
+        out_shape=shape((owners, MSG // 2, 2, width), BF16),
         in_specs=[VMEM] * 8,
         out_specs=VMEM,
         scratch_shapes=[

time: 37 us -> 36.7 us (level)
  no operation moved by 1% of the time
where the time goes in v6:
time: 36.7 us; the launch traced here: 36.4 us
  starting transfers between devices  23.6 us (64%)
  Pallas kernels  6.33 us (17%)
  waiting for transfers between devices  5.73 us (16%)
  between operations  0.76 us (2%)
    ppermute x4, starting transfers between devices, swap(): return lax.ppermute(block, axis, pairs + [(j, i) for i, j in pairs])  19.3 us
    all_to_all x1, waiting for transfers between devices, per_device(): lax.all_to_all(message, 'gy', split_axis=0, concat_axis=0, tiled=True)  5.23 us
    all_to_all x1, starting transfers between devices, per_device(): lax.all_to_all(message, 'gy', split_axis=0, concat_axis=0, tiled=True)  4.25 us
    pallas_call x1, Pallas kernels, per_device(): pl.pallas_call(update_body, out_shape=(shape(adjoint_trace.shape, BF16),...  2.94 us
    pallas_call x1, Pallas kernels, per_device(): pl.pallas_call(pack_body, out_shape=(shape((cb + 2, nl, width), BF16), sh...  1.24 us
    pallas_call x1, Pallas kernels, per_device(): pl.pallas_call(message_body, out_shape=shape((owners, MSG // 2, 2, width)...  0.99 us
    pallas_call x1, Pallas kernels, per_device(): pl.pallas_call(gradient_body, out_shape=shape(log_friction.shape, F32), i...  0.83 us
  transfers between devices with their start and end apart: 5, of which 2 were waited for; matrix products, arithmetic and copies ran while one was open for 0% of the time, Pallas kernels for 9%

profile of v6, /device:TPU:1, one launch (start us, length us, event | category | flops | bytes accessed | tf_op | source)
XLA Modules:
  0.0 36.4 jit_solution(10936280930623930452)
XLA Ops:
  0.6 0.0 copy-start
  0.6 0.0 copy-start.4
  0.6 1.2 %pack.1 = (bf16[18,16,128]{2,1,0:T(8,128)(2,1)S(1)}, bf16[18,16,128]{2,1,0:T(8,128)(2,1)S(1)}, bf16[17,16,128]{2,1,0:T(8,128)(2,1)S(1)}, bf16[17,16,128]{2,1,0:T(8,128)(2,1)S(1)}, bf16[7,128,128]{2,1,0:T(8,128)(2,1)S(1)}) custom-call(bf16[16,16,16,128]{3,2,1,0:T(8,128)(2,1)} %adj.3, f32[8,16,128]{2,1,0:T(8,128)} %logf.1, bf16[7,128,128]{2,1,0:T(8,128)(2,1)} %coupling_hbm.1), custom_call_target="tpu_custom_call" | custom-call | tf_op jit(solution)/shard_map/pack/pallas_call | solution.py:236
  1.9 0.0 copy-start.2
  1.9 0.7 %collective-permute-start = (bf16[18,16,128]{2,1,0:T(8,128)(2,1)S(1)}, bf16[18,16,128]{2,1,0:T(8,128)(2,1)S(1)}, u32[]{:S(2)}, u32[]{:S(2)}) collective-permute-start(bf16[18,16,128]{2,1,0:T(8,128)(2,1)S(1)} %get-tuple-element.14), channel_id=1, source_target_pairs={{16,32},{48,64},{80,96},{112,128},{144,160},{176,192},{208,224},{2... | collective-permute-start | bytes 221192 | tf_op jit(solution)/shard_map/ppermute | solution.py:26
  2.6 6.8 %collective-permute-start.1 = (bf16[18,16,128]{2,1,0:T(8,128)(2,1)S(1)}, bf16[18,16,128]{2,1,0:T(8,128)(2,1)S(1)}, u32[]{:S(2)}, u32[]{:S(2)}) collective-permute-start(bf16[18,16,128]{2,1,0:T(8,128)(2,1)S(1)} %get-tuple-element.15), channel_id=1, source_target_pairs={{0,16},{32,48},{64,80},{96,112},{128,144},{160,176},{192,208},{224... | collective-permute-start | bytes 221192 | tf_op jit(solution)/shard_map/ppermute | solution.py:26
  9.4 4.2 %collective-permute-start.2 = (bf16[17,16,128]{2,1,0:T(8,128)(2,1)S(1)}, bf16[17,16,128]{2,1,0:T(8,128)(2,1)S(1)}, u32[]{:S(2)}, u32[]{:S(2)}) collective-permute-start(bf16[17,16,128]{2,1,0:T(8,128)(2,1)S(1)} %get-tuple-element.16), channel_id=1, source_target_pairs={{1,2},{3,4},{5,6},{7,8},{9,10},{11,12},{13,14},{2,1},{4,3},{6,5},{... | collective-permute-start | bytes 208904 | tf_op jit(solution)/shard_map/ppermute | solution.py:26
  13.6 0.0 copy-start.3
  13.6 7.6 %collective-permute-start.3 = (bf16[17,16,128]{2,1,0:T(8,128)(2,1)S(1)}, bf16[17,16,128]{2,1,0:T(8,128)(2,1)S(1)}, u32[]{:S(2)}, u32[]{:S(2)}) collective-permute-start(bf16[17,16,128]{2,1,0:T(8,128)(2,1)S(1)} %get-tuple-element.17), channel_id=1, source_target_pairs={{0,1},{2,3},{4,5},{6,7},{8,9},{10,11},{12,13},{14,15},{1,0},{3,2},... | collective-permute-start | bytes 208904 | tf_op jit(solution)/shard_map/ppermute | solution.py:26
  21.3 0.0 copy-done
  21.3 0.0 copy-done.4
  21.3 0.0 copy-done.2
  21.3 0.0 copy-done.3
  21.3 0.3 local.1
  21.6 0.0 collective-permute-done.2.b_far
  21.7 0.5 %collective-permute-done.3.b_near = bf16[17,16,128]{2,1,0:T(8,128)(2,1)S(1)} collective-permute-done((bf16[17,16,128]{2,1,0:T(8,128)(2,1)S(1)}, bf16[17,16,128]{2,1,0:T(8,128)(2,1)S(1)}, u32[]{:S(2)}, u32[]{:S(2)}) %collective-permute-start.3) | collective-permute-done | bytes 69664 | tf_op jit(solution)/shard_map/ppermute | solution.py:26
  22.1 0.0 collective-permute-done.a_far
  22.2 0.0 collective-permute-done.1.a_near
  22.2 1.0 %message.1 = bf16[16,10,2,128]{3,2,1,0:T(2,128)(2,1)} custom-call(f32[256,128]{1,0:T(8,128)S(1)} %get-tuple-element.19.base, bf16[256,256]{1,0:T(8,128)(2,1)S(1)} %get-tuple-element.20.pick, f32[16,128]{1,0:T(8,128)S(1)} %get-tuple-element.21.ids, bf16[7,128,128]{2,1,0:T(8,128)(2,1)S(1)} %get-tuple-element.13.coupling, ...), custom_call_target="tpu_custom_call" | custom-call | flops 16777216 | bytes 1048576 | tf_op jit(solution)/shard_map/message/pallas_call | solution.py:271
  23.1 0.0 copy-start.1
  23.1 4.3 %all-to-all-start = ((bf16[16,10,2,128]{3,2,1,0:T(2,128)(2,1)}), bf16[16,10,2,128]{3,2,1,0:T(2,128)(2,1)S(1)}, u32[]{:S(2)}, u32[]{:S(2)}) async-start(bf16[16,10,2,128]{3,2,1,0:T(2,128)(2,1)} %message.1), calls=%async_computation | async-start | bytes 163840 | tf_op jit(solution)/shard_map/all_to_all | solution.py:285
  27.4 0.0 copy-done.1
  27.4 2.9 %update.1 = (bf16[16,16,16,128]{3,2,1,0:T(8,128)(2,1)}, f32[8,16,128]{2,1,0:T(8,128)S(1)}, f32[8,16,128]{2,1,0:T(8,128)S(1)}) custom-call(bf16[16,16,16,128]{3,2,1,0:T(8,128)(2,1)S(1)} %copy-done, bf16[7,128,128]{2,1,0:T(8,128)(2,1)S(1)} %get-tuple-element.13.coupling, f32[8,16,128]{2,1,0:T(8,128)S(1)} %copy-done.1, ...), custom_call_target="tpu_custom_call" | custom-call | flops 939524096 | bytes 4194304 | tf_op jit(solution)/shard_map/update/pallas_call | solution.py:287
  30.4 5.2 %all-to-all-done.got = bf16[16,10,2,128]{3,2,1,0:T(2,128)(2,1)S(1)} async-done(((bf16[16,10,2,128]{3,2,1,0:T(2,128)(2,1)}), bf16[16,10,2,128]{3,2,1,0:T(2,128)(2,1)S(1)}, u32[]{:S(2)}, u32[]{:S(2)}) %all-to-all-start) | async-done | bytes 81952 | tf_op jit(solution)/shard_map/all_to_all | solution.py:285
  35.6 0.8 %gradient.1 = f32[8,16,128]{2,1,0:T(8,128)} custom-call(bf16[16,10,2,128]{3,2,1,0:T(2,128)(2,1)S(1)} %all-to-all-done.got, f32[8,16,128]{2,1,0:T(8,128)S(1)} %get-tuple-element.22.prior, f32[8,16,128]{2,1,0:T(8,128)S(1)} %get-tuple-element.23.scale), custom_call_target="tpu_custom_call" | custom-call | flops 8388608 | bytes 524288 | tf_op jit(solution)/shard_map/gradient/pallas_call | solution.py:311
Async XLA Ops:
  0.6 20.6 %copy-start = (bf16[16,16,16,128]{3,2,1,0:T(8,128)(2,1)S(1)}, bf16[16,16,16,128]{3,2,1,0:T(8,128)(2,1)}, u32[]{:S(2)}) copy-start(bf16[16,16,16,128]{3,2,1,0:T(8,128)(2,1)} %adj.3) | copy-start | bytes 3145732
  0.6 20.6 %copy-start.4 = (s32[1,1,16]{2,1,0:T(1,128)S(1)}, s32[1,1,16]{2,1,0:T(1,128)}, u32[]{:S(2)}) copy-start(s32[1,1,16]{2,1,0:T(1,128)} %live.1) | copy-start | bytes 196
  1.9 19.4 %copy-start.2 = (s32[1,1,16,16]{3,2,1,0:T(8,128)S(1)}, s32[1,1,16,16]{3,2,1,0:T(8,128)}, u32[]{:S(2)}) copy-start(s32[1,1,16,16]{3,2,1,0:T(8,128)} %nodes.1) | copy-start | bytes 3076
  1.9 20.2 %collective-permute-start = (bf16[18,16,128]{2,1,0:T(8,128)(2,1)S(1)}, bf16[18,16,128]{2,1,0:T(8,128)(2,1)S(1)}, u32[]{:S(2)}, u32[]{:S(2)}) collective-permute-start(bf16[18,16,128]{2,1,0:T(8,128)(2,1)S(1)} %get-tuple-element.14), channel_id=1, source_target_pairs={{16,32},{48,64},{80,96},{112,128},{144,160},{176,192},{208,224},{2... | collective-permute-start | bytes 221192 | tf_op jit(solution)/shard_map/ppermute | solution.py:26
  2.6 19.6 %collective-permute-start.1 = (bf16[18,16,128]{2,1,0:T(8,128)(2,1)S(1)}, bf16[18,16,128]{2,1,0:T(8,128)(2,1)S(1)}, u32[]{:S(2)}, u32[]{:S(2)}) collective-permute-start(bf16[18,16,128]{2,1,0:T(8,128)(2,1)S(1)} %get-tuple-element.15), channel_id=1, source_target_pairs={{0,16},{32,48},{64,80},{96,112},{128,144},{160,176},{192,208},{224... | collective-permute-start | bytes 221192 | tf_op jit(solution)/shard_map/ppermute | solution.py:26
  9.4 12.3 %collective-permute-start.2 = (bf16[17,16,128]{2,1,0:T(8,128)(2,1)S(1)}, bf16[17,16,128]{2,1,0:T(8,128)(2,1)S(1)}, u32[]{:S(2)}, u32[]{:S(2)}) collective-permute-start(bf16[17,16,128]{2,1,0:T(8,128)(2,1)S(1)} %get-tuple-element.16), channel_id=1, source_target_pairs={{1,2},{3,4},{5,6},{7,8},{9,10},{11,12},{13,14},{2,1},{4,3},{6,5},{... | collective-permute-start | bytes 208904 | tf_op jit(solution)/shard_map/ppermute | solution.py:26
  13.6 7.7 %copy-start.3 = (s32[1,1,256]{2,1,0:T(1,128)S(1)}, s32[1,1,256]{2,1,0:T(1,128)}, u32[]{:S(2)}) copy-start(s32[1,1,256]{2,1,0:T(1,128)} %send.1) | copy-start | bytes 3076
  13.6 8.5 %collective-permute-start.3 = (bf16[17,16,128]{2,1,0:T(8,128)(2,1)S(1)}, bf16[17,16,128]{2,1,0:T(8,128)(2,1)S(1)}, u32[]{:S(2)}, u32[]{:S(2)}) collective-permute-start(bf16[17,16,128]{2,1,0:T(8,128)(2,1)S(1)} %get-tuple-element.17), channel_id=1, source_target_pairs={{0,1},{2,3},{4,5},{6,7},{8,9},{10,11},{12,13},{14,15},{1,0},{3,2},... | collective-permute-start | bytes 208904 | tf_op jit(solution)/shard_map/ppermute | solution.py:26
  23.1 4.3 %copy-start.1 = (f32[8,16,128]{2,1,0:T(8,128)S(1)}, f32[8,16,128]{2,1,0:T(8,128)}, u32[]{:S(2)}) copy-start(f32[8,16,128]{2,1,0:T(8,128)} %logf.1) | copy-start | bytes 196612
  23.1 12.4 %all-to-all-start = ((bf16[16,10,2,128]{3,2,1,0:T(2,128)(2,1)}), bf16[16,10,2,128]{3,2,1,0:T(2,128)(2,1)S(1)}, u32[]{:S(2)}, u32[]{:S(2)}) async-start(bf16[16,10,2,128]{3,2,1,0:T(2,128)(2,1)} %message.1), calls=%async_computation | async-start | bytes 163840 | tf_op jit(solution)/shard_map/all_to_all | solution.py:285

commit v7 on v6

--- a/solution.py
+++ b/solution.py
@@ -26,7 +26,7 @@
     return lax.ppermute(block, axis, pairs + [(j, i) for i, j in pairs])
 
 
-def pack_body(adj_hbm, logf_hbm, coupling_hbm, to_a_far, to_a_near, to_b_far, to_b_near, coupling,
+def pack_body(adj_hbm, logf_hbm, coupling_hbm, to_a_near, to_a_far, to_b_far, to_b_near, coupling,
               logf, sems):
     ca, cb = adj_hbm.shape[0], adj_hbm.shape[1]
     pa, pb, _ = logf.shape
@@ -92,7 +92,7 @@
     ids[...] = jnp.where(jnp.logical_and(mine, alive), listed, 0.0)
 
 
-def message_body(base, pick, ids, coupling, a_far, a_near, b_far, b_near, out, total, wide):
+def message_body(base, pick, ids, coupling, a_near, a_far, b_far, b_near, out, total, wide):
     faces, width = base.shape
     owners, slots = out.shape[0], faces // out.shape[0]
     cb = a_far.shape[0] - 2
@@ -134,7 +134,7 @@
         out[o, slots // 2:MSG // 2] = rest.reshape((MSG - slots) // 2, 2, width)
 
 
-def update_body(adj, coupling, logf, a_far, a_near, b_far, b_near, out, prior, scale,
+def update_body(adj, coupling, logf, a_near, a_far, b_far, b_near, out, prior, scale,
                 a_lo, a_hi, b_lo, b_hi, held, field, once, sems):
     ca, cb, nl, width = adj.shape
     rows = cb * nl
@@ -233,7 +233,7 @@
     shape = jax.ShapeDtypeStruct
     wire = pltpu.CompilerParams(vmem_limit_bytes=16 * 2**20)
 
-    to_a_far, to_a_near, to_b_far, to_b_near, blocks = pl.pallas_call(
+    to_a_near, to_a_far, to_b_far, to_b_near, blocks = pl.pallas_call(
         pack_body,
         out_shape=(
             shape((cb + 2, nl, width), BF16),
@@ -280,7 +280,7 @@
         compiler_params=wire,
         cost_estimate=cost(2 * faces * faces * width, 2**20),
         name="message",
-    )(base, pick, ids, blocks, a_far, a_near, b_far, b_near)
+    )(base, pick, ids, blocks, a_near, a_far, b_far, b_near)
 
     received = lax.all_to_all(message, "gy", split_axis=0, concat_axis=0, tiled=True)
 
@@ -306,7 +306,7 @@
         compiler_params=wire,
         cost_estimate=cost(2 * 7 * faces * nl * width * width, 4 * 2**20),
         name="update",
-    )(adjoint_trace, blocks, log_friction, a_far, a_near, b_far, b_near)
+    )(adjoint_trace, blocks, log_friction, a_near, a_far, b_far, b_near)
 
     gradient = pl.pallas_call(
         gradient_body,

time: 36.7 us -> 37.5 us (1.022)
  the two profiles are of different devices: /device:TPU:1 before, /device:TPU:17 now
where the time goes in v7:
time: 37.5 us; the launch traced here: 37.2 us
  starting transfers between devices  24.3 us (65%)
  Pallas kernels  6.33 us (17%)
  waiting for transfers between devices  5.73 us (15%)
  between operations  0.76 us (2%)
    ppermute x4, starting transfers between devices, swap(): return lax.ppermute(block, axis, pairs + [(j, i) for i, j in pairs])  20.1 us
    all_to_all x1, waiting for transfers between devices, per_device(): lax.all_to_all(message, 'gy', split_axis=0, concat_axis=0, tiled=True)  5.23 us
    all_to_all x1, starting transfers between devices, per_device(): lax.all_to_all(message, 'gy', split_axis=0, concat_axis=0, tiled=True)  4.25 us
    pallas_call x1, Pallas kernels, per_device(): pl.pallas_call(update_body, out_shape=(shape(adjoint_trace.shape, BF16),...  2.94 us
    pallas_call x1, Pallas kernels, per_device(): pl.pallas_call(pack_body, out_shape=(shape((cb + 2, nl, width), BF16), sh...  1.24 us
    pallas_call x1, Pallas kernels, per_device(): pl.pallas_call(message_body, out_shape=shape((owners, MSG // 2, 2, width)...  0.99 us
    pallas_call x1, Pallas kernels, per_device(): pl.pallas_call(gradient_body, out_shape=shape(log_friction.shape, F32), i...  0.83 us
  transfers between devices with their start and end apart: 5, of which 2 were waited for; matrix products, arithmetic and copies ran while one was open for 0% of the time, Pallas kernels for 9%

profile of v7, /device:TPU:17, one launch (start us, length us, event | category | flops | bytes accessed | tf_op | source)
XLA Modules:
  0.0 37.2 jit_solution(9313043946718856803)
XLA Ops:
  0.6 0.0 copy-start
  0.6 0.0 copy-start.4
  0.6 1.2 %pack.1 = (bf16[18,16,128]{2,1,0:T(8,128)(2,1)S(1)}, bf16[18,16,128]{2,1,0:T(8,128)(2,1)S(1)}, bf16[17,16,128]{2,1,0:T(8,128)(2,1)S(1)}, bf16[17,16,128]{2,1,0:T(8,128)(2,1)S(1)}, bf16[7,128,128]{2,1,0:T(8,128)(2,1)S(1)}) custom-call(bf16[16,16,16,128]{3,2,1,0:T(8,128)(2,1)} %adj.3, f32[8,16,128]{2,1,0:T(8,128)} %logf.1, bf16[7,128,128]{2,1,0:T(8,128)(2,1)} %coupling_hbm.1), custom_call_target="tpu_custom_call" | custom-call | tf_op jit(solution)/shard_map/pack/pallas_call | solution.py:236
  1.9 0.0 copy-start.2
  1.9 1.9 %collective-permute-start = (bf16[18,16,128]{2,1,0:T(8,128)(2,1)S(1)}, bf16[18,16,128]{2,1,0:T(8,128)(2,1)S(1)}, u32[]{:S(2)}, u32[]{:S(2)}) collective-permute-start(bf16[18,16,128]{2,1,0:T(8,128)(2,1)S(1)} %get-tuple-element.14), channel_id=1, source_target_pairs={{0,16},{32,48},{64,80},{96,112},{128,144},{160,176},{192,208},{224... | collective-permute-start | bytes 221192 | tf_op jit(solution)/shard_map/ppermute | solution.py:26
  3.8 4.7 %collective-permute-start.1 = (bf16[18,16,128]{2,1,0:T(8,128)(2,1)S(1)}, bf16[18,16,128]{2,1,0:T(8,128)(2,1)S(1)}, u32[]{:S(2)}, u32[]{:S(2)}) collective-permute-start(bf16[18,16,128]{2,1,0:T(8,128)(2,1)S(1)} %get-tuple-element.15), channel_id=1, source_target_pairs={{16,32},{48,64},{80,96},{112,128},{144,160},{176,192},{208,224},{2... | collective-permute-start | bytes 221192 | tf_op jit(solution)/shard_map/ppermute | solution.py:26
  8.6 4.2 %collective-permute-start.2 = (bf16[17,16,128]{2,1,0:T(8,128)(2,1)S(1)}, bf16[17,16,128]{2,1,0:T(8,128)(2,1)S(1)}, u32[]{:S(2)}, u32[]{:S(2)}) collective-permute-start(bf16[17,16,128]{2,1,0:T(8,128)(2,1)S(1)} %get-tuple-element.16), channel_id=1, source_target_pairs={{1,2},{3,4},{5,6},{7,8},{9,10},{11,12},{13,14},{2,1},{4,3},{6,5},{... | collective-permute-start | bytes 208904 | tf_op jit(solution)/shard_map/ppermute | solution.py:26
  12.8 0.0 copy-start.3
  12.8 9.2 %collective-permute-start.3 = (bf16[17,16,128]{2,1,0:T(8,128)(2,1)S(1)}, bf16[17,16,128]{2,1,0:T(8,128)(2,1)S(1)}, u32[]{:S(2)}, u32[]{:S(2)}) collective-permute-start(bf16[17,16,128]{2,1,0:T(8,128)(2,1)S(1)} %get-tuple-element.17), channel_id=1, source_target_pairs={{0,1},{2,3},{4,5},{6,7},{8,9},{10,11},{12,13},{14,15},{1,0},{3,2},... | collective-permute-start | bytes 208904 | tf_op jit(solution)/shard_map/ppermute | solution.py:26
  22.0 0.0 copy-done
  22.0 0.0 copy-done.4
  22.0 0.0 copy-done.2
  22.0 0.0 copy-done.3
  22.1 0.3 local.1
  22.4 0.0 collective-permute-done.2.b_far
  22.4 0.5 %collective-permute-done.3.b_near = bf16[17,16,128]{2,1,0:T(8,128)(2,1)S(1)} collective-permute-done((bf16[17,16,128]{2,1,0:T(8,128)(2,1)S(1)}, bf16[17,16,128]{2,1,0:T(8,128)(2,1)S(1)}, u32[]{:S(2)}, u32[]{:S(2)}) %collective-permute-start.3) | collective-permute-done | bytes 69664 | tf_op jit(solution)/shard_map/ppermute | solution.py:26
  22.9 0.0 collective-permute-done.a_near
  22.9 0.0 collective-permute-done.1.a_far
  22.9 1.0 %message.1 = bf16[16,10,2,128]{3,2,1,0:T(2,128)(2,1)} custom-call(f32[256,128]{1,0:T(8,128)S(1)} %get-tuple-element.19.base, bf16[256,256]{1,0:T(8,128)(2,1)S(1)} %get-tuple-element.20.pick, f32[16,128]{1,0:T(8,128)S(1)} %get-tuple-element.21.ids, bf16[7,128,128]{2,1,0:T(8,128)(2,1)S(1)} %get-tuple-element.13.coupling, ...), custom_call_target="tpu_custom_call" | custom-call | flops 16777216 | bytes 1048576 | tf_op jit(solution)/shard_map/message/pallas_call | solution.py:271
  23.9 0.0 copy-start.1
  23.9 4.2 %all-to-all-start = ((bf16[16,10,2,128]{3,2,1,0:T(2,128)(2,1)}), bf16[16,10,2,128]{3,2,1,0:T(2,128)(2,1)S(1)}, u32[]{:S(2)}, u32[]{:S(2)}) async-start(bf16[16,10,2,128]{3,2,1,0:T(2,128)(2,1)} %message.1), calls=%async_computation | async-start | bytes 163840 | tf_op jit(solution)/shard_map/all_to_all | solution.py:285
  28.1 0.0 copy-done.1
  28.2 2.9 %update.1 = (bf16[16,16,16,128]{3,2,1,0:T(8,128)(2,1)}, f32[8,16,128]{2,1,0:T(8,128)S(1)}, f32[8,16,128]{2,1,0:T(8,128)S(1)}) custom-call(bf16[16,16,16,128]{3,2,1,0:T(8,128)(2,1)S(1)} %copy-done, bf16[7,128,128]{2,1,0:T(8,128)(2,1)S(1)} %get-tuple-element.13.coupling, f32[8,16,128]{2,1,0:T(8,128)S(1)} %copy-done.1, ...), custom_call_target="tpu_custom_call" | custom-call | flops 939524096 | bytes 4194304 | tf_op jit(solution)/shard_map/update/pallas_call | solution.py:287
  31.1 5.2 %all-to-all-done.got = bf16[16,10,2,128]{3,2,1,0:T(2,128)(2,1)S(1)} async-done(((bf16[16,10,2,128]{3,2,1,0:T(2,128)(2,1)}), bf16[16,10,2,128]{3,2,1,0:T(2,128)(2,1)S(1)}, u32[]{:S(2)}, u32[]{:S(2)}) %all-to-all-start) | async-done | bytes 81952 | tf_op jit(solution)/shard_map/all_to_all | solution.py:285
  36.3 0.8 %gradient.1 = f32[8,16,128]{2,1,0:T(8,128)} custom-call(bf16[16,10,2,128]{3,2,1,0:T(2,128)(2,1)S(1)} %all-to-all-done.got, f32[8,16,128]{2,1,0:T(8,128)S(1)} %get-tuple-element.22.prior, f32[8,16,128]{2,1,0:T(8,128)S(1)} %get-tuple-element.23.scale), custom_call_target="tpu_custom_call" | custom-call | flops 8388608 | bytes 524288 | tf_op jit(solution)/shard_map/gradient/pallas_call | solution.py:311
Async XLA Ops:
  0.6 21.4 %copy-start = (bf16[16,16,16,128]{3,2,1,0:T(8,128)(2,1)S(1)}, bf16[16,16,16,128]{3,2,1,0:T(8,128)(2,1)}, u32[]{:S(2)}) copy-start(bf16[16,16,16,128]{3,2,1,0:T(8,128)(2,1)} %adj.3) | copy-start | bytes 3145732
  0.6 21.4 %copy-start.4 = (s32[1,1,16]{2,1,0:T(1,128)S(1)}, s32[1,1,16]{2,1,0:T(1,128)}, u32[]{:S(2)}) copy-start(s32[1,1,16]{2,1,0:T(1,128)} %live.1) | copy-start | bytes 196
  1.9 20.1 %copy-start.2 = (s32[1,1,16,16]{3,2,1,0:T(8,128)S(1)}, s32[1,1,16,16]{3,2,1,0:T(8,128)}, u32[]{:S(2)}) copy-start(s32[1,1,16,16]{3,2,1,0:T(8,128)} %nodes.1) | copy-start | bytes 3076
  1.9 21.0 %collective-permute-start = (bf16[18,16,128]{2,1,0:T(8,128)(2,1)S(1)}, bf16[18,16,128]{2,1,0:T(8,128)(2,1)S(1)}, u32[]{:S(2)}, u32[]{:S(2)}) collective-permute-start(bf16[18,16,128]{2,1,0:T(8,128)(2,1)S(1)} %get-tuple-element.14), channel_id=1, source_target_pairs={{0,16},{32,48},{64,80},{96,112},{128,144},{160,176},{192,208},{224... | collective-permute-start | bytes 221192 | tf_op jit(solution)/shard_map/ppermute | solution.py:26
  3.8 19.1 %collective-permute-start.1 = (bf16[18,16,128]{2,1,0:T(8,128)(2,1)S(1)}, bf16[18,16,128]{2,1,0:T(8,128)(2,1)S(1)}, u32[]{:S(2)}, u32[]{:S(2)}) collective-permute-start(bf16[18,16,128]{2,1,0:T(8,128)(2,1)S(1)} %get-tuple-element.15), channel_id=1, source_target_pairs={{16,32},{48,64},{80,96},{112,128},{144,160},{176,192},{208,224},{2... | collective-permute-start | bytes 221192 | tf_op jit(solution)/shard_map/ppermute | solution.py:26
  8.6 13.8 %collective-permute-start.2 = (bf16[17,16,128]{2,1,0:T(8,128)(2,1)S(1)}, bf16[17,16,128]{2,1,0:T(8,128)(2,1)S(1)}, u32[]{:S(2)}, u32[]{:S(2)}) collective-permute-start(bf16[17,16,128]{2,1,0:T(8,128)(2,1)S(1)} %get-tuple-element.16), channel_id=1, source_target_pairs={{1,2},{3,4},{5,6},{7,8},{9,10},{11,12},{13,14},{2,1},{4,3},{6,5},{... | collective-permute-start | bytes 208904 | tf_op jit(solution)/shard_map/ppermute | solution.py:26
  12.8 9.2 %copy-start.3 = (s32[1,1,256]{2,1,0:T(1,128)S(1)}, s32[1,1,256]{2,1,0:T(1,128)}, u32[]{:S(2)}) copy-start(s32[1,1,256]{2,1,0:T(1,128)} %send.1) | copy-start | bytes 3076
  12.8 10.1 %collective-permute-start.3 = (bf16[17,16,128]{2,1,0:T(8,128)(2,1)S(1)}, bf16[17,16,128]{2,1,0:T(8,128)(2,1)S(1)}, u32[]{:S(2)}, u32[]{:S(2)}) collective-permute-start(bf16[17,16,128]{2,1,0:T(8,128)(2,1)S(1)} %get-tuple-element.17), channel_id=1, source_target_pairs={{0,1},{2,3},{4,5},{6,7},{8,9},{10,11},{12,13},{14,15},{1,0},{3,2},... | collective-permute-start | bytes 208904 | tf_op jit(solution)/shard_map/ppermute | solution.py:26
  23.9 4.3 %copy-start.1 = (f32[8,16,128]{2,1,0:T(8,128)S(1)}, f32[8,16,128]{2,1,0:T(8,128)}, u32[]{:S(2)}) copy-start(f32[8,16,128]{2,1,0:T(8,128)} %logf.1) | copy-start | bytes 196612
  23.9 12.4 %all-to-all-start = ((bf16[16,10,2,128]{3,2,1,0:T(2,128)(2,1)}), bf16[16,10,2,128]{3,2,1,0:T(2,128)(2,1)S(1)}, u32[]{:S(2)}, u32[]{:S(2)}) async-start(bf16[16,10,2,128]{3,2,1,0:T(2,128)(2,1)} %message.1), calls=%async_computation | async-start | bytes 163840 | tf_op jit(solution)/shard_map/all_to_all | solution.py:285

commit v8 on v6

--- a/solution.py
+++ b/solution.py
@@ -26,8 +26,7 @@
     return lax.ppermute(block, axis, pairs + [(j, i) for i, j in pairs])
 
 
-def pack_body(adj_hbm, logf_hbm, coupling_hbm, to_a_far, to_a_near, to_b_far, to_b_near, coupling,
-              logf, sems):
+def pack_body(adj_hbm, logf_hbm, to_a_far, to_a_near, to_b_far, to_b_near, logf, sems):
     ca, cb = adj_hbm.shape[0], adj_hbm.shape[1]
     pa, pb, _ = logf.shape
     odd_a, odd_b = lax.axis_index("gx") % 2, lax.axis_index("gy") % 2
@@ -42,7 +41,6 @@
                 (adj_hbm.at[near_a], to_a_near.at[pl.ds(0, cb)]),
                 (adj_hbm.at[:, cb - 1 - near_b], to_b_far.at[pl.ds(0, ca)]),
                 (adj_hbm.at[:, near_b], to_b_near.at[pl.ds(0, ca)]),
-                (coupling_hbm, coupling),
             )
         )
     ]
@@ -60,22 +58,13 @@
         copy.wait()
 
 
-def local_body(adj, coupling, send, live, nodes, base, pick, ids, wide):
+def local_body(adj, coupling_hbm, send, live, nodes, base, pick, ids, coupling, wide, sem):
+    fetch = pltpu.make_async_copy(coupling_hbm, coupling, sem)
+    fetch.start()
     ca, cb, nl, width = adj.shape
     faces = ca * cb
     for a in range(ca):
         wide[a * cb * 8:(a + 1) * cb * 8] = adj[a, :, 0:8, :].astype(F32).reshape(cb * 8, width)
-    low = wide[pl.ds(0, faces, stride=8), :].astype(BF16)
-    above = wide[pl.ds(1, faces, stride=8), :].astype(BF16)
-    total = dot(low, coupling[0]) + dot(above, coupling[2])
-    zeros = jnp.zeros((cb, width), F32)
-    total = total + jnp.concatenate([zeros, dot(low[:faces - cb], coupling[3])], axis=0)
-    total = total + jnp.concatenate([dot(low[cb:], coupling[4]), zeros], axis=0)
-    column = lax.broadcasted_iota(jnp.int32, (faces, width), 0) % cb
-    before = pltpu.roll(dot(low, coupling[5]), 1, 0)
-    after = pltpu.roll(dot(low, coupling[6]), faces - 1, 0)
-    total = total + jnp.where(column > 0, before, 0.0) + jnp.where(column < cb - 1, after, 0.0)
-    base[...] = total
     face = lax.broadcasted_iota(jnp.int32, (faces, faces), 0)
     pick[...] = jnp.where(send[0] == face, 1.0, 0.0).T.astype(BF16)
     owners, slots = nodes.shape[2], nodes.shape[3]
@@ -90,6 +79,18 @@
     mine = lane // slots == lax.axis_index("gy") % (width // slots)
     alive = (lane % slots).astype(F32) < counts
     ids[...] = jnp.where(jnp.logical_and(mine, alive), listed, 0.0)
+    fetch.wait()
+    low = wide[pl.ds(0, faces, stride=8), :].astype(BF16)
+    above = wide[pl.ds(1, faces, stride=8), :].astype(BF16)
+    total = dot(low, coupling[0]) + dot(above, coupling[2])
+    zeros = jnp.zeros((cb, width), F32)
+    total = total + jnp.concatenate([zeros, dot(low[:faces - cb], coupling[3])], axis=0)
+    total = total + jnp.concatenate([dot(low[cb:], coupling[4]), zeros], axis=0)
+    column = lax.broadcasted_iota(jnp.int32, (faces, width), 0) % cb
+    before = pltpu.roll(dot(low, coupling[5]), 1, 0)
+    after = pltpu.roll(dot(low, coupling[6]), faces - 1, 0)
+    total = total + jnp.where(column > 0, before, 0.0) + jnp.where(column < cb - 1, after, 0.0)
+    base[...] = total
 
 
 def message_body(base, pick, ids, coupling, a_far, a_near, b_far, b_near, out, total, wide):
@@ -233,40 +234,40 @@
     shape = jax.ShapeDtypeStruct
     wire = pltpu.CompilerParams(vmem_limit_bytes=16 * 2**20)
 
-    to_a_far, to_a_near, to_b_far, to_b_near, blocks = pl.pallas_call(
+    to_a_far, to_a_near, to_b_far, to_b_near = pl.pallas_call(
         pack_body,
         out_shape=(
             shape((cb + 2, nl, width), BF16),
             shape((cb + 2, nl, width), BF16),
             shape((ca + 1, nl, width), BF16),
             shape((ca + 1, nl, width), BF16),
-            shape(coupling.shape, BF16),
         ),
-        in_specs=[HBM] * 3,
-        out_specs=(VMEM,) * 5,
-        scratch_shapes=[pltpu.VMEM(log_friction.shape, F32), pltpu.SemaphoreType.DMA((6,))],
+        in_specs=[HBM] * 2,
+        out_specs=(VMEM,) * 4,
+        scratch_shapes=[pltpu.VMEM(log_friction.shape, F32), pltpu.SemaphoreType.DMA((5,))],
         compiler_params=wire,
         name="pack",
-    )(*map(in_hbm, (adjoint_trace, log_friction, coupling)))
+    )(in_hbm(adjoint_trace), in_hbm(log_friction))
     a_near = swap(to_a_near, "gx", 0)
     a_far = swap(to_a_far, "gx", 1)
     b_far = swap(to_b_far, "gy", 1)
     b_near = swap(to_b_near, "gy", 0)
 
-    base, pick, ids = pl.pallas_call(
+    base, pick, ids, blocks = pl.pallas_call(
         local_body,
         out_shape=(
             shape((faces, width), F32),
             shape((faces, faces), BF16),
             shape((owners, width), F32),
+            shape(coupling.shape, BF16),
         ),
-        in_specs=[VMEM] * 5,
-        out_specs=(VMEM,) * 3,
-        scratch_shapes=[pltpu.VMEM((faces * 8, width), F32)],
+        in_specs=[VMEM, HBM] + [VMEM] * 3,
+        out_specs=(VMEM,) * 4,
+        scratch_shapes=[pltpu.VMEM((faces * 8, width), F32), pltpu.SemaphoreType.DMA],
         compiler_params=wire,
         cost_estimate=cost(2 * 6 * faces * width * width, 2 * 2**20),
         name="local",
-    )(adjoint_trace, blocks, send_column, live_count, target_node)
+    )(adjoint_trace, in_hbm(coupling), send_column, live_count, target_node)
 
     message = pl.pallas_call(
         message_body,

time: 36.7 us -> 36.6 us (level)
  Pallas kernels: 6.33 us -> 7.1 us
  starting transfers between devices: 23.6 us -> 23.1 us
  waiting for transfers between devices: 5.73 us -> 5.24 us
    pallas_call x1, Pallas kernels: 0.33 us -> 1.24 us  [per_device(): pl.pallas_call(local_body, out_shape=(shape((faces, width), F32), shape((...]
    ppermute x4, waiting for transfers between devices: 0.5 us -> 0.01 us  [swap(): return lax.ppermute(block, axis, pairs + [(j, i) for i, j in pairs])]
    all_to_all x1, starting transfers between devices: 4.25 us -> 3.8 us  [per_device(): lax.all_to_all(message, 'gy', split_axis=0, concat_axis=0, tiled=True)]
  transfers between devices with their start and end apart: 5 -> 5, of which waited for: 2 -> 1; matrix products, arithmetic and copies ran while one was open for 0% -> 0% of each run, Pallas kernels for 9% -> 12%
where the time goes in v8:
time: 36.6 us; the launch traced here: 36.3 us
  starting transfers between devices  23.1 us (63%)
  Pallas kernels  7.1 us (19%)
  waiting for transfers between devices  5.24 us (14%)
  between operations  0.78 us (2%)
    ppermute x4, starting transfers between devices, swap(): return lax.ppermute(block, axis, pairs + [(j, i) for i, j in pairs])  19.3 us
    all_to_all x1, waiting for transfers between devices, per_device(): lax.all_to_all(message, 'gy', split_axis=0, concat_axis=0, tiled=True)  5.23 us
    all_to_all x1, starting transfers between devices, per_device(): lax.all_to_all(message, 'gy', split_axis=0, concat_axis=0, tiled=True)  3.8 us
    pallas_call x1, Pallas kernels, per_device(): pl.pallas_call(update_body, out_shape=(shape(adjoint_trace.shape, BF16),...  2.94 us
    pallas_call x1, Pallas kernels, per_device(): pl.pallas_call(local_body, out_shape=(shape((faces, width), F32), shape((...  1.24 us
    pallas_call x1, Pallas kernels, per_device(): pl.pallas_call(pack_body, out_shape=(shape((cb + 2, nl, width), BF16), sh...  1.1 us
    pallas_call x1, Pallas kernels, per_device(): pl.pallas_call(message_body, out_shape=shape((owners, MSG // 2, 2, width)...  0.99 us
    pallas_call x1, Pallas kernels, per_device(): pl.pallas_call(gradient_body, out_shape=shape(log_friction.shape, F32), i...  0.83 us
  transfers between devices with their start and end apart: 5, of which 1 were waited for; matrix products, arithmetic and copies ran while one was open for 0% of the time, Pallas kernels for 12%

profile of v8, /device:TPU:1, one launch (start us, length us, event | category | flops | bytes accessed | tf_op | source)
XLA Modules:
  0.0 36.3 jit_solution(5333374760951007563)
XLA Ops:
  0.6 0.0 copy-start
  0.6 0.0 copy-start.2
  0.6 1.1 %pack.1 = (bf16[18,16,128]{2,1,0:T(8,128)(2,1)S(1)}, bf16[18,16,128]{2,1,0:T(8,128)(2,1)S(1)}, bf16[17,16,128]{2,1,0:T(8,128)(2,1)S(1)}, bf16[17,16,128]{2,1,0:T(8,128)(2,1)S(1)}) custom-call(bf16[16,16,16,128]{3,2,1,0:T(8,128)(2,1)} %adj.3, f32[8,16,128]{2,1,0:T(8,128)} %logf.1), custom_call_target="tpu_custom_call" | custom-call | tf_op jit(solution)/shard_map/pack/pallas_call | solution.py:237
  1.8 0.7 %collective-permute-start = (bf16[18,16,128]{2,1,0:T(8,128)(2,1)S(1)}, bf16[18,16,128]{2,1,0:T(8,128)(2,1)S(1)}, u32[]{:S(2)}, u32[]{:S(2)}) collective-permute-start(bf16[18,16,128]{2,1,0:T(8,128)(2,1)S(1)} %get-tuple-element.14), channel_id=1, source_target_pairs={{16,32},{48,64},{80,96},{112,128},{144,160},{176,192},{208,224},{2... | collective-permute-start | bytes 221192 | tf_op jit(solution)/shard_map/ppermute | solution.py:26
  2.4 6.8 %collective-permute-start.1 = (bf16[18,16,128]{2,1,0:T(8,128)(2,1)S(1)}, bf16[18,16,128]{2,1,0:T(8,128)(2,1)S(1)}, u32[]{:S(2)}, u32[]{:S(2)}) collective-permute-start(bf16[18,16,128]{2,1,0:T(8,128)(2,1)S(1)} %get-tuple-element.15), channel_id=1, source_target_pairs={{0,16},{32,48},{64,80},{96,112},{128,144},{160,176},{192,208},{224... | collective-permute-start | bytes 221192 | tf_op jit(solution)/shard_map/ppermute | solution.py:26
  9.2 0.0 copy-start.3
  9.2 0.0 copy-start.4
  9.3 4.2 %collective-permute-start.2 = (bf16[17,16,128]{2,1,0:T(8,128)(2,1)S(1)}, bf16[17,16,128]{2,1,0:T(8,128)(2,1)S(1)}, u32[]{:S(2)}, u32[]{:S(2)}) collective-permute-start(bf16[17,16,128]{2,1,0:T(8,128)(2,1)S(1)} %get-tuple-element.16), channel_id=1, source_target_pairs={{1,2},{3,4},{5,6},{7,8},{9,10},{11,12},{13,14},{2,1},{4,3},{6,5},{... | collective-permute-start | bytes 208904 | tf_op jit(solution)/shard_map/ppermute | solution.py:26
  13.5 7.6 %collective-permute-start.3 = (bf16[17,16,128]{2,1,0:T(8,128)(2,1)S(1)}, bf16[17,16,128]{2,1,0:T(8,128)(2,1)S(1)}, u32[]{:S(2)}, u32[]{:S(2)}) collective-permute-start(bf16[17,16,128]{2,1,0:T(8,128)(2,1)S(1)} %get-tuple-element.17), channel_id=1, source_target_pairs={{0,1},{2,3},{4,5},{6,7},{8,9},{10,11},{12,13},{14,15},{1,0},{3,2},... | collective-permute-start | bytes 208904 | tf_op jit(solution)/shard_map/ppermute | solution.py:26
  21.1 0.0 copy-done
  21.1 0.0 copy-done.2
  21.1 0.0 copy-done.3
  21.2 0.0 copy-done.4
  21.2 1.2 %local.1 = (f32[256,128]{1,0:T(8,128)S(1)}, bf16[256,256]{1,0:T(8,128)(2,1)S(1)}, f32[16,128]{1,0:T(8,128)S(1)}, bf16[7,128,128]{2,1,0:T(8,128)(2,1)S(1)}) custom-call(bf16[16,16,16,128]{3,2,1,0:T(8,128)(2,1)S(1)} %copy-done, bf16[7,128,128]{2,1,0:T(8,128)(2,1)} %coupling_hbm.1, s32[1,1,256]{2,1,0:T(1,128)S(1)} %copy-done.3, s32[1,1,16]{2,1,0:T(1,128)S(1)} %copy-done.4, ...), custom_call_target="tpu_custom_call" | custom-call | flops 50331648 | bytes 2097152 | tf_op jit(solution)/shard_map/local/pallas_call | solution.py:256
  22.4 0.0 collective-permute-done.2.b_far
  22.4 0.0 collective-permute-done.3.b_near
  22.4 0.0 collective-permute-done.a_far
  22.4 0.0 collective-permute-done.1.a_near
  22.5 1.0 %message.1 = bf16[16,10,2,128]{3,2,1,0:T(2,128)(2,1)} custom-call(f32[256,128]{1,0:T(8,128)S(1)} %get-tuple-element.19.base, bf16[256,256]{1,0:T(8,128)(2,1)S(1)} %get-tuple-element.20.pick, f32[16,128]{1,0:T(8,128)S(1)} %get-tuple-element.21.ids, bf16[7,128,128]{2,1,0:T(8,128)(2,1)S(1)} %get-tuple-element.13.coupling, ...), custom_call_target="tpu_custom_call" | custom-call | flops 16777216 | bytes 1048576 | tf_op jit(solution)/shard_map/message/pallas_call | solution.py:272
  23.4 0.0 copy-start.1
  23.4 3.8 %all-to-all-start = ((bf16[16,10,2,128]{3,2,1,0:T(2,128)(2,1)}), bf16[16,10,2,128]{3,2,1,0:T(2,128)(2,1)S(1)}, u32[]{:S(2)}, u32[]{:S(2)}) async-start(bf16[16,10,2,128]{3,2,1,0:T(2,128)(2,1)} %message.1), calls=%async_computation | async-start | bytes 163840 | tf_op jit(solution)/shard_map/all_to_all | solution.py:286
  27.2 0.0 copy-done.1
  27.3 2.9 %update.1 = (bf16[16,16,16,128]{3,2,1,0:T(8,128)(2,1)}, f32[8,16,128]{2,1,0:T(8,128)S(1)}, f32[8,16,128]{2,1,0:T(8,128)S(1)}) custom-call(bf16[16,16,16,128]{3,2,1,0:T(8,128)(2,1)S(1)} %copy-done, bf16[7,128,128]{2,1,0:T(8,128)(2,1)S(1)} %get-tuple-element.13.coupling, f32[8,16,128]{2,1,0:T(8,128)S(1)} %copy-done.1, ...), custom_call_target="tpu_custom_call" | custom-call | flops 939524096 | bytes 4194304 | tf_op jit(solution)/shard_map/update/pallas_call | solution.py:288
  30.2 5.2 %all-to-all-done.got = bf16[16,10,2,128]{3,2,1,0:T(2,128)(2,1)S(1)} async-done(((bf16[16,10,2,128]{3,2,1,0:T(2,128)(2,1)}), bf16[16,10,2,128]{3,2,1,0:T(2,128)(2,1)S(1)}, u32[]{:S(2)}, u32[]{:S(2)}) %all-to-all-start) | async-done | bytes 81952 | tf_op jit(solution)/shard_map/all_to_all | solution.py:286
  35.4 0.8 %gradient.1 = f32[8,16,128]{2,1,0:T(8,128)} custom-call(bf16[16,10,2,128]{3,2,1,0:T(2,128)(2,1)S(1)} %all-to-all-done.got, f32[8,16,128]{2,1,0:T(8,128)S(1)} %get-tuple-element.22.prior, f32[8,16,128]{2,1,0:T(8,128)S(1)} %get-tuple-element.23.scale), custom_call_target="tpu_custom_call" | custom-call | flops 8388608 | bytes 524288 | tf_op jit(solution)/shard_map/gradient/pallas_call | solution.py:312
Async XLA Ops:
  0.6 20.5 %copy-start = (bf16[16,16,16,128]{3,2,1,0:T(8,128)(2,1)S(1)}, bf16[16,16,16,128]{3,2,1,0:T(8,128)(2,1)}, u32[]{:S(2)}) copy-start(bf16[16,16,16,128]{3,2,1,0:T(8,128)(2,1)} %adj.3) | copy-start | bytes 3145732
  0.6 20.5 %copy-start.2 = (s32[1,1,16,16]{3,2,1,0:T(8,128)S(1)}, s32[1,1,16,16]{3,2,1,0:T(8,128)}, u32[]{:S(2)}) copy-start(s32[1,1,16,16]{3,2,1,0:T(8,128)} %nodes.1) | copy-start | bytes 3076
  1.8 20.7 %collective-permute-start = (bf16[18,16,128]{2,1,0:T(8,128)(2,1)S(1)}, bf16[18,16,128]{2,1,0:T(8,128)(2,1)S(1)}, u32[]{:S(2)}, u32[]{:S(2)}) collective-permute-start(bf16[18,16,128]{2,1,0:T(8,128)(2,1)S(1)} %get-tuple-element.14), channel_id=1, source_target_pairs={{16,32},{48,64},{80,96},{112,128},{144,160},{176,192},{208,224},{2... | collective-permute-start | bytes 221192 | tf_op jit(solution)/shard_map/ppermute | solution.py:26
  2.4 20.0 %collective-permute-start.1 = (bf16[18,16,128]{2,1,0:T(8,128)(2,1)S(1)}, bf16[18,16,128]{2,1,0:T(8,128)(2,1)S(1)}, u32[]{:S(2)}, u32[]{:S(2)}) collective-permute-start(bf16[18,16,128]{2,1,0:T(8,128)(2,1)S(1)} %get-tuple-element.15), channel_id=1, source_target_pairs={{0,16},{32,48},{64,80},{96,112},{128,144},{160,176},{192,208},{224... | collective-permute-start | bytes 221192 | tf_op jit(solution)/shard_map/ppermute | solution.py:26
  9.2 11.9 %copy-start.3 = (s32[1,1,256]{2,1,0:T(1,128)S(1)}, s32[1,1,256]{2,1,0:T(1,128)}, u32[]{:S(2)}) copy-start(s32[1,1,256]{2,1,0:T(1,128)} %send.1) | copy-start | bytes 3076
  9.2 11.9 %copy-start.4 = (s32[1,1,16]{2,1,0:T(1,128)S(1)}, s32[1,1,16]{2,1,0:T(1,128)}, u32[]{:S(2)}) copy-start(s32[1,1,16]{2,1,0:T(1,128)} %live.1) | copy-start | bytes 196
  9.3 13.2 %collective-permute-start.2 = (bf16[17,16,128]{2,1,0:T(8,128)(2,1)S(1)}, bf16[17,16,128]{2,1,0:T(8,128)(2,1)S(1)}, u32[]{:S(2)}, u32[]{:S(2)}) collective-permute-start(bf16[17,16,128]{2,1,0:T(8,128)(2,1)S(1)} %get-tuple-element.16), channel_id=1, source_target_pairs={{1,2},{3,4},{5,6},{7,8},{9,10},{11,12},{13,14},{2,1},{4,3},{6,5},{... | collective-permute-start | bytes 208904 | tf_op jit(solution)/shard_map/ppermute | solution.py:26
  13.5 8.9 %collective-permute-start.3 = (bf16[17,16,128]{2,1,0:T(8,128)(2,1)S(1)}, bf16[17,16,128]{2,1,0:T(8,128)(2,1)S(1)}, u32[]{:S(2)}, u32[]{:S(2)}) collective-permute-start(bf16[17,16,128]{2,1,0:T(8,128)(2,1)S(1)} %get-tuple-element.17), channel_id=1, source_target_pairs={{0,1},{2,3},{4,5},{6,7},{8,9},{10,11},{12,13},{14,15},{1,0},{3,2},... | collective-permute-start | bytes 208904 | tf_op jit(solution)/shard_map/ppermute | solution.py:26
  23.4 3.8 %copy-start.1 = (f32[8,16,128]{2,1,0:T(8,128)S(1)}, f32[8,16,128]{2,1,0:T(8,128)}, u32[]{:S(2)}) copy-start(f32[8,16,128]{2,1,0:T(8,128)} %logf.1) | copy-start | bytes 196612
  23.4 12.0 %all-to-all-start = ((bf16[16,10,2,128]{3,2,1,0:T(2,128)(2,1)}), bf16[16,10,2,128]{3,2,1,0:T(2,128)(2,1)S(1)}, u32[]{:S(2)}, u32[]{:S(2)}) async-start(bf16[16,10,2,128]{3,2,1,0:T(2,128)(2,1)} %message.1), calls=%async_computation | async-start | bytes 163840 | tf_op jit(solution)/shard_map/all_to_all | solution.py:286

commit v9 on v8

--- a/solution.py
+++ b/solution.py
@@ -58,9 +58,7 @@
         copy.wait()
 
 
-def local_body(adj, coupling_hbm, send, live, nodes, base, pick, ids, coupling, wide, sem):
-    fetch = pltpu.make_async_copy(coupling_hbm, coupling, sem)
-    fetch.start()
+def local_body(adj, coupling, send, live, nodes, base, pick, ids, wide):
     ca, cb, nl, width = adj.shape
     faces = ca * cb
     for a in range(ca):
@@ -79,7 +77,6 @@
     mine = lane // slots == lax.axis_index("gy") % (width // slots)
     alive = (lane % slots).astype(F32) < counts
     ids[...] = jnp.where(jnp.logical_and(mine, alive), listed, 0.0)
-    fetch.wait()
     low = wide[pl.ds(0, faces, stride=8), :].astype(BF16)
     above = wide[pl.ds(1, faces, stride=8), :].astype(BF16)
     total = dot(low, coupling[0]) + dot(above, coupling[2])
@@ -246,6 +243,7 @@
         out_specs=(VMEM,) * 4,
         scratch_shapes=[pltpu.VMEM(log_friction.shape, F32), pltpu.SemaphoreType.DMA((5,))],
         compiler_params=wire,
+        cost_estimate=cost(10**9, 3 * 2**20),
         name="pack",
     )(in_hbm(adjoint_trace), in_hbm(log_friction))
     a_near = swap(to_a_near, "gx", 0)
@@ -253,21 +251,20 @@
     b_far = swap(to_b_far, "gy", 1)
     b_near = swap(to_b_near, "gy", 0)
 
-    base, pick, ids, blocks = pl.pallas_call(
+    base, pick, ids = pl.pallas_call(
         local_body,
         out_shape=(
             shape((faces, width), F32),
             shape((faces, faces), BF16),
             shape((owners, width), F32),
-            shape(coupling.shape, BF16),
         ),
-        in_specs=[VMEM, HBM] + [VMEM] * 3,
-        out_specs=(VMEM,) * 4,
-        scratch_shapes=[pltpu.VMEM((faces * 8, width), F32), pltpu.SemaphoreType.DMA],
+        in_specs=[VMEM] * 5,
+        out_specs=(VMEM,) * 3,
+        scratch_shapes=[pltpu.VMEM((faces * 8, width), F32)],
         compiler_params=wire,
         cost_estimate=cost(2 * 6 * faces * width * width, 2 * 2**20),
         name="local",
-    )(adjoint_trace, in_hbm(coupling), send_column, live_count, target_node)
+    )(adjoint_trace, coupling, send_column, live_count, target_node)
 
     message = pl.pallas_call(
         message_body,
@@ -281,7 +278,7 @@
         compiler_params=wire,
         cost_estimate=cost(2 * faces * faces * width, 2**20),
         name="message",
-    )(base, pick, ids, blocks, a_far, a_near, b_far, b_near)
+    )(base, pick, ids, coupling, a_far, a_near, b_far, b_near)
 
     received = lax.all_to_all(message, "gy", split_axis=0, concat_axis=0, tiled=True)
 
@@ -307,7 +304,7 @@
         compiler_params=wire,
         cost_estimate=cost(2 * 7 * faces * nl * width * width, 4 * 2**20),
         name="update",
-    )(adjoint_trace, blocks, log_friction, a_far, a_near, b_far, b_near)
+    )(adjoint_trace, coupling, log_friction, a_far, a_near, b_far, b_near)
 
     gradient = pl.pallas_call(
         gradient_body,

time: 36.6 us -> 36.6 us (level)
  Pallas kernels: 7.1 us -> 6.21 us
  starting transfers between devices: 23.1 us -> 23.6 us
  waiting for transfers between devices: 5.24 us -> 5.71 us
    pallas_call x1, Pallas kernels: 1.24 us -> 0.35 us  [per_device(): pl.pallas_call(local_body, out_shape=(shape((faces, width), F32), shape((...]
    ppermute x4, waiting for transfers between devices: 0.01 us -> 0.48 us  [swap(): return lax.ppermute(block, axis, pairs + [(j, i) for i, j in pairs])]
    all_to_all x1, starting transfers between devices: 3.8 us -> 4.24 us  [per_device(): lax.all_to_all(message, 'gy', split_axis=0, concat_axis=0, tiled=True)]
  transfers between devices with their start and end apart: 5 -> 5, of which waited for: 1 -> 2; matrix products, arithmetic and copies ran while one was open for 0% -> 0% of each run, Pallas kernels for 12% -> 9%
where the time goes in v9:
time: 36.6 us; the launch traced here: 36.3 us
  starting transfers between devices  23.6 us (64%)
  Pallas kernels  6.21 us (17%)
  waiting for transfers between devices  5.71 us (16%)
  between operations  0.78 us (2%)
    ppermute x4, starting transfers between devices, swap(): return lax.ppermute(block, axis, pairs + [(j, i) for i, j in pairs])  19.3 us
    all_to_all x1, waiting for transfers between devices, per_device(): lax.all_to_all(message, 'gy', split_axis=0, concat_axis=0, tiled=True)  5.23 us
    all_to_all x1, starting transfers between devices, per_device(): lax.all_to_all(message, 'gy', split_axis=0, concat_axis=0, tiled=True)  4.24 us
    pallas_call x1, Pallas kernels, per_device(): pl.pallas_call(update_body, out_shape=(shape(adjoint_trace.shape, BF16),...  2.94 us
    pallas_call x1, Pallas kernels, per_device(): pl.pallas_call(pack_body, out_shape=(shape((cb + 2, nl, width), BF16), sh...  1.11 us
    pallas_call x1, Pallas kernels, per_device(): pl.pallas_call(message_body, out_shape=shape((owners, MSG // 2, 2, width)...  0.98 us
    pallas_call x1, Pallas kernels, per_device(): pl.pallas_call(gradient_body, out_shape=shape(log_friction.shape, F32), i...  0.83 us
  transfers between devices with their start and end apart: 5, of which 2 were waited for; matrix products, arithmetic and copies ran while one was open for 0% of the time, Pallas kernels for 9%

profile of v9, /device:TPU:1, one launch (start us, length us, event | category | flops | bytes accessed | tf_op | source)
XLA Modules:
  0.0 36.3 jit_solution(17725662836086239639)
XLA Ops:
  0.6 0.0 copy-start
  0.6 0.0 copy-start.1
  0.6 0.0 copy-start.2
  0.7 1.1 %pack.1 = (bf16[18,16,128]{2,1,0:T(8,128)(2,1)S(1)}, bf16[18,16,128]{2,1,0:T(8,128)(2,1)S(1)}, bf16[17,16,128]{2,1,0:T(8,128)(2,1)S(1)}, bf16[17,16,128]{2,1,0:T(8,128)(2,1)S(1)}) custom-call(bf16[16,16,16,128]{3,2,1,0:T(8,128)(2,1)} %adj.3, f32[8,16,128]{2,1,0:T(8,128)} %logf.1), custom_call_target="tpu_custom_call" | custom-call | flops 1000000000 | bytes 3145728 | tf_op jit(solution)/shard_map/pack/pallas_call | solution.py:234
  1.8 0.7 %collective-permute-start = (bf16[18,16,128]{2,1,0:T(8,128)(2,1)S(1)}, bf16[18,16,128]{2,1,0:T(8,128)(2,1)S(1)}, u32[]{:S(2)}, u32[]{:S(2)}) collective-permute-start(bf16[18,16,128]{2,1,0:T(8,128)(2,1)S(1)} %get-tuple-element.12), channel_id=1, source_target_pairs={{16,32},{48,64},{80,96},{112,128},{144,160},{176,192},{208,224},{2... | collective-permute-start | bytes 221192 | tf_op jit(solution)/shard_map/ppermute | solution.py:26
  2.4 6.8 %collective-permute-start.1 = (bf16[18,16,128]{2,1,0:T(8,128)(2,1)S(1)}, bf16[18,16,128]{2,1,0:T(8,128)(2,1)S(1)}, u32[]{:S(2)}, u32[]{:S(2)}) collective-permute-start(bf16[18,16,128]{2,1,0:T(8,128)(2,1)S(1)} %get-tuple-element.13), channel_id=1, source_target_pairs={{0,16},{32,48},{64,80},{96,112},{128,144},{160,176},{192,208},{224... | collective-permute-start | bytes 221192 | tf_op jit(solution)/shard_map/ppermute | solution.py:26
  9.3 0.0 copy-start.3
  9.3 0.0 copy-start.4
  9.3 4.2 %collective-permute-start.2 = (bf16[17,16,128]{2,1,0:T(8,128)(2,1)S(1)}, bf16[17,16,128]{2,1,0:T(8,128)(2,1)S(1)}, u32[]{:S(2)}, u32[]{:S(2)}) collective-permute-start(bf16[17,16,128]{2,1,0:T(8,128)(2,1)S(1)} %get-tuple-element.14), channel_id=1, source_target_pairs={{1,2},{3,4},{5,6},{7,8},{9,10},{11,12},{13,14},{2,1},{4,3},{6,5},{... | collective-permute-start | bytes 208904 | tf_op jit(solution)/shard_map/ppermute | solution.py:26
  13.5 7.6 %collective-permute-start.3 = (bf16[17,16,128]{2,1,0:T(8,128)(2,1)S(1)}, bf16[17,16,128]{2,1,0:T(8,128)(2,1)S(1)}, u32[]{:S(2)}, u32[]{:S(2)}) collective-permute-start(bf16[17,16,128]{2,1,0:T(8,128)(2,1)S(1)} %get-tuple-element.15), channel_id=1, source_target_pairs={{0,1},{2,3},{4,5},{6,7},{8,9},{10,11},{12,13},{14,15},{1,0},{3,2},... | collective-permute-start | bytes 208904 | tf_op jit(solution)/shard_map/ppermute | solution.py:26
  21.1 0.0 copy-done
  21.2 0.0 copy-done.1
  21.2 0.0 copy-done.2
  21.2 0.0 copy-done.3
  21.2 0.0 copy-done.4
  21.2 0.3 local.1
  21.5 0.0 collective-permute-done.2.b_far
  21.6 0.5 %collective-permute-done.3.b_near = bf16[17,16,128]{2,1,0:T(8,128)(2,1)S(1)} collective-permute-done((bf16[17,16,128]{2,1,0:T(8,128)(2,1)S(1)}, bf16[17,16,128]{2,1,0:T(8,128)(2,1)S(1)}, u32[]{:S(2)}, u32[]{:S(2)}) %collective-permute-start.3) | collective-permute-done | bytes 69664 | tf_op jit(solution)/shard_map/ppermute | solution.py:26
  22.0 0.0 collective-permute-done.a_far
  22.0 0.0 collective-permute-done.1.a_near
  22.0 1.0 %message.1 = bf16[16,10,2,128]{3,2,1,0:T(2,128)(2,1)} custom-call(f32[256,128]{1,0:T(8,128)S(1)} %get-tuple-element.17.base, bf16[256,256]{1,0:T(8,128)(2,1)S(1)} %get-tuple-element.18.pick, f32[16,128]{1,0:T(8,128)S(1)} %get-tuple-element.19.ids, bf16[7,128,128]{2,1,0:T(8,128)(2,1)S(1)} %copy-done.1, bf16[18,16,128]{2,1,0:T(8,128)(2,1)S(1)} %collective-permute-done.a_far, ...), custom_call_target="tpu_custom_call" | custom-call | flops 16777216 | bytes 1048576 | tf_op jit(solution)/shard_map/message/pallas_call | solution.py:269
  23.0 0.0 copy-start.5
  23.0 4.2 %all-to-all-start = ((bf16[16,10,2,128]{3,2,1,0:T(2,128)(2,1)}), bf16[16,10,2,128]{3,2,1,0:T(2,128)(2,1)S(1)}, u32[]{:S(2)}, u32[]{:S(2)}) async-start(bf16[16,10,2,128]{3,2,1,0:T(2,128)(2,1)} %message.1), calls=%async_computation | async-start | bytes 163840 | tf_op jit(solution)/shard_map/all_to_all | solution.py:283
  27.3 0.0 copy-done.5
  27.3 2.9 %update.1 = (bf16[16,16,16,128]{3,2,1,0:T(8,128)(2,1)}, f32[8,16,128]{2,1,0:T(8,128)S(1)}, f32[8,16,128]{2,1,0:T(8,128)S(1)}) custom-call(bf16[16,16,16,128]{3,2,1,0:T(8,128)(2,1)S(1)} %copy-done, bf16[7,128,128]{2,1,0:T(8,128)(2,1)S(1)} %copy-done.1, f32[8,16,128]{2,1,0:T(8,128)S(1)} %copy-done.5, bf16[18,16,128]{2,1,0:T(8,128)(2,1)S(1)} %collective-permute-done.a_far, ...), custom_call_target="tpu_custom_call" | custom-call | flops 939524096 | bytes 4194304 | tf_op jit(solution)/shard_map/update/pallas_call | solution.py:285
  30.2 5.2 %all-to-all-done.got = bf16[16,10,2,128]{3,2,1,0:T(2,128)(2,1)S(1)} async-done(((bf16[16,10,2,128]{3,2,1,0:T(2,128)(2,1)}), bf16[16,10,2,128]{3,2,1,0:T(2,128)(2,1)S(1)}, u32[]{:S(2)}, u32[]{:S(2)}) %all-to-all-start) | async-done | bytes 81952 | tf_op jit(solution)/shard_map/all_to_all | solution.py:283
  35.4 0.8 %gradient.1 = f32[8,16,128]{2,1,0:T(8,128)} custom-call(bf16[16,10,2,128]{3,2,1,0:T(2,128)(2,1)S(1)} %all-to-all-done.got, f32[8,16,128]{2,1,0:T(8,128)S(1)} %get-tuple-element.20.prior, f32[8,16,128]{2,1,0:T(8,128)S(1)} %get-tuple-element.21.scale), custom_call_target="tpu_custom_call" | custom-call | flops 8388608 | bytes 524288 | tf_op jit(solution)/shard_map/gradient/pallas_call | solution.py:309
Async XLA Ops:
  0.6 20.5 %copy-start = (bf16[16,16,16,128]{3,2,1,0:T(8,128)(2,1)S(1)}, bf16[16,16,16,128]{3,2,1,0:T(8,128)(2,1)}, u32[]{:S(2)}) copy-start(bf16[16,16,16,128]{3,2,1,0:T(8,128)(2,1)} %adj.3) | copy-start | bytes 3145732
  0.6 20.5 %copy-start.1 = (bf16[7,128,128]{2,1,0:T(8,128)(2,1)S(1)}, bf16[7,128,128]{2,1,0:T(8,128)(2,1)}, u32[]{:S(2)}) copy-start(bf16[7,128,128]{2,1,0:T(8,128)(2,1)} %coupling.5) | copy-start | bytes 688132
  0.6 20.5 %copy-start.2 = (s32[1,1,16,16]{3,2,1,0:T(8,128)S(1)}, s32[1,1,16,16]{3,2,1,0:T(8,128)}, u32[]{:S(2)}) copy-start(s32[1,1,16,16]{3,2,1,0:T(8,128)} %nodes.1) | copy-start | bytes 3076
  1.8 20.3 %collective-permute-start = (bf16[18,16,128]{2,1,0:T(8,128)(2,1)S(1)}, bf16[18,16,128]{2,1,0:T(8,128)(2,1)S(1)}, u32[]{:S(2)}, u32[]{:S(2)}) collective-permute-start(bf16[18,16,128]{2,1,0:T(8,128)(2,1)S(1)} %get-tuple-element.12), channel_id=1, source_target_pairs={{16,32},{48,64},{80,96},{112,128},{144,160},{176,192},{208,224},{2... | collective-permute-start | bytes 221192 | tf_op jit(solution)/shard_map/ppermute | solution.py:26
  2.4 19.6 %collective-permute-start.1 = (bf16[18,16,128]{2,1,0:T(8,128)(2,1)S(1)}, bf16[18,16,128]{2,1,0:T(8,128)(2,1)S(1)}, u32[]{:S(2)}, u32[]{:S(2)}) collective-permute-start(bf16[18,16,128]{2,1,0:T(8,128)(2,1)S(1)} %get-tuple-element.13), channel_id=1, source_target_pairs={{0,16},{32,48},{64,80},{96,112},{128,144},{160,176},{192,208},{224... | collective-permute-start | bytes 221192 | tf_op jit(solution)/shard_map/ppermute | solution.py:26
  9.3 11.9 %copy-start.3 = (s32[1,1,256]{2,1,0:T(1,128)S(1)}, s32[1,1,256]{2,1,0:T(1,128)}, u32[]{:S(2)}) copy-start(s32[1,1,256]{2,1,0:T(1,128)} %send.1) | copy-start | bytes 3076
  9.3 11.9 %copy-start.4 = (s32[1,1,16]{2,1,0:T(1,128)S(1)}, s32[1,1,16]{2,1,0:T(1,128)}, u32[]{:S(2)}) copy-start(s32[1,1,16]{2,1,0:T(1,128)} %live.1) | copy-start | bytes 196
  9.3 12.3 %collective-permute-start.2 = (bf16[17,16,128]{2,1,0:T(8,128)(2,1)S(1)}, bf16[17,16,128]{2,1,0:T(8,128)(2,1)S(1)}, u32[]{:S(2)}, u32[]{:S(2)}) collective-permute-start(bf16[17,16,128]{2,1,0:T(8,128)(2,1)S(1)} %get-tuple-element.14), channel_id=1, source_target_pairs={{1,2},{3,4},{5,6},{7,8},{9,10},{11,12},{13,14},{2,1},{4,3},{6,5},{... | collective-permute-start | bytes 208904 | tf_op jit(solution)/shard_map/ppermute | solution.py:26
  13.5 8.5 %collective-permute-start.3 = (bf16[17,16,128]{2,1,0:T(8,128)(2,1)S(1)}, bf16[17,16,128]{2,1,0:T(8,128)(2,1)S(1)}, u32[]{:S(2)}, u32[]{:S(2)}) collective-permute-start(bf16[17,16,128]{2,1,0:T(8,128)(2,1)S(1)} %get-tuple-element.15), channel_id=1, source_target_pairs={{0,1},{2,3},{4,5},{6,7},{8,9},{10,11},{12,13},{14,15},{1,0},{3,2},... | collective-permute-start | bytes 208904 | tf_op jit(solution)/shard_map/ppermute | solution.py:26
  23.0 4.2 %copy-start.5 = (f32[8,16,128]{2,1,0:T(8,128)S(1)}, f32[8,16,128]{2,1,0:T(8,128)}, u32[]{:S(2)}) copy-start(f32[8,16,128]{2,1,0:T(8,128)} %logf.1) | copy-start | bytes 196612
  23.0 12.4 %all-to-all-start = ((bf16[16,10,2,128]{3,2,1,0:T(2,128)(2,1)}), bf16[16,10,2,128]{3,2,1,0:T(2,128)(2,1)S(1)}, u32[]{:S(2)}, u32[]{:S(2)}) async-start(bf16[16,10,2,128]{3,2,1,0:T(2,128)(2,1)} %message.1), calls=%async_computation | async-start | bytes 163840 | tf_op jit(solution)/shard_map/all_to_all | solution.py:283

commit v10 on v9

--- a/solution.py
+++ b/solution.py
@@ -90,31 +90,40 @@
     base[...] = total
 
 
-def message_body(base, pick, ids, coupling, a_far, a_near, b_far, b_near, out, total, wide):
+def gx_edge(total, halo, wide, coupling, high):
+    faces, width = total.shape
+    cb = halo.shape[0] - 2
+    wide[0:cb * 8] = halo[0:cb, 0:8, :].astype(F32).reshape(cb * 8, width)
+    rows = pl.ds(pl.multiple_of((faces - cb) * high, cb), cb)
+    total[rows, :] += dot(wide[pl.ds(0, cb, stride=8), :].astype(BF16), coupling[3 + high])
+
+
+def edges_body(base, coupling, a_far, b_far, b_near, total, wide):
     faces, width = base.shape
+    ca = b_far.shape[0] - 1
+    cb = faces // ca
+    odd_b = lax.axis_index("gy") % 2 == 1
+    total[...] = base[...]
+    gx_edge(total, a_far, wide, coupling, lax.axis_index("gx") % 2)
+    for k, halo in enumerate((b_far, b_near)):
+        wide[k * ca * 8:(k + 1) * ca * 8] = halo[0:ca, 0:8, :].astype(F32).reshape(ca * 8, width)
+
+    def edge(k):
+        own, other = (wide[pl.ds(n * ca * 8, ca, stride=8), :] for n in (k, 1 - k))
+        return jnp.where(odd_b, other, own).astype(BF16)
+
+    total[pl.ds(0, ca, stride=cb), :] += dot(edge(0), coupling[5])
+    total[pl.ds(cb - 1, ca, stride=cb), :] += dot(edge(1), coupling[6])
+
+
+def message_body(partial, pick, ids, coupling, a_far, a_near, out, total, wide):
+    faces, width = partial.shape
     owners, slots = out.shape[0], faces // out.shape[0]
     cb = a_far.shape[0] - 2
-    ca = b_far.shape[0] - 1
     here = lax.axis_index("gy")
-    odd_a, odd_b = lax.axis_index("gx") % 2 == 1, here % 2 == 1
-    for k, halo in enumerate((a_far, a_near, b_far, b_near)):
-        rows = cb if k < 2 else ca
-        wide[k * rows * 8:(k + 1) * rows * 8] = (
-            halo[0:rows, 0:8, :].astype(F32).reshape(rows * 8, width)
-        )
-
-    def row(k, rows):
-        return wide[pl.ds(k * rows * 8, rows, stride=8), :]
-
-    def edge(k, rows):
-        odd = odd_a if k < 2 else odd_b
-        return jnp.where(odd, row(k ^ 1, rows), row(k, rows)).astype(BF16)
-
-    total[...] = base[...]
-    total[0:cb] += dot(edge(0, cb), coupling[3])
-    total[faces - cb:faces] += dot(edge(1, cb), coupling[4])
-    total[pl.ds(0, ca, stride=cb), :] += dot(edge(2, ca), coupling[5])
-    total[pl.ds(cb - 1, ca, stride=cb), :] += dot(edge(3, ca), coupling[6])
+    odd_a = lax.axis_index("gx") % 2 == 1
+    total[...] = partial[...]
+    gx_edge(total, a_near, wide, coupling, 1 - lax.axis_index("gx") % 2)
     picked = dot(pick[...], total[...].astype(BF16)).astype(BF16)
     pb = a_far.shape[1]
     top = jnp.where(odd_a, a_near[cb + 1].astype(F32), a_far[cb + 1].astype(F32))
@@ -266,19 +275,30 @@
         name="local",
     )(adjoint_trace, coupling, send_column, live_count, target_node)
 
+    partial = pl.pallas_call(
+        edges_body,
+        out_shape=shape((faces, width), F32),
+        in_specs=[VMEM] * 5,
+        out_specs=VMEM,
+        scratch_shapes=[pltpu.VMEM((2 * ca * 8, width), F32)],
+        compiler_params=wire,
+        cost_estimate=cost(2 * 3 * ca * width * width, 2**18),
+        name="edges",
+    )(base, coupling, a_far, b_far, b_near)
+
     message = pl.pallas_call(
         message_body,
         out_shape=shape((owners, MSG // 2, 2, width), BF16),
-        in_specs=[VMEM] * 8,
+        in_specs=[VMEM] * 6,
         out_specs=VMEM,
         scratch_shapes=[
             pltpu.VMEM((faces, width), F32),
-            pltpu.VMEM((2 * (ca + cb) * 8, width), F32),
+            pltpu.VMEM((cb * 8, width), F32),
         ],
         compiler_params=wire,
         cost_estimate=cost(2 * faces * faces * width, 2**20),
         name="message",
-    )(base, pick, ids, coupling, a_far, a_near, b_far, b_near)
+    )(partial, pick, ids, coupling, a_far, a_near)
 
     received = lax.all_to_all(message, "gy", split_axis=0, concat_axis=0, tiled=True)
 

time: 36.6 us -> 36.6 us (level)
  no operation moved by 1% of the time
where the time goes in v10:
time: 36.6 us; the launch traced here: 36.3 us
  starting transfers between devices  23.4 us (64%)
  Pallas kernels  6.36 us (17%)
  waiting for transfers between devices  5.71 us (16%)
  between operations  0.79 us (2%)
    ppermute x4, starting transfers between devices, swap(): return lax.ppermute(block, axis, pairs + [(j, i) for i, j in pairs])  19.3 us
    all_to_all x1, waiting for transfers between devices, per_device(): lax.all_to_all(message, 'gy', split_axis=0, concat_axis=0, tiled=True)  5.23 us
    all_to_all x1, starting transfers between devices, per_device(): lax.all_to_all(message, 'gy', split_axis=0, concat_axis=0, tiled=True)  4.05 us
    pallas_call x1, Pallas kernels, per_device(): pl.pallas_call(update_body, out_shape=(shape(adjoint_trace.shape, BF16),...  2.94 us
    pallas_call x1, Pallas kernels, per_device(): pl.pallas_call(pack_body, out_shape=(shape((cb + 2, nl, width), BF16), sh...  1.11 us
    pallas_call x1, Pallas kernels, per_device(): pl.pallas_call(message_body, out_shape=shape((owners, MSG // 2, 2, width)...  0.97 us
    pallas_call x1, Pallas kernels, per_device(): pl.pallas_call(gradient_body, out_shape=shape(log_friction.shape, F32), i...  0.83 us
  transfers between devices with their start and end apart: 5, of which 2 were waited for; matrix products, arithmetic and copies ran while one was open for 0% of the time, Pallas kernels for 9%

profile of v10, /device:TPU:1, one launch (start us, length us, event | category | flops | bytes accessed | tf_op | source)
XLA Modules:
  0.0 36.3 jit_solution(3493974533599974701)
XLA Ops:
  0.6 0.0 copy-start.1
  0.6 0.0 copy-start
  0.6 0.0 copy-start.2
  0.7 1.1 %pack.1 = (bf16[18,16,128]{2,1,0:T(8,128)(2,1)S(1)}, bf16[18,16,128]{2,1,0:T(8,128)(2,1)S(1)}, bf16[17,16,128]{2,1,0:T(8,128)(2,1)S(1)}, bf16[17,16,128]{2,1,0:T(8,128)(2,1)S(1)}) custom-call(bf16[16,16,16,128]{3,2,1,0:T(8,128)(2,1)} %adj.3, f32[8,16,128]{2,1,0:T(8,128)} %logf.1), custom_call_target="tpu_custom_call" | custom-call | flops 1000000000 | bytes 3145728 | tf_op jit(solution)/shard_map/pack/pallas_call | solution.py:243
  1.8 0.7 %collective-permute-start = (bf16[18,16,128]{2,1,0:T(8,128)(2,1)S(1)}, bf16[18,16,128]{2,1,0:T(8,128)(2,1)S(1)}, u32[]{:S(2)}, u32[]{:S(2)}) collective-permute-start(bf16[18,16,128]{2,1,0:T(8,128)(2,1)S(1)} %get-tuple-element.12), channel_id=1, source_target_pairs={{16,32},{48,64},{80,96},{112,128},{144,160},{176,192},{208,224},{2... | collective-permute-start | bytes 221192 | tf_op jit(solution)/shard_map/ppermute | solution.py:26
  2.4 6.8 %collective-permute-start.1 = (bf16[18,16,128]{2,1,0:T(8,128)(2,1)S(1)}, bf16[18,16,128]{2,1,0:T(8,128)(2,1)S(1)}, u32[]{:S(2)}, u32[]{:S(2)}) collective-permute-start(bf16[18,16,128]{2,1,0:T(8,128)(2,1)S(1)} %get-tuple-element.13), channel_id=1, source_target_pairs={{0,16},{32,48},{64,80},{96,112},{128,144},{160,176},{192,208},{224... | collective-permute-start | bytes 221192 | tf_op jit(solution)/shard_map/ppermute | solution.py:26
  9.3 0.0 copy-start.3
  9.3 0.0 copy-start.4
  9.3 4.2 %collective-permute-start.2 = (bf16[17,16,128]{2,1,0:T(8,128)(2,1)S(1)}, bf16[17,16,128]{2,1,0:T(8,128)(2,1)S(1)}, u32[]{:S(2)}, u32[]{:S(2)}) collective-permute-start(bf16[17,16,128]{2,1,0:T(8,128)(2,1)S(1)} %get-tuple-element.14), channel_id=1, source_target_pairs={{1,2},{3,4},{5,6},{7,8},{9,10},{11,12},{13,14},{2,1},{4,3},{6,5},{... | collective-permute-start | bytes 208904 | tf_op jit(solution)/shard_map/ppermute | solution.py:26
  13.5 7.6 %collective-permute-start.3 = (bf16[17,16,128]{2,1,0:T(8,128)(2,1)S(1)}, bf16[17,16,128]{2,1,0:T(8,128)(2,1)S(1)}, u32[]{:S(2)}, u32[]{:S(2)}) collective-permute-start(bf16[17,16,128]{2,1,0:T(8,128)(2,1)S(1)} %get-tuple-element.15), channel_id=1, source_target_pairs={{0,1},{2,3},{4,5},{6,7},{8,9},{10,11},{12,13},{14,15},{1,0},{3,2},... | collective-permute-start | bytes 208904 | tf_op jit(solution)/shard_map/ppermute | solution.py:26
  21.1 0.0 copy-done.1
  21.2 0.0 copy-done
  21.2 0.0 copy-done.2
  21.2 0.0 copy-done.3
  21.2 0.0 copy-done.4
  21.2 0.3 local.1
  21.5 0.0 collective-permute-done.2.b_far
  21.6 0.5 %collective-permute-done.3.b_near = bf16[17,16,128]{2,1,0:T(8,128)(2,1)S(1)} collective-permute-done((bf16[17,16,128]{2,1,0:T(8,128)(2,1)S(1)}, bf16[17,16,128]{2,1,0:T(8,128)(2,1)S(1)}, u32[]{:S(2)}, u32[]{:S(2)}) %collective-permute-start.3) | collective-permute-done | bytes 69664 | tf_op jit(solution)/shard_map/ppermute | solution.py:26
  22.0 0.0 collective-permute-done.a_far
  22.0 0.2 edges.1.partial
  22.2 0.0 collective-permute-done.1.a_near
  22.2 1.0 %message.1 = bf16[16,10,2,128]{3,2,1,0:T(2,128)(2,1)} custom-call(f32[256,128]{1,0:T(8,128)S(1)} %edges.1.partial, bf16[256,256]{1,0:T(8,128)(2,1)S(1)} %get-tuple-element.18.pick, f32[16,128]{1,0:T(8,128)S(1)} %get-tuple-element.19.ids, bf16[7,128,128]{2,1,0:T(8,128)(2,1)S(1)} %copy-done, bf16[18,16,128]{2,1,0:T(8,128)(2,1)S(1)} %collective-permute-done.a_far, ...), custom_call_target="tpu_custom_call" | custom-call | flops 16777216 | bytes 1048576 | tf_op jit(solution)/shard_map/message/pallas_call | solution.py:289
  23.2 0.0 copy-start.5
  23.2 4.0 %all-to-all-start = ((bf16[16,10,2,128]{3,2,1,0:T(2,128)(2,1)}), bf16[16,10,2,128]{3,2,1,0:T(2,128)(2,1)S(1)}, u32[]{:S(2)}, u32[]{:S(2)}) async-start(bf16[16,10,2,128]{3,2,1,0:T(2,128)(2,1)} %message.1), calls=%async_computation | async-start | bytes 163840 | tf_op jit(solution)/shard_map/all_to_all | solution.py:303
  27.2 0.0 copy-done.5
  27.2 2.9 %update.1 = (bf16[16,16,16,128]{3,2,1,0:T(8,128)(2,1)}, f32[8,16,128]{2,1,0:T(8,128)S(1)}, f32[8,16,128]{2,1,0:T(8,128)S(1)}) custom-call(bf16[16,16,16,128]{3,2,1,0:T(8,128)(2,1)S(1)} %copy-done.1, bf16[7,128,128]{2,1,0:T(8,128)(2,1)S(1)} %copy-done, f32[8,16,128]{2,1,0:T(8,128)S(1)} %copy-done.5, bf16[18,16,128]{2,1,0:T(8,128)(2,1)S(1)} %collective-permute-done.a_far, ...), custom_call_target="tpu_custom_call" | custom-call | flops 939524096 | bytes 4194304 | tf_op jit(solution)/shard_map/update/pallas_call | solution.py:305
  30.2 5.2 %all-to-all-done.got = bf16[16,10,2,128]{3,2,1,0:T(2,128)(2,1)S(1)} async-done(((bf16[16,10,2,128]{3,2,1,0:T(2,128)(2,1)}), bf16[16,10,2,128]{3,2,1,0:T(2,128)(2,1)S(1)}, u32[]{:S(2)}, u32[]{:S(2)}) %all-to-all-start) | async-done | bytes 81952 | tf_op jit(solution)/shard_map/all_to_all | solution.py:303
  35.4 0.8 %gradient.1 = f32[8,16,128]{2,1,0:T(8,128)} custom-call(bf16[16,10,2,128]{3,2,1,0:T(2,128)(2,1)S(1)} %all-to-all-done.got, f32[8,16,128]{2,1,0:T(8,128)S(1)} %get-tuple-element.20.prior, f32[8,16,128]{2,1,0:T(8,128)S(1)} %get-tuple-element.21.scale), custom_call_target="tpu_custom_call" | custom-call | flops 8388608 | bytes 524288 | tf_op jit(solution)/shard_map/gradient/pallas_call | solution.py:329
Async XLA Ops:
  0.6 20.5 %copy-start.1 = (bf16[16,16,16,128]{3,2,1,0:T(8,128)(2,1)S(1)}, bf16[16,16,16,128]{3,2,1,0:T(8,128)(2,1)}, u32[]{:S(2)}) copy-start(bf16[16,16,16,128]{3,2,1,0:T(8,128)(2,1)} %adj.3) | copy-start | bytes 3145732
  0.6 20.5 %copy-start = (bf16[7,128,128]{2,1,0:T(8,128)(2,1)S(1)}, bf16[7,128,128]{2,1,0:T(8,128)(2,1)}, u32[]{:S(2)}) copy-start(bf16[7,128,128]{2,1,0:T(8,128)(2,1)} %coupling.7) | copy-start | bytes 688132
  0.6 20.5 %copy-start.2 = (s32[1,1,16,16]{3,2,1,0:T(8,128)S(1)}, s32[1,1,16,16]{3,2,1,0:T(8,128)}, u32[]{:S(2)}) copy-start(s32[1,1,16,16]{3,2,1,0:T(8,128)} %nodes.1) | copy-start | bytes 3076
  1.8 20.3 %collective-permute-start = (bf16[18,16,128]{2,1,0:T(8,128)(2,1)S(1)}, bf16[18,16,128]{2,1,0:T(8,128)(2,1)S(1)}, u32[]{:S(2)}, u32[]{:S(2)}) collective-permute-start(bf16[18,16,128]{2,1,0:T(8,128)(2,1)S(1)} %get-tuple-element.12), channel_id=1, source_target_pairs={{16,32},{48,64},{80,96},{112,128},{144,160},{176,192},{208,224},{2... | collective-permute-start | bytes 221192 | tf_op jit(solution)/shard_map/ppermute | solution.py:26
  2.4 19.8 %collective-permute-start.1 = (bf16[18,16,128]{2,1,0:T(8,128)(2,1)S(1)}, bf16[18,16,128]{2,1,0:T(8,128)(2,1)S(1)}, u32[]{:S(2)}, u32[]{:S(2)}) collective-permute-start(bf16[18,16,128]{2,1,0:T(8,128)(2,1)S(1)} %get-tuple-element.13), channel_id=1, source_target_pairs={{0,16},{32,48},{64,80},{96,112},{128,144},{160,176},{192,208},{224... | collective-permute-start | bytes 221192 | tf_op jit(solution)/shard_map/ppermute | solution.py:26
  9.3 11.9 %copy-start.3 = (s32[1,1,256]{2,1,0:T(1,128)S(1)}, s32[1,1,256]{2,1,0:T(1,128)}, u32[]{:S(2)}) copy-start(s32[1,1,256]{2,1,0:T(1,128)} %send.1) | copy-start | bytes 3076
  9.3 11.9 %copy-start.4 = (s32[1,1,16]{2,1,0:T(1,128)S(1)}, s32[1,1,16]{2,1,0:T(1,128)}, u32[]{:S(2)}) copy-start(s32[1,1,16]{2,1,0:T(1,128)} %live.1) | copy-start | bytes 196
  9.3 12.3 %collective-permute-start.2 = (bf16[17,16,128]{2,1,0:T(8,128)(2,1)S(1)}, bf16[17,16,128]{2,1,0:T(8,128)(2,1)S(1)}, u32[]{:S(2)}, u32[]{:S(2)}) collective-permute-start(bf16[17,16,128]{2,1,0:T(8,128)(2,1)S(1)} %get-tuple-element.14), channel_id=1, source_target_pairs={{1,2},{3,4},{5,6},{7,8},{9,10},{11,12},{13,14},{2,1},{4,3},{6,5},{... | collective-permute-start | bytes 208904 | tf_op jit(solution)/shard_map/ppermute | solution.py:26
  13.5 8.5 %collective-permute-start.3 = (bf16[17,16,128]{2,1,0:T(8,128)(2,1)S(1)}, bf16[17,16,128]{2,1,0:T(8,128)(2,1)S(1)}, u32[]{:S(2)}, u32[]{:S(2)}) collective-permute-start(bf16[17,16,128]{2,1,0:T(8,128)(2,1)S(1)} %get-tuple-element.15), channel_id=1, source_target_pairs={{0,1},{2,3},{4,5},{6,7},{8,9},{10,11},{12,13},{14,15},{1,0},{3,2},... | collective-permute-start | bytes 208904 | tf_op jit(solution)/shard_map/ppermute | solution.py:26
  23.2 4.1 %copy-start.5 = (f32[8,16,128]{2,1,0:T(8,128)S(1)}, f32[8,16,128]{2,1,0:T(8,128)}, u32[]{:S(2)}) copy-start(f32[8,16,128]{2,1,0:T(8,128)} %logf.1) | copy-start | bytes 196612
  23.2 12.2 %all-to-all-start = ((bf16[16,10,2,128]{3,2,1,0:T(2,128)(2,1)}), bf16[16,10,2,128]{3,2,1,0:T(2,128)(2,1)S(1)}, u32[]{:S(2)}, u32[]{:S(2)}) async-start(bf16[16,10,2,128]{3,2,1,0:T(2,128)(2,1)} %message.1), calls=%async_computation | async-start | bytes 163840 | tf_op jit(solution)/shard_map/all_to_all | solution.py:303

commit v11 on v10

--- a/solution.py
+++ b/solution.py
@@ -37,10 +37,10 @@
         pltpu.make_async_copy(source, target, sems.at[1 + k])
         for k, (source, target) in enumerate(
             (
+                (adj_hbm.at[:, cb - 1 - near_b], to_b_far.at[pl.ds(0, ca)]),
+                (adj_hbm.at[:, near_b], to_b_near.at[pl.ds(0, ca)]),
                 (adj_hbm.at[ca - 1 - near_a], to_a_far.at[pl.ds(0, cb)]),
                 (adj_hbm.at[near_a], to_a_near.at[pl.ds(0, cb)]),
-                (adj_hbm.at[:, cb - 1 - near_b], to_b_far.at[pl.ds(0, ca)]),
-                (adj_hbm.at[:, near_b], to_b_near.at[pl.ds(0, ca)]),
             )
         )
     ]

time: 36.6 us -> 36.6 us (level)
  no operation moved by 1% of the time
where the time goes in v11:
time: 36.6 us; the launch traced here: 36.3 us
  starting transfers between devices  23.4 us (64%)
  Pallas kernels  6.35 us (17%)
  waiting for transfers between devices  5.71 us (16%)
  between operations  0.79 us (2%)
    ppermute x4, starting transfers between devices, swap(): return lax.ppermute(block, axis, pairs + [(j, i) for i, j in pairs])  19.3 us
    all_to_all x1, waiting for transfers between devices, per_device(): lax.all_to_all(message, 'gy', split_axis=0, concat_axis=0, tiled=True)  5.23 us
    all_to_all x1, starting transfers between devices, per_device(): lax.all_to_all(message, 'gy', split_axis=0, concat_axis=0, tiled=True)  4.05 us
    pallas_call x1, Pallas kernels, per_device(): pl.pallas_call(update_body, out_shape=(shape(adjoint_trace.shape, BF16),...  2.94 us
    pallas_call x1, Pallas kernels, per_device(): pl.pallas_call(pack_body, out_shape=(shape((cb + 2, nl, width), BF16), sh...  1.11 us
    pallas_call x1, Pallas kernels, per_device(): pl.pallas_call(message_body, out_shape=shape((owners, MSG // 2, 2, width)...  0.97 us
    pallas_call x1, Pallas kernels, per_device(): pl.pallas_call(gradient_body, out_shape=shape(log_friction.shape, F32), i...  0.83 us
  transfers between devices with their start and end apart: 5, of which 2 were waited for; matrix products, arithmetic and copies ran while one was open for 0% of the time, Pallas kernels for 9%

profile of v11, /device:TPU:1, one launch (start us, length us, event | category | flops | bytes accessed | tf_op | source)
XLA Modules:
  0.0 36.3 jit_solution(6618496287309106776)
XLA Ops:
  0.6 0.0 copy-start.1
  0.6 0.0 copy-start
  0.6 0.0 copy-start.2
  0.7 1.1 %pack.1 = (bf16[18,16,128]{2,1,0:T(8,128)(2,1)S(1)}, bf16[18,16,128]{2,1,0:T(8,128)(2,1)S(1)}, bf16[17,16,128]{2,1,0:T(8,128)(2,1)S(1)}, bf16[17,16,128]{2,1,0:T(8,128)(2,1)S(1)}) custom-call(bf16[16,16,16,128]{3,2,1,0:T(8,128)(2,1)} %adj.3, f32[8,16,128]{2,1,0:T(8,128)} %logf.1), custom_call_target="tpu_custom_call" | custom-call | flops 1000000000 | bytes 3145728 | tf_op jit(solution)/shard_map/pack/pallas_call | solution.py:243
  1.8 0.7 %collective-permute-start = (bf16[18,16,128]{2,1,0:T(8,128)(2,1)S(1)}, bf16[18,16,128]{2,1,0:T(8,128)(2,1)S(1)}, u32[]{:S(2)}, u32[]{:S(2)}) collective-permute-start(bf16[18,16,128]{2,1,0:T(8,128)(2,1)S(1)} %get-tuple-element.12), channel_id=1, source_target_pairs={{16,32},{48,64},{80,96},{112,128},{144,160},{176,192},{208,224},{2... | collective-permute-start | bytes 221192 | tf_op jit(solution)/shard_map/ppermute | solution.py:26
  2.5 6.8 %collective-permute-start.1 = (bf16[18,16,128]{2,1,0:T(8,128)(2,1)S(1)}, bf16[18,16,128]{2,1,0:T(8,128)(2,1)S(1)}, u32[]{:S(2)}, u32[]{:S(2)}) collective-permute-start(bf16[18,16,128]{2,1,0:T(8,128)(2,1)S(1)} %get-tuple-element.13), channel_id=1, source_target_pairs={{0,16},{32,48},{64,80},{96,112},{128,144},{160,176},{192,208},{224... | collective-permute-start | bytes 221192 | tf_op jit(solution)/shard_map/ppermute | solution.py:26
  9.3 0.0 copy-start.3
  9.3 0.0 copy-start.4
  9.3 4.2 %collective-permute-start.2 = (bf16[17,16,128]{2,1,0:T(8,128)(2,1)S(1)}, bf16[17,16,128]{2,1,0:T(8,128)(2,1)S(1)}, u32[]{:S(2)}, u32[]{:S(2)}) collective-permute-start(bf16[17,16,128]{2,1,0:T(8,128)(2,1)S(1)} %get-tuple-element.14), channel_id=1, source_target_pairs={{1,2},{3,4},{5,6},{7,8},{9,10},{11,12},{13,14},{2,1},{4,3},{6,5},{... | collective-permute-start | bytes 208904 | tf_op jit(solution)/shard_map/ppermute | solution.py:26
  13.5 7.6 %collective-permute-start.3 = (bf16[17,16,128]{2,1,0:T(8,128)(2,1)S(1)}, bf16[17,16,128]{2,1,0:T(8,128)(2,1)S(1)}, u32[]{:S(2)}, u32[]{:S(2)}) collective-permute-start(bf16[17,16,128]{2,1,0:T(8,128)(2,1)S(1)} %get-tuple-element.15), channel_id=1, source_target_pairs={{0,1},{2,3},{4,5},{6,7},{8,9},{10,11},{12,13},{14,15},{1,0},{3,2},... | collective-permute-start | bytes 208904 | tf_op jit(solution)/shard_map/ppermute | solution.py:26
  21.1 0.0 copy-done.1
  21.2 0.0 copy-done
  21.2 0.0 copy-done.2
  21.2 0.0 copy-done.3
  21.2 0.0 copy-done.4
  21.2 0.3 local.1
  21.5 0.0 collective-permute-done.2.b_far
  21.6 0.5 %collective-permute-done.3.b_near = bf16[17,16,128]{2,1,0:T(8,128)(2,1)S(1)} collective-permute-done((bf16[17,16,128]{2,1,0:T(8,128)(2,1)S(1)}, bf16[17,16,128]{2,1,0:T(8,128)(2,1)S(1)}, u32[]{:S(2)}, u32[]{:S(2)}) %collective-permute-start.3) | collective-permute-done | bytes 69664 | tf_op jit(solution)/shard_map/ppermute | solution.py:26
  22.0 0.0 collective-permute-done.a_far
  22.0 0.2 edges.1.partial
  22.2 0.0 collective-permute-done.1.a_near
  22.2 1.0 %message.1 = bf16[16,10,2,128]{3,2,1,0:T(2,128)(2,1)} custom-call(f32[256,128]{1,0:T(8,128)S(1)} %edges.1.partial, bf16[256,256]{1,0:T(8,128)(2,1)S(1)} %get-tuple-element.18.pick, f32[16,128]{1,0:T(8,128)S(1)} %get-tuple-element.19.ids, bf16[7,128,128]{2,1,0:T(8,128)(2,1)S(1)} %copy-done, bf16[18,16,128]{2,1,0:T(8,128)(2,1)S(1)} %collective-permute-done.a_far, ...), custom_call_target="tpu_custom_call" | custom-call | flops 16777216 | bytes 1048576 | tf_op jit(solution)/shard_map/message/pallas_call | solution.py:289
  23.2 0.0 copy-start.5
  23.2 4.0 %all-to-all-start = ((bf16[16,10,2,128]{3,2,1,0:T(2,128)(2,1)}), bf16[16,10,2,128]{3,2,1,0:T(2,128)(2,1)S(1)}, u32[]{:S(2)}, u32[]{:S(2)}) async-start(bf16[16,10,2,128]{3,2,1,0:T(2,128)(2,1)} %message.1), calls=%async_computation | async-start | bytes 163840 | tf_op jit(solution)/shard_map/all_to_all | solution.py:303
  27.2 0.0 copy-done.5
  27.2 2.9 %update.1 = (bf16[16,16,16,128]{3,2,1,0:T(8,128)(2,1)}, f32[8,16,128]{2,1,0:T(8,128)S(1)}, f32[8,16,128]{2,1,0:T(8,128)S(1)}) custom-call(bf16[16,16,16,128]{3,2,1,0:T(8,128)(2,1)S(1)} %copy-done.1, bf16[7,128,128]{2,1,0:T(8,128)(2,1)S(1)} %copy-done, f32[8,16,128]{2,1,0:T(8,128)S(1)} %copy-done.5, bf16[18,16,128]{2,1,0:T(8,128)(2,1)S(1)} %collective-permute-done.a_far, ...), custom_call_target="tpu_custom_call" | custom-call | flops 939524096 | bytes 4194304 | tf_op jit(solution)/shard_map/update/pallas_call | solution.py:305
  30.2 5.2 %all-to-all-done.got = bf16[16,10,2,128]{3,2,1,0:T(2,128)(2,1)S(1)} async-done(((bf16[16,10,2,128]{3,2,1,0:T(2,128)(2,1)}), bf16[16,10,2,128]{3,2,1,0:T(2,128)(2,1)S(1)}, u32[]{:S(2)}, u32[]{:S(2)}) %all-to-all-start) | async-done | bytes 81952 | tf_op jit(solution)/shard_map/all_to_all | solution.py:303
  35.4 0.8 %gradient.1 = f32[8,16,128]{2,1,0:T(8,128)} custom-call(bf16[16,10,2,128]{3,2,1,0:T(2,128)(2,1)S(1)} %all-to-all-done.got, f32[8,16,128]{2,1,0:T(8,128)S(1)} %get-tuple-element.20.prior, f32[8,16,128]{2,1,0:T(8,128)S(1)} %get-tuple-element.21.scale), custom_call_target="tpu_custom_call" | custom-call | flops 8388608 | bytes 524288 | tf_op jit(solution)/shard_map/gradient/pallas_call | solution.py:329
Async XLA Ops:
  0.6 20.5 %copy-start.1 = (bf16[16,16,16,128]{3,2,1,0:T(8,128)(2,1)S(1)}, bf16[16,16,16,128]{3,2,1,0:T(8,128)(2,1)}, u32[]{:S(2)}) copy-start(bf16[16,16,16,128]{3,2,1,0:T(8,128)(2,1)} %adj.3) | copy-start | bytes 3145732
  0.6 20.5 %copy-start = (bf16[7,128,128]{2,1,0:T(8,128)(2,1)S(1)}, bf16[7,128,128]{2,1,0:T(8,128)(2,1)}, u32[]{:S(2)}) copy-start(bf16[7,128,128]{2,1,0:T(8,128)(2,1)} %coupling.7) | copy-start | bytes 688132
  0.6 20.5 %copy-start.2 = (s32[1,1,16,16]{3,2,1,0:T(8,128)S(1)}, s32[1,1,16,16]{3,2,1,0:T(8,128)}, u32[]{:S(2)}) copy-start(s32[1,1,16,16]{3,2,1,0:T(8,128)} %nodes.1) | copy-start | bytes 3076
  1.8 20.3 %collective-permute-start = (bf16[18,16,128]{2,1,0:T(8,128)(2,1)S(1)}, bf16[18,16,128]{2,1,0:T(8,128)(2,1)S(1)}, u32[]{:S(2)}, u32[]{:S(2)}) collective-permute-start(bf16[18,16,128]{2,1,0:T(8,128)(2,1)S(1)} %get-tuple-element.12), channel_id=1, source_target_pairs={{16,32},{48,64},{80,96},{112,128},{144,160},{176,192},{208,224},{2... | collective-permute-start | bytes 221192 | tf_op jit(solution)/shard_map/ppermute | solution.py:26
  2.5 19.8 %collective-permute-start.1 = (bf16[18,16,128]{2,1,0:T(8,128)(2,1)S(1)}, bf16[18,16,128]{2,1,0:T(8,128)(2,1)S(1)}, u32[]{:S(2)}, u32[]{:S(2)}) collective-permute-start(bf16[18,16,128]{2,1,0:T(8,128)(2,1)S(1)} %get-tuple-element.13), channel_id=1, source_target_pairs={{0,16},{32,48},{64,80},{96,112},{128,144},{160,176},{192,208},{224... | collective-permute-start | bytes 221192 | tf_op jit(solution)/shard_map/ppermute | solution.py:26
  9.3 11.9 %copy-start.3 = (s32[1,1,256]{2,1,0:T(1,128)S(1)}, s32[1,1,256]{2,1,0:T(1,128)}, u32[]{:S(2)}) copy-start(s32[1,1,256]{2,1,0:T(1,128)} %send.1) | copy-start | bytes 3076
  9.3 11.9 %copy-start.4 = (s32[1,1,16]{2,1,0:T(1,128)S(1)}, s32[1,1,16]{2,1,0:T(1,128)}, u32[]{:S(2)}) copy-start(s32[1,1,16]{2,1,0:T(1,128)} %live.1) | copy-start | bytes 196
  9.3 12.3 %collective-permute-start.2 = (bf16[17,16,128]{2,1,0:T(8,128)(2,1)S(1)}, bf16[17,16,128]{2,1,0:T(8,128)(2,1)S(1)}, u32[]{:S(2)}, u32[]{:S(2)}) collective-permute-start(bf16[17,16,128]{2,1,0:T(8,128)(2,1)S(1)} %get-tuple-element.14), channel_id=1, source_target_pairs={{1,2},{3,4},{5,6},{7,8},{9,10},{11,12},{13,14},{2,1},{4,3},{6,5},{... | collective-permute-start | bytes 208904 | tf_op jit(solution)/shard_map/ppermute | solution.py:26
  13.5 8.5 %collective-permute-start.3 = (bf16[17,16,128]{2,1,0:T(8,128)(2,1)S(1)}, bf16[17,16,128]{2,1,0:T(8,128)(2,1)S(1)}, u32[]{:S(2)}, u32[]{:S(2)}) collective-permute-start(bf16[17,16,128]{2,1,0:T(8,128)(2,1)S(1)} %get-tuple-element.15), channel_id=1, source_target_pairs={{0,1},{2,3},{4,5},{6,7},{8,9},{10,11},{12,13},{14,15},{1,0},{3,2},... | collective-permute-start | bytes 208904 | tf_op jit(solution)/shard_map/ppermute | solution.py:26
  23.2 4.1 %copy-start.5 = (f32[8,16,128]{2,1,0:T(8,128)S(1)}, f32[8,16,128]{2,1,0:T(8,128)}, u32[]{:S(2)}) copy-start(f32[8,16,128]{2,1,0:T(8,128)} %logf.1) | copy-start | bytes 196612
  23.2 12.2 %all-to-all-start = ((bf16[16,10,2,128]{3,2,1,0:T(2,128)(2,1)}), bf16[16,10,2,128]{3,2,1,0:T(2,128)(2,1)S(1)}, u32[]{:S(2)}, u32[]{:S(2)}) async-start(bf16[16,10,2,128]{3,2,1,0:T(2,128)(2,1)} %message.1), calls=%async_computation | async-start | bytes 163840 | tf_op jit(solution)/shard_map/all_to_all | solution.py:303
